TPU v7x, 32 devices: a whole 2x2x4 slice. The times are simulated.
32 devices in a mesh: region: 4 (over z), tile: 8 (over y, x, core).
Axes of the slice: x: 2, y: 2, z: 4, core: 2. Of those that a mesh axis runs over, the one named last changes fastest.
Arguments:
- water_depth: float32 [1536, 2048], P('region', 'tile'), may hold values from 0.12 to 3
- momentum: float32 [2, 1536, 2048], P(None, 'region', 'tile'), may hold values from -3 to 3
- wet_mask: int32 [96, 8], P('region', 'tile'), may hold values from 0 to 1, as said below
- helper_plan: int32 [96, 8], P('region', 'tile'), may hold values from -1 to 7, as said below
- breach_cells: int32 [4, 8, 64], P('region', 'tile'), may hold values from 0 to 98303
- breach_rate: float32 [4, 8, 64], P('region', 'tile'), may hold values from 1 to 4
Outputs:
- new_depth: float32 [1536, 2048], P('region', 'tile')
- new_momentum: float32 [2, 1536, 2048], P(None, 'region', 'tile')
- helper_speed: float32 [4, 8], P('region', 'tile')
Inputs may be any that keep to these rules, and one draw needn't show every extreme that they name: `wet_mask`: along the tile axis the wet block counts of a region's devices run cyclically through 24, 12, 8, 6, 4, 4, 4, 2, at a starting point drawn for each region. `helper_plan`: -1 exactly on dry blocks. The k-th wet block of device t (k from 0), in an order drawn from the seed, goes to helper (t + k - 1) mod 8 of the same region; so one device hands one helper at most 3 blocks, a helper receives at most 10 blocks in all, and some helper of every region receives exactly 10.
All inputs are finite; a program needn't handle non-finite values.
Results may differ from a plain program's by a relative error of at most 0.0003.
Values sent between devices are 32-bit elements; how exact they have to be, the bound alone decides.
No kernel may reach another device: no remote copies, remote signals or barrier semaphores. Data moves between devices by JAX's collectives and lax.ppermute only.
A program may use at most 128 MiB of HBM per device.

v0:
```python
import jax
import jax.numpy as jnp
from jax import lax
from jax.sharding import PartitionSpec as P

STEPS = 4


GRAVITY = 9.81
COURANT = 0.45
SPACING = 1.0


def extended_2(cells, sides, width):
    for axis, dim in sides:
        count = lax.axis_size(axis)
        ends = count - 1
        head = lax.slice_in_dim(cells, 0, width, axis=dim)
        tail = lax.slice_in_dim(cells, cells.shape[dim] - width, cells.shape[dim], axis=dim)
        cells = jnp.concatenate(
            [
                lax.ppermute(tail, axis, [(i, (i + 1) % count) for i in range(ends)]),
                cells,
                lax.ppermute(head, axis, [((i + 1) % count, i) for i in range(ends)]),
            ],
            axis=dim,
        )
    return cells


def wave_speed(depth_now, along_now, across_now):
    return jnp.maximum(jnp.abs(along_now / depth_now), jnp.abs(across_now / depth_now)) + jnp.sqrt(
        GRAVITY * depth_now
    )


def roe_flux(depth_left, normal_left, tangent_left, depth_right, normal_right, tangent_right):
    speed_left = normal_left / depth_left
    speed_right = normal_right / depth_right
    drift_left = tangent_left / depth_left
    drift_right = tangent_right / depth_right
    root_left = jnp.sqrt(depth_left)
    root_right = jnp.sqrt(depth_right)
    root_sum = root_left + root_right
    mean_speed = (root_left * speed_left + root_right * speed_right) / root_sum
    mean_drift = (root_left * drift_left + root_right * drift_right) / root_sum
    celerity = jnp.sqrt(GRAVITY * 0.5 * (depth_left + depth_right))
    jump_depth = depth_right - depth_left
    jump_normal = normal_right - normal_left
    jump_tangent = tangent_right - tangent_left
    strength_one = ((mean_speed + celerity) * jump_depth - jump_normal) / (2.0 * celerity)
    strength_three = (jump_normal - (mean_speed - celerity) * jump_depth) / (2.0 * celerity)
    strength_two = jump_tangent - mean_drift * jump_depth
    wave_one = jnp.abs(mean_speed - celerity) * strength_one
    wave_two = jnp.abs(mean_speed) * strength_two
    wave_three = jnp.abs(mean_speed + celerity) * strength_three
    flux_depth = 0.5 * (normal_left + normal_right) - 0.5 * (wave_one + wave_three)
    flux_normal = 0.5 * (
        normal_left * speed_left
        + normal_right * speed_right
        + 0.5 * GRAVITY * (depth_left * depth_left + depth_right * depth_right)
    ) - 0.5 * (wave_one * (mean_speed - celerity) + wave_three * (mean_speed + celerity))
    flux_tangent = 0.5 * (normal_left * drift_left + normal_right * drift_right) - 0.5 * (
        (wave_one + wave_three) * mean_drift + wave_two
    )
    return (flux_depth, flux_normal, flux_tangent)


def advance(depth_pad, along_pad, across_pad, active, source, step_size):
    step_ratio = step_size / SPACING
    row_depth, row_along, row_across = roe_flux(
        depth_pad[..., :-1, 1:-1],
        along_pad[..., :-1, 1:-1],
        across_pad[..., :-1, 1:-1],
        depth_pad[..., 1:, 1:-1],
        along_pad[..., 1:, 1:-1],
        across_pad[..., 1:, 1:-1],
    )
    col_depth, col_across, col_along = roe_flux(
        depth_pad[..., 1:-1, :-1],
        across_pad[..., 1:-1, :-1],
        along_pad[..., 1:-1, :-1],
        depth_pad[..., 1:-1, 1:],
        across_pad[..., 1:-1, 1:],
        along_pad[..., 1:-1, 1:],
    )
    depth_now = depth_pad[..., 1:-1, 1:-1]
    along_now = along_pad[..., 1:-1, 1:-1]
    across_now = across_pad[..., 1:-1, 1:-1]
    new_depth = (
        depth_now
        - step_ratio
        * (
            row_depth[..., 1:, :]
            - row_depth[..., :-1, :]
            + col_depth[..., 1:]
            - col_depth[..., :-1]
        )
        + step_size * source
    )
    new_along = along_now - step_ratio * (
        row_along[..., 1:, :] - row_along[..., :-1, :] + col_along[..., 1:] - col_along[..., :-1]
    )
    new_across = across_now - step_ratio * (
        row_across[..., 1:, :]
        - row_across[..., :-1, :]
        + col_across[..., 1:]
        - col_across[..., :-1]
    )
    keep_cell = active > 0.5
    return (
        jnp.where(keep_cell, new_depth, depth_now),
        jnp.where(keep_cell, new_along, along_now),
        jnp.where(keep_cell, new_across, across_now),
    )


def mirror(values, edge_flags, row_factor, col_factor):
    top_side = (edge_flags[0] > 0.5)[:, None, None]
    bottom_side = (edge_flags[1] > 0.5)[:, None, None]
    left_side = (edge_flags[2] > 0.5)[:, None, None]
    right_side = (edge_flags[3] > 0.5)[:, None, None]
    upper_fix = jnp.concatenate([row_factor * jnp.flip(values[:, 4:8], 1), values[:, 4:]], 1)
    values = jnp.where(top_side, upper_fix, values)
    lower_fix = jnp.concatenate([values[:, :-4], row_factor * jnp.flip(values[:, -8:-4], 1)], 1)
    values = jnp.where(bottom_side, lower_fix, values)
    left_fix = jnp.concatenate([col_factor * jnp.flip(values[:, :, 4:8], 2), values[:, :, 4:]], 2)
    values = jnp.where(left_side, left_fix, values)
    right_fix = jnp.concatenate(
        [values[:, :, :-4], col_factor * jnp.flip(values[:, :, -8:-4], 2)], 2
    )
    return jnp.where(right_side, right_fix, values)


def run_steps(work_blocks, edge_flags):
    depth_now = work_blocks[0]
    along_now = work_blocks[1]
    across_now = work_blocks[2]
    active = work_blocks[3]
    source = work_blocks[4]
    inner_active = active[:, 4:-4, 4:-4] > 0.5
    edge_pad = ((0, 0), (1, 1), (1, 1))
    for step_index in range(STEPS):
        depth_now = mirror(depth_now, edge_flags, 1.0, 1.0)
        along_now = mirror(along_now, edge_flags, -1.0, 1.0)
        across_now = mirror(across_now, edge_flags, 1.0, -1.0)
        inner_speed = wave_speed(
            depth_now[:, 4:-4, 4:-4], along_now[:, 4:-4, 4:-4], across_now[:, 4:-4, 4:-4]
        )
        local_peak = jnp.max(jnp.where(inner_active, inner_speed, jnp.float32(0.0)))
        speed_peak = lax.pmax(local_peak, ("region", "tile"))
        step_size = COURANT * SPACING / speed_peak
        depth_now, along_now, across_now = advance(
            jnp.pad(depth_now, edge_pad, mode="edge"),
            jnp.pad(along_now, edge_pad, mode="edge"),
            jnp.pad(across_now, edge_pad, mode="edge"),
            active,
            source,
            step_size,
        )
    return (depth_now, along_now, across_now)


def on_device(water_depth, momentum, wet_mask, helper_plan, breach_cells, breach_rate):
    row_count, col_count = water_depth.shape
    block_count = wet_mask.shape[0]
    block_rows = row_count // block_count
    tile_count = lax.axis_size("tile")
    region_count = lax.axis_size("region")
    region_at = lax.axis_index("region")
    tile_at = lax.axis_index("tile")
    source = (
        jnp.zeros((row_count * col_count,), jnp.float32)
        .at[breach_cells.reshape(-1)]
        .add(breach_rate.reshape(-1))
        .reshape(row_count, col_count)
    )
    own_plan = helper_plan[:, 0]
    wet_rows = jnp.repeat(wet_mask[:, 0].astype(jnp.float32), block_rows)
    active = jnp.broadcast_to(wet_rows[:, None], (row_count, col_count))
    fields = jnp.stack([water_depth, momentum[0], momentum[1], active, source])
    halo_out = extended_2(fields, (("region", 1), ("tile", 2)), 4)
    top_edge = (region_at == 0).astype(jnp.float32)
    bottom_edge = (region_at == region_count - 1).astype(jnp.float32)
    left_edge = (tile_at == 0).astype(jnp.float32)
    right_edge = (tile_at == tile_count - 1).astype(jnp.float32)
    own_flags = jnp.stack([top_edge, bottom_edge, left_edge, right_edge])[:, None]
    depth_now, along_now, across_now = run_steps(halo_out[:, None], own_flags)
    inner_depth = depth_now[0, 4:-4, 4:-4]
    inner_along = along_now[0, 4:-4, 4:-4]
    inner_across = across_now[0, 4:-4, 4:-4]
    final_speed = jnp.where(
        active > 0.5, wave_speed(inner_depth, inner_along, inner_across), jnp.float32(0.0)
    )
    block_peak = jnp.max(final_speed.reshape(block_count, block_rows, col_count), axis=(1, 2))
    tile_ids = jnp.arange(tile_count, dtype=jnp.int32)
    hit_table = own_plan[:, None] == tile_ids[None, :]
    helper_vector = jnp.max(jnp.where(hit_table, block_peak[:, None], jnp.float32(0.0)), axis=0)
    helper_vector = lax.pmax(helper_vector, "tile")
    own_value = jnp.sum(jnp.where(tile_ids == tile_at, helper_vector, jnp.float32(0.0)))
    updated = jnp.stack([inner_depth, inner_along, inner_across]).reshape(
        3, block_count, block_rows, col_count
    )
    updated = updated.reshape(3, row_count, col_count)
    return (updated[0], updated[1:3], own_value.reshape(1, 1))


def solution(mesh):
    return jax.shard_map(
        on_device,
        mesh=mesh,
        in_specs=(
            P("region", "tile"),
            P(None, "region", "tile"),
            P("region", "tile"),
            P("region", "tile"),
            P("region", "tile", None),
            P("region", "tile", None),
        ),
        out_specs=(P("region", "tile"), P(None, "region", "tile"), P("region", "tile")),
        check_vma=False,
    )
```

profile of v0, /device:TPU:0, one launch (start us, length us, event | category | flops | bytes accessed | tf_op | source)
XLA Modules:
  0.0 349.0 jit_solution(5817909773080586037)
XLA Ops:
  4.5 4.9 %collective-permute-start = (f32[5,4,256]{2,1,0:T(4,128)S(1)}, f32[5,4,256]{2,1,0:T(4,128)S(1)}, u32[]{:S(2)}, u32[]{:S(2)}) collective-permute-start(f32[5,4,256]{2,1,0:T(4,128)S(1)} %get-tuple-element.25), channel_id=1, source_target_pairs={{0,8},{8,16},{16,24},{1,9},{9,17},{17,25},{2,10},{10,18},{18,26},{... | collective-permute-start | bytes 61448 | tf_op jit(solution)/shard_map/ppermute | solution.py:22
  10.9 4.2 %collective-permute-done.1 = f32[5,4,256]{2,1,0:T(4,128)S(1)} collective-permute-done((f32[5,4,256]{2,1,0:T(4,128)S(1)}, f32[5,4,256]{2,1,0:T(4,128)S(1)}, u32[]{:S(2)}, u32[]{:S(2)}) %collective-permute-start.1) | collective-permute-done | bytes 20512 | tf_op jit(solution)/shard_map/ppermute | solution.py:24
  18.2 3.0 collective-permute-start.2
  24.9 3.2 pad_maximum_fusion
  30.0 2.7 slice_select_fusion
  49.3 2.6 multiply_subtract_fusion.22
  55.4 2.5 multiply_subtract_fusion.11
  57.9 43.5 %pmax.35 = f32[]{:T(128)} all-reduce(f32[]{:T(128)} %fusion.161), channel_id=1, replica_groups=mesh['region'=4,'tile'=8] {'region','tile'}, use_global_device_ids=true, to_apply=%region_2.3 | all-reduce | flops 1 | bytes 8 | tf_op jit(solution)/shard_map/pmax | solution.py:151
  103.9 3.6 %fusion.169 = (f32[1,392,264]{2,1,0:T(8,128)}, f32[1,392,264]{2,1,0:T(8,128)S(1)}, f32[1,392,264]{2,1,0:T(8,128)S(1)}) fusion(f32[5,392,264]{2,1,0:T(8,128)} %copy-done, pred[1,392,264]{2,1,0:T(8,128)(4,1)S(1)} %get-tuple-element.11, f32[1,392,264]{2,1,0:T(8,128)S(1)} %maximum_select_fusion.2, f32[1,392,265]{2,1,0:T(8,128)} %multiply_subtract_fusion.23, ...), kind=kLoop, calls=%fused_computation.479 | loop fusion | flops 1448832 | bytes 5898820 | tf_op jit(solution)/shard_map/slice | solution.py:140
  129.8 3.4 multiply_subtract_fusion.19
  133.2 2.3 multiply_subtract_fusion.6
  135.6 2.5 multiply_subtract_fusion.8
  138.1 40.2 %pmax.36 = f32[]{:T(128)} all-reduce(f32[]{:T(128)} %fusion.162), channel_id=1, replica_groups=mesh['region'=4,'tile'=8] {'region','tile'}, use_global_device_ids=true, to_apply=%region_4.5 | all-reduce | flops 1 | bytes 8 | tf_op jit(solution)/shard_map/pmax | solution.py:151
  179.0 4.0 %subtract_select_fusion.2 = (f32[1,392,264]{2,1,0:T(8,128)S(1)}, f32[1,392,264]{2,1,0:T(8,128)S(1)}, f32[1,392,264]{2,1,0:T(8,128)S(1)}) fusion(pred[1,392,264]{2,1,0:T(8,128)(4,1)S(1)} %get-tuple-element.11, f32[1,392,264]{2,1,0:T(8,128)S(1)} %maximum_select_fusion.20, f32[1,392,265]{2,1,0:T(8,128)} %multiply_subtract_fusion.18, ...), kind=kLoop, calls=%fused_computation.5 | loop fusion | flops 2069760 | bytes 7968580 | tf_op jit(solution)/shard_map/jit(_where)/select_n | solution.py:114
  201.8 3.5 multiply_subtract_fusion.16
  207.6 2.5 multiply_subtract_fusion.5
  210.1 41.8 %pmax.37 = f32[]{:T(128)} all-reduce(f32[]{:T(128)} %fusion.163), channel_id=1, replica_groups=mesh['region'=4,'tile'=8] {'region','tile'}, use_global_device_ids=true, to_apply=%region_6.7 | all-reduce | flops 1 | bytes 8 | tf_op jit(solution)/shard_map/pmax | solution.py:151
  252.6 4.0 %subtract_select_fusion = (f32[1,392,264]{2,1,0:T(8,128)S(1)}, f32[1,392,264]{2,1,0:T(8,128)S(1)}, f32[1,392,264]{2,1,0:T(8,128)S(1)}) fusion(pred[1,392,264]{2,1,0:T(8,128)(4,1)S(1)} %get-tuple-element.11, f32[1,392,264]{2,1,0:T(8,128)S(1)} %maximum_select_fusion.32, f32[1,392,265]{2,1,0:T(8,128)} %multiply_subtract_fusion.15, ...), kind=kLoop, calls=%fused_computation.3 | loop fusion | flops 2069760 | bytes 7968580 | tf_op jit(solution)/shard_map/jit(_where)/select_n | solution.py:114
  275.0 3.6 %multiply_subtract_fusion.13 = f32[1,392,265]{2,1,0:T(8,128)} fusion(f32[1,1,264]{2,1,0:T(1,128)S(1)} %get-tuple-element.50, f32[1,1,264]{2,1,0:T(1,128)S(1)} %get-tuple-element.49, f32[1,392,264]{2,1,0:T(8,128)S(1)} %maximum_select_fusion.40, f32[1,1,264]{2,1,0:T(1,128)S(1)} %get-tuple-element.48, f32[1,392,264]{2,1,0:T(8,128)S(1)} %maximum_select_fusion.36, ...), kind=kLoop, calls=%fused_computation.346 | loop fusion | flops 9764720 | bytes 1663712 | tf_op jit(solution)/shard_map/sub | solution.py:63
  278.6 2.4 multiply_subtract_fusion
  280.9 2.5 multiply_subtract_fusion.2
  283.4 40.8 %pmax.38 = f32[]{:T(128)} all-reduce(f32[]{:T(128)} %select_reduce_fusion.1), channel_id=1, replica_groups=mesh['region'=4,'tile'=8] {'region','tile'}, use_global_device_ids=true, to_apply=%region_8.9 | all-reduce | flops 1 | bytes 8 | tf_op jit(solution)/shard_map/pmax | solution.py:151
  328.1 3.6 %select_reduce_fusion = (f32[384]{0:T(512)}, f32[1,384,256]{2,1,0:T(8,128)S(1)}, f32[1,384,256]{2,1,0:T(8,128)}, f32[1,384,256]{2,1,0:T(8,128)}) fusion(pred[384]{0:T(512)(128)(4,1)S(1)} %copy-done.24, f32[1,392,264]{2,1,0:T(8,128)S(1)} %get-tuple-element.44, f32[1,392,264]{2,1,0:T(8,128)S(1)} %get-tuple-element.43, ...), kind=kLoop, calls=%fused_computation.443 | loop fusion | flops 2752128 | bytes 7178116 | tf_op jit(solution)/shard_map/reduce_max | solution.py:195
  333.4 12.9 %pmax.39 = f32[8]{0:T(128)S(1)} all-reduce(f32[8]{0:T(128)S(1)} %select_reduce_fusion.2), channel_id=1, replica_groups=mesh['region'=4,'tile'=8] {'tile'}, use_global_device_ids=true, to_apply=%region_12.13 | all-reduce | flops 8 | bytes 64 | tf_op jit(solution)/shard_map/pmax | solution.py:199
  (289 shorter events, 103.8 us)
Async XLA Ops:
  0.6 14.5 %copy-start.1 = (f32[2,384,256]{2,1,0:T(8,128)S(1)}, f32[2,384,256]{2,1,0:T(8,128)}, u32[]{:S(2)}) copy-start(f32[2,384,256]{2,1,0:T(8,128)} %param.7) | copy-start | bytes 2359300
  0.6 14.5 %copy-start.13 = (f32[384,256]{1,0:T(8,128)S(1)}, f32[384,256]{1,0:T(8,128)}, u32[]{:S(2)}) copy-start(f32[384,256]{1,0:T(8,128)} %param.6) | copy-start | bytes 1179652
  3.6 11.7 %copy-start.2 = (f32[1,384,256]{2,1,0:T(8,128)}, f32[1,384,256]{2,1,0:T(8,128)S(1)}, u32[]{:S(2)}) copy-start(f32[1,384,256]{2,1,0:T(8,128)S(1)} %stack_broadcast_in_dim.10) | copy-start | bytes 1179652
  4.5 6.4 %collective-permute-start = (f32[5,4,256]{2,1,0:T(4,128)S(1)}, f32[5,4,256]{2,1,0:T(4,128)S(1)}, u32[]{:S(2)}, u32[]{:S(2)}) collective-permute-start(f32[5,4,256]{2,1,0:T(4,128)S(1)} %get-tuple-element.25), channel_id=1, source_target_pairs={{0,8},{8,16},{16,24},{1,9},{9,17},{17,25},{2,10},{10,18},{18,26},{... | collective-permute-start | bytes 61448 | tf_op jit(solution)/shard_map/ppermute | solution.py:22
  9.5 5.7 %collective-permute-start.1 = (f32[5,4,256]{2,1,0:T(4,128)S(1)}, f32[5,4,256]{2,1,0:T(4,128)S(1)}, u32[]{:S(2)}, u32[]{:S(2)}) collective-permute-start(f32[5,4,256]{2,1,0:T(4,128)S(1)} %get-tuple-element.26), channel_id=1, source_target_pairs={{8,0},{16,8},{24,16},{9,1},{17,9},{25,17},{10,2},{18,10},{26,18},{... | collective-permute-start | bytes 61448 | tf_op jit(solution)/shard_map/ppermute | solution.py:24
  15.3 6.0 %copy-start.25 = (s32[24,1]{0,1:T(1,128)S(1)}, s32[24,1]{0,1:T(1,128)}, u32[]{:S(2)}) copy-start(s32[24,1]{0,1:T(1,128)} %param.8) | copy-start | bytes 292
  16.9 6.6 %collective-permute-start.3 = (f32[5,392,4]{1,0,2:T(8,128)S(1)}, f32[5,392,4]{1,0,2:T(8,128)S(1)}, u32[]{:S(2)}, u32[]{:S(2)}) collective-permute-start(f32[5,392,4]{1,0,2:T(8,128)S(1)} %copy.18), channel_id=1, source_target_pairs={{1,0},{2,1},{3,2},{4,3},{5,4},{6,5},{7,6},{9,8},{10,9},{11,10},{12... | collective-permute-start | bytes 94088 | tf_op jit(solution)/shard_map/ppermute | solution.py:24
  18.2 3.9 %collective-permute-start.2 = (f32[5,392,4]{1,0,2:T(8,128)S(1)}, f32[5,392,4]{1,0,2:T(8,128)S(1)}, u32[]{:S(2)}, u32[]{:S(2)}) collective-permute-start(f32[5,392,4]{1,0,2:T(8,128)S(1)} %copy.17), channel_id=1, source_target_pairs={{0,1},{1,2},{2,3},{3,4},{4,5},{5,6},{6,7},{8,9},{9,10},{10,11},{11... | collective-permute-start | bytes 94088 | tf_op jit(solution)/shard_map/ppermute | solution.py:22
  28.1 4.7 %copy-start = (f32[5,392,264]{2,1,0:T(8,128)}, f32[5,392,264]{2,1,0:T(8,128)S(1)}, u32[]{:S(2)}) copy-start(f32[5,392,264]{2,1,0:T(8,128)S(1)} %pad_maximum_fusion) | copy-start | bytes 6209284
  33.6 2.7 copy-start.6
  33.6 3.8 %copy-start.5 = (f32[1,392,264]{2,1,0:T(8,128)S(1)}, f32[1,392,264]{2,1,0:T(8,128)}, u32[]{:S(2)}) copy-start(f32[1,392,264]{2,1,0:T(8,128)} %get-tuple-element.14) | copy-start | bytes 1241860
  43.5 4.5 %copy-start.18 = (f32[1,392,4]{2,1,0:T(8,128)S(1)}, f32[1,392,4]{2,1,0:T(8,128)}, u32[]{:S(2)}) copy-start(f32[1,392,4]{2,1,0:T(8,128)} %slice.1171) | copy-start | bytes 18820
  102.0 1.9 copy-start.12
  103.9 6.2 %copy-start.8 = (f32[1,392,264]{2,1,0:T(8,128)}, f32[1,392,264]{2,1,0:T(8,128)S(1)}, u32[]{:S(2)}) copy-start(f32[1,392,264]{2,1,0:T(8,128)S(1)} %get-tuple-element.10) | copy-start | bytes 1241860
  108.7 2.5 copy-start.16
  112.7 4.3 %copy-start.14 = (f32[1,392,260]{2,1,0:T(8,128)S(1)}, f32[1,392,260]{2,1,0:T(8,128)}, u32[]{:S(2)}) copy-start(f32[1,392,260]{2,1,0:T(8,128)} %slice.1229) | copy-start | bytes 1223044
  188.0 2.5 copy-start.15
  191.4 2.5 copy-start.21
  263.7 2.5 copy-start.19
  266.1 2.5 copy-start.22
  324.9 2.0 copy-start.11
  326.6 1.3 copy-start.10
  326.9 1.3 copy-start.17
  326.9 1.2 copy-start.24
  (6 other events, 5.4 us)
where the time goes:
time: 354 us; the launch traced here: 349 us
  blocking collectives  179 us (51%)
  other arithmetic  101 us (29%)
  local copies, waits for them, and re-layouts  48.8 us (14%)
  starting transfers between devices  10.5 us (3%)
  between operations  5.15 us (1%)
  waiting for transfers between devices  4.52 us (1%)
    pmax x4, blocking collectives, run_steps(): speed_peak = lax.pmax(local_peak, ('region', 'tile'))  166 us
    sub x8, other arithmetic, roe_flux(): 0.5 * (normal_left * drift_left + normal_right * drift_right)  22.5 us
    sub x8, other arithmetic, roe_flux(): 0.5 * (normal_left + normal_right) - 0.5 * (wave_one + wave_three)  17.6 us
    pmax x1, blocking collectives, on_device(): helper_vector = lax.pmax(helper_vector, 'tile')  12.9 us
    select_n x12, other arithmetic, mirror(): values = jnp.where(left_side, left_fix, values)  12.4 us
    slice x12, local copies, waits for them, and re-layouts, mirror(): values[:, :, 4:]  11.8 us
    sub x4, other arithmetic, roe_flux(): 0.5 * (normal_left * speed_left + normal_right * speed_right + 0.5 * GRAV...  8.33 us
    select_n x2, other arithmetic, advance(): jnp.where(keep_cell, new_across, across_now)  7.99 us
  transfers between devices with their start and end apart: 4, of which 3 were waited for; matrix products, arithmetic and copies ran while one was open for 1% of the time, Pallas kernels for 0%

commit v1 on v0

v1 whole, which is shorter than its diff:
```python
import jax
import jax.numpy as jnp
from jax import lax
from jax.experimental import pallas as pl
from jax.experimental.pallas import tpu as pltpu
from jax.sharding import PartitionSpec as P

STEPS = 4
HALO = 4
LANES = 128
TOP = 8

GRAVITY = 9.81
COURANT = 0.45
SPACING = 1.0

VMEM_LIMIT = 20 << 20


def vmem_spec():
    return pl.BlockSpec(memory_space=pltpu.VMEM)


def smem_spec():
    return pl.BlockSpec(memory_space=pltpu.SMEM)


def vmem_out(*shape):
    return pltpu.VMEM(shape, jnp.float32)


def params():
    return pltpu.CompilerParams(vmem_limit_bytes=VMEM_LIMIT)


def cost(flops, nbytes):
    return pl.CostEstimate(flops=flops, bytes_accessed=nbytes, transcendentals=0)


def lane_ids(rows):
    return lax.broadcasted_iota(jnp.int32, (rows, LANES), 1)


def speed_of(depth, along, across):
    root = lax.rsqrt(depth)
    inverse = root * root
    return jnp.maximum(jnp.abs(along), jnp.abs(across)) * inverse + jnp.sqrt(
        jnp.float32(GRAVITY)
    ) * (depth * root)


def spread_peak(acc, out_ref):
    top = jnp.max(jnp.max(acc, axis=0, keepdims=True), axis=1, keepdims=True)
    out_ref[...] = jnp.broadcast_to(top[None], out_ref.shape)


def start_kernel(
    wet_ref, cell_ref, rate_ref, depth_ref, mom_ref, peak_ref, src_ref, up_ref, down_ref
):
    rows, cols = depth_ref.shape
    blocks = wet_ref.shape[0]
    block_rows = rows // blocks
    src_ref[...] = jnp.zeros_like(src_ref)
    lane = lax.broadcasted_iota(jnp.int32, (1, cols), 1)

    def add_cell(i, carry):
        cell = cell_ref[i]
        row = cell // cols
        col = cell - row * cols
        old = src_ref[pl.ds(row, 1), :]
        src_ref[pl.ds(row, 1), :] = old + jnp.where(lane == col, rate_ref[i], 0.0)
        return carry

    lax.fori_loop(0, cell_ref.shape[0], add_cell, 0)

    def one_block(b, acc):
        at = pl.multiple_of(b * block_rows, 8)
        wet = wet_ref[b, 0] > 0
        rows_at = pl.ds(at, block_rows)
        speed = speed_of(depth_ref[rows_at, :], mom_ref[0, rows_at, :], mom_ref[1, rows_at, :])
        speed = jnp.where(wet, speed, 0.0)
        for r in range(0, block_rows, 8):
            for c in range(0, cols, LANES):
                acc = jnp.maximum(acc, speed[r : r + 8, c : c + LANES])
        return acc

    acc = lax.fori_loop(0, blocks, one_block, jnp.zeros((8, LANES), jnp.float32))
    spread_peak(acc, peak_ref)
    for ref, lo, block in ((up_ref, 0, 0), (down_ref, rows - HALO, blocks - 1)):
        at = slice(lo, lo + HALO)
        ref[0] = depth_ref[at, :]
        ref[1] = mom_ref[0, at, :]
        ref[2] = mom_ref[1, at, :]
        ref[3] = jnp.full((HALO, cols), wet_ref[block, 0].astype(jnp.float32))
        ref[4] = src_ref[at, :]


def rows_kernel(
    edge_ref,
    wet_ref,
    depth_ref,
    mom_ref,
    src_ref,
    above_ref,
    below_ref,
    state_ref,
    fixed_ref,
    left_ref,
    right_ref,
    pack,
):
    rows, cols = depth_ref.shape
    blocks = wet_ref.shape[0]
    block_rows = rows // blocks
    tiles = cols // LANES
    padded = state_ref.shape[2]
    bottom = TOP + rows
    is_top = edge_ref[0] > 0
    is_bottom = edge_ref[1] > 0
    fields = [(state_ref, 0), (state_ref, 1), (state_ref, 2), (fixed_ref, 0), (fixed_ref, 1)]
    own = [depth_ref, mom_ref.at[0], mom_ref.at[1], None, src_ref]

    for b in range(blocks):
        wet = wet_ref[b, 0].astype(jnp.float32)
        for c in range(tiles):
            fixed_ref[0, c, TOP + b * block_rows : TOP + (b + 1) * block_rows, :] = jnp.full(
                (block_rows, LANES), wet
            )
    for f, (ref, k) in enumerate(fields):
        fill = 1.0 if f == 0 else 0.0
        flip = -1.0 if f == 1 else 1.0
        for c in range(tiles):
            at = slice(c * LANES, (c + 1) * LANES)
            if own[f] is not None:
                ref[k, c, TOP:bottom, :] = own[f][:, at]
            ref[k, c, 0:TOP, :] = jnp.full((TOP, LANES), fill, jnp.float32)
            ref[k, c, bottom:padded, :] = jnp.full((padded - bottom, LANES), fill, jnp.float32)
            for j in range(HALO):
                inside = ref[k, c, TOP + j : TOP + j + 1, :] * flip
                other = above_ref[f, HALO - 1 - j : HALO - j, at]
                ref[k, c, TOP - 1 - j : TOP - j, :] = jnp.where(is_top, inside, other)
                inside = ref[k, c, bottom - 1 - j : bottom - j, :] * flip
                other = below_ref[f, j : j + 1, at]
                ref[k, c, bottom + j : bottom + j + 1, :] = jnp.where(is_bottom, inside, other)

    lane = lane_ids(8)
    pack[padded:, :] = jnp.zeros((pack.shape[0] - padded, LANES), jnp.float32)

    def pack_rows(r, carry):
        at = pl.ds(pl.multiple_of(r * 8, 8), 8)
        out = jnp.zeros((8, LANES), jnp.float32)
        for f, (ref, k) in enumerate(fields):
            head = ref[k, 0, at, :]
            tail = ref[k, tiles - 1, at, :]
            first, second = HALO * f, 64 + HALO * f
            if first:
                head = pltpu.roll(head, first, 1)
            tail = pltpu.roll(tail, (second - (LANES - HALO)) % LANES, 1)
            out = jnp.where((lane >= first) & (lane < first + HALO), head, out)
            out = jnp.where((lane >= second) & (lane < second + HALO), tail, out)
        pack[at, :] = out
        return carry

    lax.fori_loop(0, padded // 8, pack_rows, 0)
    for q in range(pack.shape[0] // LANES):
        turned = pack[q * LANES : (q + 1) * LANES, :].T
        left_ref[:, q * LANES : (q + 1) * LANES] = turned[0 : left_ref.shape[0], :]
        right_ref[:, q * LANES : (q + 1) * LANES] = turned[64 : 64 + right_ref.shape[0], :]


def columns_kernel(
    edge_ref,
    state_in,
    fixed_in,
    own_left,
    own_right,
    from_left,
    from_right,
    state_ref,
    fixed_ref,
    both,
    turned,
):
    padded = state_ref.shape[2]
    last = state_ref.shape[1] - 1
    high = own_left.shape[0]
    is_left = edge_ref[2] > 0
    is_right = edge_ref[3] > 0
    both[...] = jnp.zeros_like(both)
    for f in range(5):
        flip = -1.0 if f == 2 else 1.0
        for j in range(HALO):
            row = HALO * f + j
            back = HALO * f + HALO - 1 - j
            both[row : row + 1, :] = jnp.where(
                is_left, own_left[back : back + 1, :] * flip, from_left[row : row + 1, :]
            )
            both[high + row : high + row + 1, :] = jnp.where(
                is_right, own_right[back : back + 1, :] * flip, from_right[row : row + 1, :]
            )
    for q in range(turned.shape[0] // LANES):
        turned[q * LANES : (q + 1) * LANES, :] = both[:, q * LANES : (q + 1) * LANES].T
    lane = lane_ids(8)
    fields = [(state_ref, 0), (state_ref, 1), (state_ref, 2), (fixed_ref, 0), (fixed_ref, 1)]

    def place(r, carry):
        at = pl.ds(pl.multiple_of(r * 8, 8), 8)
        strip = turned[at, :]
        for f, (ref, k) in enumerate(fields):
            out = jnp.full((8, LANES), 1.0 if f == 0 else 0.0, jnp.float32)
            left = pltpu.roll(strip, (LANES - HALO - HALO * f) % LANES, 1)
            right = pltpu.roll(strip, (-(high + HALO * f)) % LANES, 1)
            out = jnp.where(lane >= LANES - HALO, left, out)
            out = jnp.where(lane < HALO, right, out)
            ref[k, last, at, :] = out
        return carry

    lax.fori_loop(0, padded // 8, place, 0)


def roe(left, right):
    depth_l, normal_l, tangent_l, root_l, sn_l, st_l, press_l, shear_l = left
    depth_r, normal_r, tangent_r, root_r, sn_r, st_r, press_r, shear_r = right
    weight = pl.reciprocal(root_l + root_r, approx=False)
    speed = (sn_l + sn_r) * weight
    drift = (st_l + st_r) * weight
    half = (0.5 * GRAVITY) * (depth_l + depth_r)
    inverse = lax.rsqrt(half)
    celerity = half * inverse
    jump = depth_r - depth_l
    excess = (normal_r - normal_l) - speed * jump
    bend = excess * (0.5 * inverse)
    half_jump = 0.5 * jump
    slow = speed - celerity
    fast = speed + celerity
    wave_one = jnp.abs(slow) * (half_jump - bend)
    wave_three = jnp.abs(fast) * (half_jump + bend)
    wave_two = jnp.abs(speed) * ((tangent_r - tangent_l) - drift * jump)
    both = wave_one + wave_three
    flux_depth = (normal_l + normal_r) - both
    flux_normal = (press_l + press_r) - speed * both - celerity * (wave_three - wave_one)
    flux_tangent = (shear_l + shear_r) - drift * both - wave_two
    return flux_depth, flux_normal, flux_tangent


def side(depth, normal, tangent, root, sn, st):
    press = sn * sn + (0.5 * GRAVITY) * (depth * depth)
    return (depth, normal, tangent, root, sn, st, press, sn * st)


def flux_kernel(state_ref, fixed_ref, diff_ref, derived, faces):
    lane_tiles = state_ref.shape[1]
    padded = state_ref.shape[2]
    row_tiles = padded // 8

    def derive(r, carry):
        at = pl.ds(pl.multiple_of(r * 24, 8), 24)
        for c in range(lane_tiles):
            depth = state_ref[0, c, at, :]
            inverse = lax.rsqrt(depth)
            derived[0, c, at, :] = depth * inverse
            derived[1, c, at, :] = state_ref[1, c, at, :] * inverse
            derived[2, c, at, :] = state_ref[2, c, at, :] * inverse
        return carry

    lax.fori_loop(0, padded // 24, derive, 0)
    lane = lane_ids(8)
    for f in range(3):
        for c in range(lane_tiles):
            faces[f, c, 0:8, :] = jnp.zeros((8, LANES), jnp.float32)
            diff_ref[f, c, padded - 8 : padded, :] = jnp.zeros((8, LANES), jnp.float32)

    def load(c, at):
        return [state_ref[k, c, at, :] for k in range(3)] + [derived[k, c, at, :] for k in range(3)]

    def flip(v):
        return (v[0], v[2], v[1], v[3], v[5], v[4])

    def row_faces(r, carry):
        at = pl.multiple_of(r * 8, 8)
        here, below = pl.ds(at, 8), pl.ds(at + 1, 8)
        now = [load(c, here) for c in range(lane_tiles)]
        across = []
        for c in range(lane_tiles):
            nxt = now[(c + 1) % lane_tiles]
            right = [
                pltpu.roll(jnp.where(lane == 0, b, a), LANES - 1, 1)
                for a, b in zip(now[c], nxt)
            ]
            f_depth, f_across, f_along = roe(side(*flip(now[c])), side(*flip(right)))
            across.append((f_depth, f_along, f_across))
            flux = roe(side(*now[c]), side(*load(c, below)))
            for f in range(3):
                faces[f, c, pl.ds(at + 8, 8), :] = flux[f]
        for c in range(lane_tiles):
            prev = across[(c - 1) % lane_tiles]
            active = fixed_ref[0, c, here, :] > 0.5
            for f in range(3):
                left = pltpu.roll(jnp.where(lane == LANES - 1, prev[f], across[c][f]), 1, 1)
                out = (across[c][f] - left) + (
                    faces[f, c, pl.ds(at + 8, 8), :] - faces[f, c, pl.ds(at + 7, 8), :]
                )
                if f == 0:
                    out = out - 2.0 * fixed_ref[1, c, here, :]
                diff_ref[f, c, here, :] = jnp.where(active, out, 0.0)
        return carry

    lax.fori_loop(0, row_tiles - 1, row_faces, 0)


def step_ratio(peak_ref):
    peak = jnp.max(jnp.max(peak_ref[...], axis=0), axis=0, keepdims=True)
    step = (COURANT * SPACING) / peak
    return jnp.broadcast_to((0.5 / SPACING) * step, (8, LANES))


def update_kernel(wet_ref, peak_ref, state_in, diff_ref, state_ref, next_ref):
    lane_tiles = state_in.shape[1]
    padded = state_in.shape[2]
    blocks = wet_ref.shape[0]
    own_tiles = lane_tiles - 1
    block_rows = (padded - 3 * 8) // blocks
    ratio = step_ratio(peak_ref)

    def move(c, at):
        new = [state_in[f, c, at, :] - ratio * diff_ref[f, c, at, :] for f in range(3)]
        for f in range(3):
            state_ref[f, c, at, :] = new[f]
        return new

    def one_block(b, acc):
        wet = wet_ref[b, 0] > 0
        for r in range(0, block_rows, 8):
            at = pl.ds(pl.multiple_of(b * block_rows + TOP + r, 8), 8)
            for c in range(lane_tiles):
                new = move(c, at)
                if c < own_tiles:
                    acc = jnp.maximum(acc, jnp.where(wet, speed_of(*new), 0.0))
        return acc

    acc = lax.fori_loop(0, blocks, one_block, jnp.zeros((8, LANES), jnp.float32))
    for at in (pl.ds(0, 8), pl.ds(padded - 16, 8), pl.ds(padded - 8, 8)):
        for c in range(lane_tiles):
            move(c, at)
    spread_peak(acc, next_ref)


def last_kernel(
    wet_ref, plan_ref, peak_ref, state_in, diff_ref, depth_ref, mom_ref, next_ref, best
):
    blocks = wet_ref.shape[0]
    rows, cols = depth_ref.shape
    block_rows = rows // blocks
    ratio = step_ratio(peak_ref)
    best[...] = jnp.zeros_like(best)

    def one_block(b, carry):
        wet = wet_ref[b, 0] > 0
        acc = jnp.zeros((8, LANES), jnp.float32)
        for r in range(0, block_rows, 8):
            out = pl.multiple_of(b * block_rows + r, 8)
            at = pl.ds(pl.multiple_of(out + TOP, 8), 8)
            out = pl.ds(out, 8)
            for c in range(cols // LANES):
                new = [state_in[f, c, at, :] - ratio * diff_ref[f, c, at, :] for f in range(3)]
                acc = jnp.maximum(acc, jnp.where(wet, speed_of(*new), 0.0))
                lanes = slice(c * LANES, (c + 1) * LANES)
                depth_ref[out, lanes] = new[0]
                mom_ref[0, out, lanes] = new[1]
                mom_ref[1, out, lanes] = new[2]
        helper = jnp.maximum(plan_ref[b, 0], 0)
        best[helper] = jnp.maximum(best[helper], acc)
        return carry

    lax.fori_loop(0, blocks, one_block, 0)
    for t in range(best.shape[0]):
        top = jnp.max(best[t], axis=0, keepdims=True)
        next_ref[t] = jnp.broadcast_to(jnp.max(top, axis=1, keepdims=True), (1, LANES))


def exchange(x, axes):
    return lax.all_to_all(x, axes, 0, 0)


def send(x, axis, forward):
    count = lax.axis_size(axis)
    pairs = [(i, i + 1) if forward else (i + 1, i) for i in range(count - 1)]
    return lax.ppermute(x, axis, pairs)


def on_device(water_depth, momentum, wet_mask, helper_plan, breach_cells, breach_rate):
    rows, cols = water_depth.shape
    tile_count = lax.axis_size("tile")
    region_count = lax.axis_size("region")
    everyone = tile_count * region_count
    region_at = lax.axis_index("region")
    tile_at = lax.axis_index("tile")
    lane_tiles = cols // LANES + 1
    padded = rows + 3 * 8
    lanes_up = -(-padded // LANES) * LANES
    strip = (5 * HALO + 7) // 8 * 8
    f32 = jnp.float32
    edges = jnp.stack(
        [region_at == 0, region_at == region_count - 1, tile_at == 0, tile_at == tile_count - 1]
    ).astype(jnp.int32)
    cells = breach_cells.reshape(-1)
    rates = breach_rate.reshape(-1)
    nbytes = 4 * 3 * rows * cols

    peak, source, up, down = pl.pallas_call(
        start_kernel,
        out_shape=(
            vmem_out(everyone, 1, LANES),
            vmem_out(rows, cols),
            vmem_out(5, HALO, cols),
            vmem_out(5, HALO, cols),
        ),
        in_specs=[smem_spec()] * 3 + [vmem_spec()] * 2,
        out_specs=(vmem_spec(),) * 4,
        compiler_params=params(),
        cost_estimate=cost(20 * rows * cols, nbytes),
        name="start",
    )(wet_mask, cells, rates, water_depth, momentum)

    peaks = exchange(peak, ("region", "tile"))
    above = send(down, "region", True)
    below = send(up, "region", False)

    state, fixed, left, right = pl.pallas_call(
        rows_kernel,
        out_shape=(
            vmem_out(3, lane_tiles, padded, LANES),
            vmem_out(2, lane_tiles, padded, LANES),
            vmem_out(strip, lanes_up),
            vmem_out(strip, lanes_up),
        ),
        in_specs=[smem_spec()] * 2 + [vmem_spec()] * 5,
        out_specs=(vmem_spec(),) * 4,
        scratch_shapes=[pltpu.VMEM((lanes_up, LANES), f32)],
        compiler_params=params(),
        cost_estimate=cost(20 * rows * cols, nbytes),
        name="rows",
    )(edges, wet_mask, water_depth, momentum, source, above, below)

    from_left = send(right, "tile", True)
    from_right = send(left, "tile", False)

    state, fixed = pl.pallas_call(
        columns_kernel,
        out_shape=(
            vmem_out(3, lane_tiles, padded, LANES),
            vmem_out(2, lane_tiles, padded, LANES),
        ),
        in_specs=[smem_spec()] + [vmem_spec()] * 6,
        out_specs=(vmem_spec(),) * 2,
        scratch_shapes=[pltpu.VMEM((LANES, lanes_up), f32), pltpu.VMEM((lanes_up, LANES), f32)],
        input_output_aliases={1: 0, 2: 1},
        compiler_params=params(),
        cost_estimate=cost(10 * rows * cols, nbytes),
        name="columns",
    )(edges, state, fixed, left, right, from_left, from_right)

    for step in range(STEPS):
        diff = pl.pallas_call(
            flux_kernel,
            out_shape=vmem_out(3, lane_tiles, padded, LANES),
            in_specs=[vmem_spec()] * 2,
            out_specs=vmem_spec(),
            scratch_shapes=[
                pltpu.VMEM((3, lane_tiles, padded, LANES), f32),
                pltpu.VMEM((3, lane_tiles, padded + 8, LANES), f32),
            ],
            compiler_params=params(),
            cost_estimate=cost(150 * rows * cols, 4 * nbytes),
            name="flux",
        )(state, fixed)
        if step < STEPS - 1:
            state, peak = pl.pallas_call(
                update_kernel,
                out_shape=(
                    vmem_out(3, lane_tiles, padded, LANES),
                    vmem_out(everyone, 1, LANES),
                ),
                in_specs=[smem_spec()] + [vmem_spec()] * 3,
                out_specs=(vmem_spec(),) * 2,
                input_output_aliases={2: 0},
                compiler_params=params(),
                cost_estimate=cost(20 * rows * cols, nbytes),
                name="update",
            )(wet_mask, peaks, state, diff)
            peaks = exchange(peak, ("region", "tile"))

    new_depth, new_momentum, best = pl.pallas_call(
        last_kernel,
        out_shape=(
            jax.ShapeDtypeStruct((rows, cols), f32),
            jax.ShapeDtypeStruct((2, rows, cols), f32),
            vmem_out(tile_count, 1, LANES),
        ),
        in_specs=[smem_spec()] * 2 + [vmem_spec()] * 3,
        out_specs=(vmem_spec(),) * 3,
        scratch_shapes=[pltpu.VMEM((tile_count, 8, LANES), f32)],
        compiler_params=params(),
        cost_estimate=cost(20 * rows * cols, 2 * nbytes),
        name="last",
    )(wet_mask, helper_plan, peaks, state, diff)
    helper = jnp.max(exchange(best, "tile")[:, :, :1], axis=0)
    return new_depth, new_momentum, helper


def solution(mesh):
    return jax.shard_map(
        on_device,
        mesh=mesh,
        in_specs=(
            P("region", "tile"),
            P(None, "region", "tile"),
            P("region", "tile"),
            P("region", "tile"),
            P("region", "tile", None),
            P("region", "tile", None),
        ),
        out_specs=(P("region", "tile"), P(None, "region", "tile"), P("region", "tile")),
        check_vma=False,
    )
```

time: 354 us -> 127 us (0.36); the launches traced: 349 us -> 126 us
  blocking collectives: 179 us -> 8.39 us
  other arithmetic: 101 us -> 0.68 us
  Pallas kernels: 0 us -> 58.4 us
  local copies, waits for them, and re-layouts: 48.8 us -> 20.1 us
  starting transfers between devices: 10.5 us -> 34.1 us
  between operations: 5.15 us -> 0.82 us
    pmax x5 -> x0, blocking collectives: 179 us -> none  [the longest x4 166 us: run_steps(): speed_peak = lax.pmax(local_peak, ('region', 'tile'))]
    pallas_call x0 -> x11, Pallas kernels: none -> 58.4 us  [the longest x4 35.4 us: on_device(): pl.pallas_call(flux_kernel, out_shape=vmem_out(3, lane_tiles, padded, LAN...]
    sub x21 -> x0, other arithmetic: 48.5 us -> none  [the longest x8 22.5 us: roe_flux(): 0.5 * (normal_left * drift_left + normal_right * drift_right)]
    select_n x49 -> x0, other arithmetic: 31.3 us -> none  [the longest x12 12.4 us: mirror(): values = jnp.where(left_side, left_fix, values)]
    slice x88 -> x0, local copies, waits for them, and re-layouts: 25.3 us -> none  [the longest x12 11.8 us: mirror(): values[:, :, 4:]]
    all_to_all x0 -> x4, starting transfers between devices: none -> 25.3 us  [exchange(): return lax.all_to_all(x, axes, 0, 0)]
    unnamed x52 -> x40, local copies, waits for them, and re-layouts: 3.53 us -> 20.1 us
    rev x48 -> x0, local copies, waits for them, and re-layouts: 15.4 us -> none  [the longest x12 7 us: mirror(): jnp.flip(values[:, :, 4:8], 2)]
  transfers between devices with their start and end apart: 4 -> 8, of which waited for: 3 -> 2; matrix products, arithmetic and copies ran while one was open for 1% -> 0% of each run, Pallas kernels for 0% -> 32%
where the time goes in v1:
time: 127 us; the launch traced here: 126 us
  Pallas kernels  58.4 us (46%)
  starting transfers between devices  34.1 us (27%)
  local copies, waits for them, and re-layouts  20.1 us (16%)
  blocking collectives  8.39 us (7%)
  waiting for transfers between devices  3.7 us (3%)
    pallas_call x4, Pallas kernels, on_device(): pl.pallas_call(flux_kernel, out_shape=vmem_out(3, lane_tiles, padded, LAN...  35.4 us
    all_to_all x4, starting transfers between devices, exchange(): return lax.all_to_all(x, axes, 0, 0)  25.3 us
    unnamed x40, local copies, waits for them, and re-layouts  20.1 us
    ppermute x4, starting transfers between devices, send(): return lax.ppermute(x, axis, pairs)  8.78 us
    all_to_all x1, blocking collectives, exchange(): return lax.all_to_all(x, axes, 0, 0)  8.39 us
    pallas_call x3, Pallas kernels, on_device(): pl.pallas_call(update_kernel, out_shape=(vmem_out(3, lane_tiles, padded,...  7.04 us
    pallas_call x1, Pallas kernels, on_device(): pl.pallas_call(rows_kernel, out_shape=(vmem_out(3, lane_tiles, padded, LA...  5.75 us
    pallas_call x1, Pallas kernels, on_device(): pl.pallas_call(columns_kernel, out_shape=(vmem_out(3, lane_tiles, padded,...  4.96 us
  transfers between devices with their start and end apart: 8, of which 2 were waited for; matrix products, arithmetic and copies ran while one was open for 0% of the time, Pallas kernels for 32%

profile of v1, /device:TPU:0, one launch (start us, length us, event | category | flops | bytes accessed | tf_op | source)
XLA Modules:
  0.0 126.2 jit_solution(17013661332020315865)
XLA Ops:
  4.8 2.9 %start.1 = (f32[32,1,128]{2,1,0:T(1,128)}, f32[384,256]{1,0:T(8,128)S(1)}, f32[5,4,256]{2,1,0:T(4,128)S(1)}, f32[5,4,256]{2,1,0:T(4,128)S(1)}) custom-call(s32[24,1]{1,0:T(8,128)S(1)} %copy.19.wet_ref, s32[64]{0:T(128)S(1)} %bitcast.7, f32[64]{0:T(128)S(1)} %bitcast.8, f32[384,256]{1,0:T(8,128)S(1)} %copy-done.10, f32[2,384,256]{2,1,0:T(8,128)S(1)} %copy-done.8), custom_call_target="tpu_custom_call" | custom-call | flops 1966080 | bytes 1179648 | tf_op jit(solution)/shard_map/start/pallas_call | solution.py:410
  7.7 4.9 %collective-permute-start = (f32[5,4,256]{2,1,0:T(4,128)S(1)}, f32[5,4,256]{2,1,0:T(4,128)S(1)}, u32[]{:S(2)}, u32[]{:S(2)}) collective-permute-start(f32[5,4,256]{2,1,0:T(4,128)S(1)} %get-tuple-element.24), channel_id=1, source_target_pairs={{0,8},{8,16},{16,24},{1,9},{9,17},{17,25},{2,10},{10,18},{18,26},{... | collective-permute-start | bytes 61448 | tf_op jit(solution)/shard_map/ppermute | solution.py:388
  12.6 1.3 %collective-permute-start.1 = (f32[5,4,256]{2,1,0:T(4,128)S(1)}, f32[5,4,256]{2,1,0:T(4,128)S(1)}, u32[]{:S(2)}, u32[]{:S(2)}) collective-permute-start(f32[5,4,256]{2,1,0:T(4,128)S(1)} %get-tuple-element.25), channel_id=1, source_target_pairs={{8,0},{16,8},{24,16},{9,1},{17,9},{25,17},{10,2},{18,10},{26,18},{... | collective-permute-start | bytes 61448 | tf_op jit(solution)/shard_map/ppermute | solution.py:388
  14.7 3.6 %collective-permute-done.1.below_ref = f32[5,4,256]{2,1,0:T(4,128)S(1)} collective-permute-done((f32[5,4,256]{2,1,0:T(4,128)S(1)}, f32[5,4,256]{2,1,0:T(4,128)S(1)}, u32[]{:S(2)}, u32[]{:S(2)}) %collective-permute-start.1) | collective-permute-done | bytes 20512 | tf_op jit(solution)/shard_map/ppermute | solution.py:388
  22.5 5.7 %rows.1 = (f32[3,3,408,128]{3,2,1,0:T(8,128)S(1)}, f32[2,3,408,128]{3,2,1,0:T(8,128)S(1)}, f32[24,512]{1,0:T(8,128)}, f32[24,512]{1,0:T(8,128)}) custom-call(s32[4]{0:T(128)S(1)} %add_convert_fusion.edge_ref, s32[24,1]{1,0:T(8,128)S(1)} %copy.19.wet_ref, f32[384,256]{1,0:T(8,128)S(1)} %copy-done.11, f32[2,384,256]{2,1,0:T(8,128)S(1)} %copy-done.9, ...), custom_call_target="tpu_custom_call" | custom-call | flops 1966080 | bytes 1179648 | tf_op jit(solution)/shard_map/rows/pallas_call | solution.py:429
  29.5 1.3 %collective-permute-start.3 = (f32[24,512]{1,0:T(8,128)}, f32[24,512]{1,0:T(8,128)S(1)}, u32[]{:S(2)}, u32[]{:S(2)}) collective-permute-start(f32[24,512]{1,0:T(8,128)} %get-tuple-element.28.own_left), channel_id=1, source_target_pairs={{1,0},{2,1},{3,2},{4,3},{5,4},{6,5},{7,6},{9,8},{10,9},{11,10},{12... | collective-permute-start | bytes 147464 | tf_op jit(solution)/shard_map/ppermute | solution.py:388
  30.8 7.8 %all-to-all-start = ((f32[32,1,128]{2,1,0:T(1,128)}), f32[32,1,128]{2,1,0:T(1,128)S(1)}, u32[]{:S(2)}, u32[]{:S(2)}) async-start(f32[32,1,128]{2,1,0:T(1,128)} %get-tuple-element.22), calls=%async_computation | async-start | bytes 32768 | tf_op jit(solution)/shard_map/all_to_all | solution.py:382
  38.7 5.0 %columns.1 = (f32[3,3,408,128]{3,2,1,0:T(8,128)S(1)}, f32[2,3,408,128]{3,2,1,0:T(8,128)S(1)}) custom-call(s32[4]{0:T(128)S(1)} %add_convert_fusion.edge_ref, f32[3,3,408,128]{3,2,1,0:T(8,128)S(1)} %get-tuple-element.26.state_in, f32[2,3,408,128]{3,2,1,0:T(8,128)S(1)} %get-tuple-element.27.fixed_in, ...), custom_call_target="tpu_custom_call", output_to_operand_aliasing={{0}: (1, {}), {1}: (2, {})} | custom-call | flops 983040 | bytes 1179648 | tf_op jit(solution)/shard_map/columns/pallas_call | solution.py:448
  43.6 8.8 %flux.4.diff_ref = f32[3,3,408,128]{3,2,1,0:T(8,128)S(1)} custom-call(f32[3,3,408,128]{3,2,1,0:T(8,128)S(1)} %get-tuple-element.30.state_ref.state_in, f32[2,3,408,128]{3,2,1,0:T(8,128)S(1)} %get-tuple-element.31.fixed_ref), custom_call_target="tpu_custom_call" | custom-call | flops 14745600 | bytes 4718592 | tf_op jit(solution)/shard_map/flux/pallas_call | solution.py:464
  53.8 1.5 %copy-done.1 = f32[3,3,408,128]{3,2,1,0:T(8,128)S(1)} copy-done((f32[3,3,408,128]{3,2,1,0:T(8,128)S(1)}, f32[3,3,408,128]{3,2,1,0:T(8,128)}, u32[]{:S(2)}) %copy-start.1) | copy-done | bytes 1880088
  55.3 2.3 %update.3 = (f32[3,3,408,128]{3,2,1,0:T(8,128)S(1)}, f32[32,1,128]{2,1,0:T(1,128)}) custom-call(s32[24,1]{1,0:T(8,128)S(1)} %copy.19.wet_ref, f32[32,1,128]{2,1,0:T(1,128)S(1)} %all-to-all-done.peak_ref, f32[3,3,408,128]{3,2,1,0:T(8,128)S(1)} %get-tuple-element.30.state_ref.state_in, f32[3,3,408,128]{3,2,1,0:T(8,128)S(1)} %copy-done.1), custom_call_target="tpu_custom_call", output_to_operand_aliasing={{0}: (2, {})} | custom-call | flops 1966080 | bytes 1179648 | tf_op jit(solution)/shard_map/update/pallas_call | solution.py:478
  57.6 5.8 %all-to-all-start.1 = ((f32[32,1,128]{2,1,0:T(1,128)}), f32[32,1,128]{2,1,0:T(1,128)S(1)}, u32[]{:S(2)}, u32[]{:S(2)}) async-start(f32[32,1,128]{2,1,0:T(1,128)} %get-tuple-element.32), calls=%async_computation.1 | async-start | bytes 32768 | tf_op jit(solution)/shard_map/all_to_all | solution.py:382
  63.5 8.8 %flux.5.diff_ref = f32[3,3,408,128]{3,2,1,0:T(8,128)S(1)} custom-call(f32[3,3,408,128]{3,2,1,0:T(8,128)S(1)} %get-tuple-element.33.state_ref.state_in, f32[2,3,408,128]{3,2,1,0:T(8,128)S(1)} %get-tuple-element.31.fixed_ref), custom_call_target="tpu_custom_call" | custom-call | flops 14745600 | bytes 4718592 | tf_op jit(solution)/shard_map/flux/pallas_call | solution.py:464
  73.6 1.5 %copy-done.3 = f32[3,3,408,128]{3,2,1,0:T(8,128)S(1)} copy-done((f32[3,3,408,128]{3,2,1,0:T(8,128)S(1)}, f32[3,3,408,128]{3,2,1,0:T(8,128)}, u32[]{:S(2)}) %copy-start.3) | copy-done | bytes 1880088
  75.1 2.3 %update.4 = (f32[3,3,408,128]{3,2,1,0:T(8,128)S(1)}, f32[32,1,128]{2,1,0:T(1,128)}) custom-call(s32[24,1]{1,0:T(8,128)S(1)} %copy.19.wet_ref, f32[32,1,128]{2,1,0:T(1,128)S(1)} %all-to-all-done.1.peak_ref, f32[3,3,408,128]{3,2,1,0:T(8,128)S(1)} %get-tuple-element.33.state_ref.state_in, f32[3,3,408,128]{3,2,1,0:T(8,128)S(1)} %copy-done.3), custom_call_target="tpu_custom_call", output_to_operand_aliasing={{0}: (2, {})} | custom-call | flops 1966080 | bytes 1179648 | tf_op jit(solution)/shard_map/update/pallas_call | solution.py:478
  77.4 5.8 %all-to-all-start.2 = ((f32[32,1,128]{2,1,0:T(1,128)}), f32[32,1,128]{2,1,0:T(1,128)S(1)}, u32[]{:S(2)}, u32[]{:S(2)}) async-start(f32[32,1,128]{2,1,0:T(1,128)} %get-tuple-element.34), calls=%async_computation.2 | async-start | bytes 32768 | tf_op jit(solution)/shard_map/all_to_all | solution.py:382
  83.3 8.8 %flux.6.diff_ref = f32[3,3,408,128]{3,2,1,0:T(8,128)S(1)} custom-call(f32[3,3,408,128]{3,2,1,0:T(8,128)S(1)} %get-tuple-element.35.state_ref.state_in, f32[2,3,408,128]{3,2,1,0:T(8,128)S(1)} %get-tuple-element.31.fixed_ref), custom_call_target="tpu_custom_call" | custom-call | flops 14745600 | bytes 4718592 | tf_op jit(solution)/shard_map/flux/pallas_call | solution.py:464
  93.4 1.5 %copy-done.5 = f32[3,3,408,128]{3,2,1,0:T(8,128)S(1)} copy-done((f32[3,3,408,128]{3,2,1,0:T(8,128)S(1)}, f32[3,3,408,128]{3,2,1,0:T(8,128)}, u32[]{:S(2)}) %copy-start.5) | copy-done | bytes 1880088
  94.9 2.3 %update.5 = (f32[3,3,408,128]{3,2,1,0:T(8,128)S(1)}, f32[32,1,128]{2,1,0:T(1,128)}) custom-call(s32[24,1]{1,0:T(8,128)S(1)} %copy.19.wet_ref, f32[32,1,128]{2,1,0:T(1,128)S(1)} %all-to-all-done.2.peak_ref, f32[3,3,408,128]{3,2,1,0:T(8,128)S(1)} %get-tuple-element.35.state_ref.state_in, f32[3,3,408,128]{3,2,1,0:T(8,128)S(1)} %copy-done.5), custom_call_target="tpu_custom_call", output_to_operand_aliasing={{0}: (2, {})} | custom-call | flops 1966080 | bytes 1179648 | tf_op jit(solution)/shard_map/update/pallas_call | solution.py:478
  97.2 5.8 %all-to-all-start.3 = ((f32[32,1,128]{2,1,0:T(1,128)}), f32[32,1,128]{2,1,0:T(1,128)S(1)}, u32[]{:S(2)}, u32[]{:S(2)}) async-start(f32[32,1,128]{2,1,0:T(1,128)} %get-tuple-element.36), calls=%async_computation.3 | async-start | bytes 32768 | tf_op jit(solution)/shard_map/all_to_all | solution.py:382
  103.2 8.8 %flux.7.diff_ref = f32[3,3,408,128]{3,2,1,0:T(8,128)S(1)} custom-call(f32[3,3,408,128]{3,2,1,0:T(8,128)S(1)} %get-tuple-element.37.state_ref.state_in, f32[2,3,408,128]{3,2,1,0:T(8,128)S(1)} %get-tuple-element.31.fixed_ref), custom_call_target="tpu_custom_call" | custom-call | flops 14745600 | bytes 4718592 | tf_op jit(solution)/shard_map/flux/pallas_call | solution.py:464
  113.3 1.5 %copy-done.7 = f32[3,3,408,128]{3,2,1,0:T(8,128)S(1)} copy-done((f32[3,3,408,128]{3,2,1,0:T(8,128)S(1)}, f32[3,3,408,128]{3,2,1,0:T(8,128)}, u32[]{:S(2)}) %copy-start.7) | copy-done | bytes 1880088
  114.8 2.4 %last.1 = (f32[384,256]{1,0:T(8,128)}, f32[2,384,256]{2,1,0:T(8,128)}, f32[8,1,128]{2,1,0:T(1,128)S(1)}) custom-call(s32[24,1]{1,0:T(8,128)S(1)} %copy.19.wet_ref, s32[24,1]{1,0:T(8,128)S(1)} %copy.20.plan_ref, f32[32,1,128]{2,1,0:T(1,128)S(1)} %all-to-all-done.3.peak_ref, f32[3,3,408,128]{3,2,1,0:T(8,128)S(1)} %get-tuple-element.37.state_ref.state_in, ...), custom_call_target="tpu_custom_call" | custom-call | flops 1966080 | bytes 2359296 | tf_op jit(solution)/shard_map/last/pallas_call | solution.py:493
  117.2 8.4 %all_to_all.25 = f32[8,1,128]{2,1,0:T(1,128)S(1)} all-to-all(f32[8,1,128]{2,1,0:T(1,128)S(1)} %get-tuple-element.40), channel_id=1, replica_groups=mesh['region'=4,'tile'=8] {'tile'}, dimensions={0} | all-to-all | bytes 8192 | tf_op jit(solution)/shard_map/all_to_all | solution.py:382
  (46 shorter events, 16.1 us)
Async XLA Ops:
  1.4 1.1 copy-start.8
  2.5 1.0 copy-start.10
  3.5 0.7 copy-start.16
  7.7 6.4 %collective-permute-start = (f32[5,4,256]{2,1,0:T(4,128)S(1)}, f32[5,4,256]{2,1,0:T(4,128)S(1)}, u32[]{:S(2)}, u32[]{:S(2)}) collective-permute-start(f32[5,4,256]{2,1,0:T(4,128)S(1)} %get-tuple-element.24), channel_id=1, source_target_pairs={{0,8},{8,16},{16,24},{1,9},{9,17},{17,25},{2,10},{10,18},{18,26},{... | collective-permute-start | bytes 61448 | tf_op jit(solution)/shard_map/ppermute | solution.py:388
  12.6 5.7 %collective-permute-start.1 = (f32[5,4,256]{2,1,0:T(4,128)S(1)}, f32[5,4,256]{2,1,0:T(4,128)S(1)}, u32[]{:S(2)}, u32[]{:S(2)}) collective-permute-start(f32[5,4,256]{2,1,0:T(4,128)S(1)} %get-tuple-element.25), channel_id=1, source_target_pairs={{8,0},{16,8},{24,16},{9,1},{17,9},{25,17},{10,2},{18,10},{26,18},{... | collective-permute-start | bytes 61448 | tf_op jit(solution)/shard_map/ppermute | solution.py:388
  18.9 1.1 copy-start.9
  20.0 1.0 copy-start.11
  21.0 0.7 copy-start.13
  21.8 0.7 copy-start.15
  28.2 10.4 %collective-permute-start.2 = (f32[24,512]{1,0:T(8,128)}, f32[24,512]{1,0:T(8,128)S(1)}, u32[]{:S(2)}, u32[]{:S(2)}) collective-permute-start(f32[24,512]{1,0:T(8,128)} %get-tuple-element.29.own_right), channel_id=1, source_target_pairs={{0,1},{1,2},{2,3},{3,4},{4,5},{5,6},{6,7},{8,9},{9,10},{10,11},{11... | collective-permute-start | bytes 147464 | tf_op jit(solution)/shard_map/ppermute | solution.py:388
  29.5 9.1 %collective-permute-start.3 = (f32[24,512]{1,0:T(8,128)}, f32[24,512]{1,0:T(8,128)S(1)}, u32[]{:S(2)}, u32[]{:S(2)}) collective-permute-start(f32[24,512]{1,0:T(8,128)} %get-tuple-element.28.own_left), channel_id=1, source_target_pairs={{1,0},{2,1},{3,2},{4,3},{5,4},{6,5},{7,6},{9,8},{10,9},{11,10},{12... | collective-permute-start | bytes 147464 | tf_op jit(solution)/shard_map/ppermute | solution.py:388
  30.8 22.9 %all-to-all-start = ((f32[32,1,128]{2,1,0:T(1,128)}), f32[32,1,128]{2,1,0:T(1,128)S(1)}, u32[]{:S(2)}, u32[]{:S(2)}) async-start(f32[32,1,128]{2,1,0:T(1,128)} %get-tuple-element.22), calls=%async_computation | async-start | bytes 32768 | tf_op jit(solution)/shard_map/all_to_all | solution.py:382
  52.5 1.3 %copy-start = (f32[3,3,408,128]{3,2,1,0:T(8,128)}, f32[3,3,408,128]{3,2,1,0:T(8,128)S(1)}, u32[]{:S(2)}) copy-start(f32[3,3,408,128]{3,2,1,0:T(8,128)S(1)} %flux.4.diff_ref) | copy-start | bytes 5640196
  53.8 1.5 %copy-start.1 = (f32[3,3,408,128]{3,2,1,0:T(8,128)S(1)}, f32[3,3,408,128]{3,2,1,0:T(8,128)}, u32[]{:S(2)}) copy-start(f32[3,3,408,128]{3,2,1,0:T(8,128)} %copy-done) | copy-start | bytes 5640196
  57.6 15.9 %all-to-all-start.1 = ((f32[32,1,128]{2,1,0:T(1,128)}), f32[32,1,128]{2,1,0:T(1,128)S(1)}, u32[]{:S(2)}, u32[]{:S(2)}) async-start(f32[32,1,128]{2,1,0:T(1,128)} %get-tuple-element.32), calls=%async_computation.1 | async-start | bytes 32768 | tf_op jit(solution)/shard_map/all_to_all | solution.py:382
  72.3 1.3 copy-start.2
  73.6 1.5 %copy-start.3 = (f32[3,3,408,128]{3,2,1,0:T(8,128)S(1)}, f32[3,3,408,128]{3,2,1,0:T(8,128)}, u32[]{:S(2)}) copy-start(f32[3,3,408,128]{3,2,1,0:T(8,128)} %copy-done.2) | copy-start | bytes 5640196
  77.4 15.9 %all-to-all-start.2 = ((f32[32,1,128]{2,1,0:T(1,128)}), f32[32,1,128]{2,1,0:T(1,128)S(1)}, u32[]{:S(2)}, u32[]{:S(2)}) async-start(f32[32,1,128]{2,1,0:T(1,128)} %get-tuple-element.34), calls=%async_computation.2 | async-start | bytes 32768 | tf_op jit(solution)/shard_map/all_to_all | solution.py:382
  92.1 1.3 copy-start.4
  93.4 1.5 %copy-start.5 = (f32[3,3,408,128]{3,2,1,0:T(8,128)S(1)}, f32[3,3,408,128]{3,2,1,0:T(8,128)}, u32[]{:S(2)}) copy-start(f32[3,3,408,128]{3,2,1,0:T(8,128)} %copy-done.4) | copy-start | bytes 5640196
  94.9 8.2 %copy-start.18 = (s32[24,1]{0,1:T(1,128)S(1)}, s32[24,1]{0,1:T(1,128)}, u32[]{:S(2)}) copy-start(s32[24,1]{0,1:T(1,128)} %param.9) | copy-start | bytes 292
  97.2 16.0 %all-to-all-start.3 = ((f32[32,1,128]{2,1,0:T(1,128)}), f32[32,1,128]{2,1,0:T(1,128)S(1)}, u32[]{:S(2)}, u32[]{:S(2)}) async-start(f32[32,1,128]{2,1,0:T(1,128)} %get-tuple-element.36), calls=%async_computation.3 | async-start | bytes 32768 | tf_op jit(solution)/shard_map/all_to_all | solution.py:382
  112.0 1.3 copy-start.6
  113.3 1.5 %copy-start.7 = (f32[3,3,408,128]{3,2,1,0:T(8,128)S(1)}, f32[3,3,408,128]{3,2,1,0:T(8,128)}, u32[]{:S(2)}) copy-start(f32[3,3,408,128]{3,2,1,0:T(8,128)} %copy-done.6) | copy-start | bytes 5640196
  (3 other events, 1.9 us)

commit v2 on v1

v2 whole, which is shorter than its diff:
```python
import jax
import jax.numpy as jnp
from jax import lax
from jax.experimental import pallas as pl
from jax.experimental.pallas import tpu as pltpu
from jax.sharding import PartitionSpec as P

STEPS = 4
HALO = 4
LANES = 128
TOP = 8

GRAVITY = 9.81
COURANT = 0.45
SPACING = 1.0

VMEM_LIMIT = 20 << 20


WORK = 8
SEND = 5
ACTIVE, SOURCE, DIFF = 3, 4, 5


def vmem_spec():
    return pl.BlockSpec(memory_space=pltpu.VMEM)


def hbm_spec():
    return pl.BlockSpec(memory_space=pltpu.HBM)


def vmem_out(*shape):
    return pltpu.VMEM(shape, jnp.float32)


def params():
    return pltpu.CompilerParams(vmem_limit_bytes=VMEM_LIMIT)


def cost(flops, nbytes):
    return pl.CostEstimate(flops=flops, bytes_accessed=nbytes, transcendentals=0)


def lane_ids(rows):
    return lax.broadcasted_iota(jnp.int32, (rows, LANES), 1)


def aligned(start, size):
    return pl.ds(pl.multiple_of(start, 8), size)


def speed_of(depth, along, across):
    root = lax.rsqrt(depth)
    inverse = root * root
    return jnp.maximum(jnp.abs(along), jnp.abs(across)) * inverse + jnp.sqrt(
        jnp.float32(GRAVITY)
    ) * (depth * root)


def spread_peak(acc, out_ref):
    top = jnp.max(jnp.max(acc, axis=0, keepdims=True), axis=1, keepdims=True)
    out_ref[...] = jnp.broadcast_to(top[None], out_ref.shape)


def start_kernel(
    wet_hbm,
    plan_hbm,
    cell_hbm,
    rate_hbm,
    depth_hbm,
    mom_hbm,
    work,
    plan_ref,
    up_ref,
    down_ref,
    wet_ref,
    plan_smem,
    cell_ref,
    rate_ref,
    small_sem,
    big_sem,
):
    rows, cols = depth_hbm.shape
    tiles = cols // LANES
    padded = work.shape[2]
    blocks = wet_hbm.shape[0]
    block_rows = rows // blocks
    bottom = TOP + rows
    small = [
        pltpu.make_async_copy(src, dst, small_sem.at[i])
        for i, (src, dst) in enumerate(
            [
                (cell_hbm, cell_ref),
                (rate_hbm, rate_ref),
                (wet_hbm, wet_ref),
                (plan_hbm, plan_smem),
            ]
        )
    ]
    big = []
    for k, src in enumerate([depth_hbm, mom_hbm.at[0], mom_hbm.at[1]]):
        for c in range(tiles):
            big.append(
                pltpu.make_async_copy(
                    src.at[:, pl.ds(c * LANES, LANES)],
                    work.at[k, c, pl.ds(TOP, rows), :],
                    big_sem.at[k, c],
                )
            )
    for copy in small + big:
        copy.start()
    for k in range(SEND):
        fill = 1.0 if k == 0 else 0.0
        for c in range(tiles):
            work[k, c, 0:TOP, :] = jnp.full((TOP, LANES), fill, jnp.float32)
            work[k, c, bottom:padded, :] = jnp.full((padded - bottom, LANES), fill, jnp.float32)
        work[k, tiles] = jnp.full((padded, LANES), fill, jnp.float32)
    for c in range(tiles):
        work[SOURCE, c, TOP:bottom, :] = jnp.zeros((rows, LANES), jnp.float32)
    for copy in small:
        copy.wait()
    lane = lane_ids(1)

    def add_cell(i, carry):
        cell = cell_ref[i]
        row = lax.div(cell, cols)
        col = cell - row * cols
        c = lax.div(col, LANES)
        at = pl.ds(row + TOP, 1)
        work[SOURCE, c, at, :] += jnp.where(lane == col - c * LANES, rate_ref[i], 0.0)
        return carry

    lax.fori_loop(0, cell_ref.shape[0], add_cell, 0)
    for b in range(blocks):
        wet = wet_ref[b].astype(jnp.float32)
        at = slice(TOP + b * block_rows, TOP + (b + 1) * block_rows)
        for c in range(tiles):
            work[ACTIVE, c, at, :] = jnp.full((block_rows, LANES), wet)
        plan_ref[b] = jnp.full((8, LANES), plan_smem[b])
    for copy in big:
        copy.wait()
    for k in range(SEND):
        for c in range(tiles):
            up_ref[k * tiles + c] = work[k, c, TOP : TOP + HALO, :]
            down_ref[k * tiles + c] = work[k, c, bottom - HALO : bottom, :]


def packed(work, at, size, lane):
    tiles = work.shape[1] - 1
    out = None
    for k in range(SEND):
        ends = jnp.where(lane < HALO, work[k, 0, at, :], work[k, tiles - 1, at, :])
        ends = pltpu.roll(ends, 2 * HALO * k + HALO, 1)
        out = ends if out is None else jnp.where(lane >= 2 * HALO * k, ends, out)
    return out


def split_packed(turned, left_ref, right_ref, at):
    for k in range(SEND):
        lo = 2 * HALO * k
        right_ref[k, :, at] = turned[lo : lo + HALO, :]
        left_ref[k, :, at] = turned[lo + HALO : lo + 2 * HALO, :]


def pack_kernel(work, peak_ref, left_ref, right_ref, pack):
    tiles = work.shape[1] - 1
    rows = pack.shape[0]
    lane = lane_ids(8)

    def one(r, acc):
        at = aligned(r * 8 + TOP, 8)
        pack[aligned(r * 8, 8), :] = packed(work, at, 8, lane)
        active = work[ACTIVE, 0, at, :] > 0.5
        for c in range(tiles):
            speed = speed_of(work[0, c, at, :], work[1, c, at, :], work[2, c, at, :])
            acc = jnp.maximum(acc, jnp.where(active, speed, 0.0))
        return acc

    acc = lax.fori_loop(0, rows // 8, one, jnp.zeros((8, LANES), jnp.float32), unroll=8)
    spread_peak(acc, peak_ref)
    for q in range(rows // LANES):
        at = slice(q * LANES, (q + 1) * LANES)
        split_packed(pack[at, :].T, left_ref, right_ref, at)


def rows_kernel(
    work_in, left_in, right_in, above_ref, below_ref, work, left_ref, right_ref, pack
):
    tiles = work.shape[1] - 1
    padded = work.shape[2]
    bottom = padded - 2 * 8
    own = left_ref.shape[2] - LANES
    is_top = lax.axis_index("region") == 0
    is_bottom = lax.axis_index("region") == lax.axis_size("region") - 1

    def mirrored(first, step, to):
        for k in range(SEND):
            flip = -1.0 if k == 1 else 1.0
            for c in range(tiles):
                for j in range(HALO):
                    work[k, c, to - step * (1 + j), :] = work[k, c, first + step * j, :] * flip

    def received(ref, lo):
        for k in range(SEND):
            for c in range(tiles):
                work[k, c, lo : lo + HALO, :] = ref[k * tiles + c]

    pl.when(is_top)(lambda: mirrored(TOP, 1, TOP))
    pl.when(jnp.logical_not(is_top))(lambda: received(above_ref, TOP - HALO))
    pl.when(is_bottom)(lambda: mirrored(bottom - 1, -1, bottom - 1))
    pl.when(jnp.logical_not(is_bottom))(lambda: received(below_ref, bottom))
    pack[...] = jnp.zeros_like(pack)
    lane = lane_ids(8)
    pack[0:8, :] = packed(work, slice(0, 8), 8, lane)
    pack[8:16, :] = packed(work, slice(bottom, bottom + 8), 8, lane)
    split_packed(pack[...].T, left_ref, right_ref, slice(own, own + LANES))


def columns_kernel(
    work_in, own_left, own_right, from_left, from_right, work, both, turned
):
    last = work.shape[1] - 1
    own = own_left.shape[2] - LANES
    bottom = TOP + own
    is_left = lax.axis_index("tile") == 0
    is_right = lax.axis_index("tile") == lax.axis_size("tile") - 1

    def mirrored(ref, to):
        for k in range(SEND):
            flip = -1.0 if k == 2 else 1.0
            for j in range(HALO):
                both[2 * HALO * k + to + HALO - 1 - j, :] = ref[k, j, :] * flip

    def received(ref, to):
        for k in range(SEND):
            at = 2 * HALO * k + to
            both[at : at + HALO, :] = ref[k]

    both[2 * HALO * SEND :, :] = jnp.zeros((LANES - 2 * HALO * SEND, own + LANES), jnp.float32)
    pl.when(is_left)(lambda: mirrored(own_left, 0))
    pl.when(jnp.logical_not(is_left))(lambda: received(from_left, 0))
    pl.when(is_right)(lambda: mirrored(own_right, HALO))
    pl.when(jnp.logical_not(is_right))(lambda: received(from_right, HALO))
    for q in range(turned.shape[0] // LANES):
        at = slice(q * LANES, (q + 1) * LANES)
        turned[at, :] = both[:, at].T
    lane = lane_ids(8)
    inside = (lane < HALO) | (lane >= LANES - HALO)

    def place(strip, at):
        for k in range(SEND):
            moved = pltpu.roll(strip, LANES - HALO - 2 * HALO * k, 1)
            work[k, last, at, :] = jnp.where(inside, moved, 1.0 if k == 0 else 0.0)

    def one(r, carry):
        place(turned[aligned(r * 8, 8), :], aligned(r * 8 + TOP, 8))
        return carry

    lax.fori_loop(0, own // 8, one, 0, unroll=8)
    place(turned[own : own + 8, :], slice(0, 8))
    place(turned[own + 8 : own + 16, :], slice(bottom, bottom + 8))


def roe(left, right):
    depth_l, normal_l, tangent_l, root_l, sn_l, st_l, press_l, shear_l = left
    depth_r, normal_r, tangent_r, root_r, sn_r, st_r, press_r, shear_r = right
    weight = pl.reciprocal(root_l + root_r, approx=False)
    speed = (sn_l + sn_r) * weight
    drift = (st_l + st_r) * weight
    half = (0.5 * GRAVITY) * (depth_l + depth_r)
    inverse = lax.rsqrt(half)
    celerity = half * inverse
    jump = depth_r - depth_l
    excess = (normal_r - normal_l) - speed * jump
    bend = excess * (0.5 * inverse)
    half_jump = 0.5 * jump
    slow = speed - celerity
    fast = speed + celerity
    wave_one = jnp.abs(slow) * (half_jump - bend)
    wave_three = jnp.abs(fast) * (half_jump + bend)
    wave_two = jnp.abs(speed) * ((tangent_r - tangent_l) - drift * jump)
    both = wave_one + wave_three
    flux_depth = (normal_l + normal_r) - both
    flux_normal = (press_l + press_r) - speed * both - celerity * (wave_three - wave_one)
    flux_tangent = (shear_l + shear_r) - drift * both - wave_two
    return flux_depth, flux_normal, flux_tangent


def side(depth, normal, tangent, root, sn, st):
    press = sn * sn + (0.5 * GRAVITY) * (depth * depth)
    return (depth, normal, tangent, root, sn, st, press, sn * st)


def flux_kernel(work_in, work, derived, faces):
    lane_tiles = work.shape[1]
    padded = work.shape[2]
    row_tiles = padded // 8

    def derive(r, carry):
        at = aligned(r * 24, 24)
        for c in range(lane_tiles):
            depth = work[0, c, at, :]
            inverse = lax.rsqrt(depth)
            derived[0, c, at, :] = depth * inverse
            derived[1, c, at, :] = work[1, c, at, :] * inverse
            derived[2, c, at, :] = work[2, c, at, :] * inverse
        return carry

    lax.fori_loop(0, padded // 24, derive, 0)
    lane = lane_ids(8)
    for f in range(3):
        for c in range(lane_tiles):
            faces[f, c, 0:8, :] = jnp.zeros((8, LANES), jnp.float32)

    def load(c, at):
        return [work[k, c, at, :] for k in range(3)] + [derived[k, c, at, :] for k in range(3)]

    def flip(v):
        return (v[0], v[2], v[1], v[3], v[5], v[4])

    def row_faces(r, carry):
        at = pl.multiple_of(r * 8, 8)
        here, below = pl.ds(at, 8), pl.ds(at + 1, 8)
        now = [load(c, here) for c in range(lane_tiles)]
        across = []
        for c in range(lane_tiles):
            nxt = now[(c + 1) % lane_tiles]
            right = [
                pltpu.roll(jnp.where(lane == 0, b, a), LANES - 1, 1)
                for a, b in zip(now[c], nxt)
            ]
            f_depth, f_across, f_along = roe(side(*flip(now[c])), side(*flip(right)))
            across.append((f_depth, f_along, f_across))
            flux = roe(side(*now[c]), side(*load(c, below)))
            for f in range(3):
                faces[f, c, pl.ds(at + 8, 8), :] = flux[f]
        for c in range(lane_tiles):
            prev = across[(c - 1) % lane_tiles]
            active = work[ACTIVE, c, here, :] > 0.5
            for f in range(3):
                left = pltpu.roll(jnp.where(lane == LANES - 1, prev[f], across[c][f]), 1, 1)
                out = (across[c][f] - left) + (
                    faces[f, c, pl.ds(at + 8, 8), :] - faces[f, c, pl.ds(at + 7, 8), :]
                )
                if f == 0:
                    out = out - 2.0 * work[SOURCE, c, here, :]
                work[DIFF + f, c, here, :] = jnp.where(active, out, 0.0)
        return carry

    lax.fori_loop(0, row_tiles - 1, row_faces, 0, unroll=5)


def step_ratio(peak_ref):
    peak = jnp.max(jnp.max(peak_ref[...], axis=0), axis=0, keepdims=True)
    step = (COURANT * SPACING) / peak
    return jnp.broadcast_to((0.5 / SPACING) * step, (8, LANES))


def moved(work, c, at, ratio):
    new = [work[f, c, at, :] - ratio * work[DIFF + f, c, at, :] for f in range(3)]
    for f in range(3):
        work[f, c, at, :] = new[f]
    return new


def update_kernel(peak_ref, work_in, work, next_ref):
    lane_tiles = work.shape[1]
    padded = work.shape[2]
    ratio = step_ratio(peak_ref)

    def one(r, acc):
        at = aligned(r * 8 + TOP, 8)
        active = work[ACTIVE, 0, at, :] > 0.5
        for c in range(lane_tiles):
            new = moved(work, c, at, ratio)
            if c < lane_tiles - 1:
                acc = jnp.maximum(acc, jnp.where(active, speed_of(*new), 0.0))
        return acc

    own_tiles = padded // 8 - 3
    acc = lax.fori_loop(0, own_tiles, one, jnp.zeros((8, LANES), jnp.float32), unroll=8)
    for at in (slice(0, 8), slice(padded - 16, padded - 8)):
        for c in range(lane_tiles):
            moved(work, c, at, ratio)
    spread_peak(acc, next_ref)


def last_kernel(peak_ref, plan_ref, work_in, work, next_ref, best):
    tiles = work.shape[1] - 1
    blocks = plan_ref.shape[0]
    block_rows = (work.shape[2] - 3 * 8) // blocks
    ratio = step_ratio(peak_ref)

    def one_block(b, carry):
        acc = jnp.zeros((8, LANES), jnp.float32)
        for r in range(0, block_rows, 8):
            at = aligned(b * block_rows + TOP + r, 8)
            for c in range(tiles):
                acc = jnp.maximum(acc, speed_of(*moved(work, c, at, ratio)))
        best[b] = acc
        return carry

    lax.fori_loop(0, blocks, one_block, 0, unroll=4)
    for t in range(next_ref.shape[0]):
        acc = jnp.zeros((8, LANES), jnp.float32)
        for b in range(blocks):
            acc = jnp.maximum(acc, jnp.where(plan_ref[b] == t, best[b], 0.0))
        top = jnp.max(acc, axis=0, keepdims=True)
        next_ref[t] = jnp.broadcast_to(jnp.max(top, axis=1, keepdims=True), (1, LANES))


def store_kernel(work, depth_hbm, mom_hbm, sem):
    rows, cols = depth_hbm.shape
    copies = []
    for k, dst in enumerate([depth_hbm, mom_hbm.at[0], mom_hbm.at[1]]):
        for c in range(cols // LANES):
            copies.append(
                pltpu.make_async_copy(
                    work.at[k, c, pl.ds(TOP, rows), :],
                    dst.at[:, pl.ds(c * LANES, LANES)],
                    sem.at[k, c],
                )
            )
    for copy in copies:
        copy.start()
    for copy in copies:
        copy.wait()


def exchange(x, axes):
    return lax.all_to_all(x, axes, 0, 0)


def send(x, axis, forward):
    count = lax.axis_size(axis)
    pairs = [(i, i + 1) if forward else (i + 1, i) for i in range(count - 1)]
    return lax.ppermute(x, axis, pairs)


def on_device(water_depth, momentum, wet_mask, helper_plan, breach_cells, breach_rate):
    rows, cols = water_depth.shape
    tile_count = lax.axis_size("tile")
    everyone = tile_count * lax.axis_size("region")
    blocks = wet_mask.shape[0]
    tiles = cols // LANES
    padded = rows + 3 * 8
    f32 = jnp.float32
    cells = breach_cells.reshape(-1)
    rates = breach_rate.reshape(-1)
    nbytes = 4 * 3 * rows * cols
    work_out = vmem_out(WORK, tiles + 1, padded, LANES)
    strip_out = vmem_out(SEND, HALO, rows + LANES)
    edge_out = vmem_out(SEND * tiles, HALO, LANES)
    peak_out = vmem_out(everyone, 1, LANES)

    work, plan, up, down = pl.pallas_call(
        start_kernel,
        out_shape=(work_out, pltpu.VMEM((blocks, 8, LANES), jnp.int32), edge_out, edge_out),
        in_specs=[hbm_spec()] * 6,
        out_specs=(vmem_spec(),) * 4,
        scratch_shapes=[
            pltpu.SMEM((blocks,), jnp.int32),
            pltpu.SMEM((blocks,), jnp.int32),
            pltpu.SMEM(cells.shape, jnp.int32),
            pltpu.SMEM(cells.shape, f32),
            pltpu.SemaphoreType.DMA((4,)),
            pltpu.SemaphoreType.DMA((3, tiles)),
        ],
        compiler_params=params(),
        cost_estimate=cost(2 * rows * cols, nbytes),
        name="start",
    )(wet_mask.reshape(-1), helper_plan.reshape(-1), cells, rates, water_depth, momentum)

    above = send(down, "region", True)
    below = send(up, "region", False)

    peak, left, right = pl.pallas_call(
        pack_kernel,
        out_shape=(peak_out, strip_out, strip_out),
        in_specs=[vmem_spec()],
        out_specs=(vmem_spec(),) * 3,
        scratch_shapes=[pltpu.VMEM((rows, LANES), f32)],
        compiler_params=params(),
        cost_estimate=cost(20 * rows * cols, nbytes),
        name="pack",
    )(work)

    work, left, right = pl.pallas_call(
        rows_kernel,
        out_shape=(work_out, strip_out, strip_out),
        in_specs=[vmem_spec()] * 5,
        out_specs=(vmem_spec(),) * 3,
        scratch_shapes=[pltpu.VMEM((LANES, LANES), f32)],
        input_output_aliases={0: 0, 1: 1, 2: 2},
        compiler_params=params(),
        cost_estimate=cost(rows * cols, nbytes // 8),
        name="rows",
    )(work, left, right, above, below)

    from_left = send(right, "tile", True)
    from_right = send(left, "tile", False)
    peaks = exchange(peak, ("region", "tile"))

    work = pl.pallas_call(
        columns_kernel,
        out_shape=work_out,
        in_specs=[vmem_spec()] * 5,
        out_specs=vmem_spec(),
        scratch_shapes=[
            pltpu.VMEM((LANES, rows + LANES), f32),
            pltpu.VMEM((rows + LANES, LANES), f32),
        ],
        input_output_aliases={0: 0},
        compiler_params=params(),
        cost_estimate=cost(10 * rows * cols, nbytes),
        name="columns",
    )(work, left, right, from_left, from_right)

    for step in range(STEPS):
        work = pl.pallas_call(
            flux_kernel,
            out_shape=work_out,
            in_specs=[vmem_spec()],
            out_specs=vmem_spec(),
            scratch_shapes=[
                pltpu.VMEM((3, tiles + 1, padded, LANES), f32),
                pltpu.VMEM((3, tiles + 1, padded + 8, LANES), f32),
            ],
            input_output_aliases={0: 0},
            compiler_params=params(),
            cost_estimate=cost(150 * rows * cols, 4 * nbytes),
            name="flux",
        )(work)
        if step < STEPS - 1:
            work, peak = pl.pallas_call(
                update_kernel,
                out_shape=(work_out, peak_out),
                in_specs=[vmem_spec()] * 2,
                out_specs=(vmem_spec(),) * 2,
                input_output_aliases={1: 0},
                compiler_params=params(),
                cost_estimate=cost(20 * rows * cols, nbytes),
                name="update",
            )(peaks, work)
            peaks = exchange(peak, ("region", "tile"))

    work, best = pl.pallas_call(
        last_kernel,
        out_shape=(work_out, vmem_out(tile_count, 1, LANES)),
        in_specs=[vmem_spec()] * 3,
        out_specs=(vmem_spec(),) * 2,
        scratch_shapes=[pltpu.VMEM((blocks, 8, LANES), f32)],
        input_output_aliases={2: 0},
        compiler_params=params(),
        cost_estimate=cost(20 * rows * cols, 2 * nbytes),
        name="last",
    )(peaks, plan, work)
    helpers = exchange(best, "tile")
    new_depth, new_momentum = pl.pallas_call(
        store_kernel,
        out_shape=(
            jax.ShapeDtypeStruct((rows, cols), f32),
            jax.ShapeDtypeStruct((2, rows, cols), f32),
        ),
        in_specs=[vmem_spec()],
        out_specs=(hbm_spec(),) * 2,
        scratch_shapes=[pltpu.SemaphoreType.DMA((3, tiles))],
        compiler_params=params(),
        cost_estimate=cost(10 * rows * cols, 2 * nbytes),
        name="store",
    )(work)
    return new_depth, new_momentum, jnp.max(helpers[:, :, :1], axis=0)


def solution(mesh):
    return jax.shard_map(
        on_device,
        mesh=mesh,
        in_specs=(
            P("region", "tile"),
            P(None, "region", "tile"),
            P("region", "tile"),
            P("region", "tile"),
            P("region", "tile", None),
            P("region", "tile", None),
        ),
        out_specs=(P("region", "tile"), P(None, "region", "tile"), P("region", "tile")),
        check_vma=False,
    )
```

time: 127 us -> 115 us (0.906)
  Pallas kernels: 58.4 us -> 24.7 us
  local copies, waits for them, and re-layouts: 20.1 us -> 46.8 us
  blocking collectives: 8.39 us -> 0 us
  starting transfers between devices: 34.1 us -> 36.8 us
    pallas_call x11 -> x13, Pallas kernels: 58.4 us -> 24.7 us  [the longest x4 15.6 us: on_device(): pl.pallas_call(flux_kernel, out_shape=work_out, in_specs=[vmem_spec()], o...]
    unnamed x40 -> x48, local copies, waits for them, and re-layouts: 20.1 us -> 46.8 us
    all_to_all x1 -> x0, blocking collectives: 8.39 us -> none  [exchange(): return lax.all_to_all(x, axes, 0, 0)]
    ppermute x4, starting transfers between devices: 8.78 us -> 10.5 us  [send(): return lax.ppermute(x, axis, pairs)]
    all_to_all x4 -> x5, starting transfers between devices: 25.3 us -> 26.3 us  [exchange(): return lax.all_to_all(x, axes, 0, 0)]
  transfers between devices with their start and end apart: 8 -> 9, of which waited for: 2 -> 2; matrix products, arithmetic and copies ran while one was open for 0% -> 0% of each run, Pallas kernels for 32% -> 17%
where the time goes in v2:
time: 115 us; the launch traced here: 114 us
  local copies, waits for them, and re-layouts  46.8 us (41%)
  starting transfers between devices  36.8 us (32%)
  Pallas kernels  24.7 us (21%)
  waiting for transfers between devices  4.24 us (4%)
    unnamed x48, local copies, waits for them, and re-layouts  46.8 us
    all_to_all x5, starting transfers between devices, exchange(): return lax.all_to_all(x, axes, 0, 0)  26.3 us
    pallas_call x4, Pallas kernels, on_device(): pl.pallas_call(flux_kernel, out_shape=work_out, in_specs=[vmem_spec()], o...  15.6 us
    ppermute x4, starting transfers between devices, send(): return lax.ppermute(x, axis, pairs)  10.5 us
    ppermute x4, waiting for transfers between devices, send(): return lax.ppermute(x, axis, pairs)  3.05 us
    pallas_call x3, Pallas kernels, on_device(): pl.pallas_call(update_kernel, out_shape=(work_out, peak_out), in_specs=[v...  3.04 us
  transfers between devices with their start and end apart: 9, of which 2 were waited for; matrix products, arithmetic and copies ran while one was open for 0% of the time, Pallas kernels for 17%

profile of v2, /device:TPU:0, one launch (start us, length us, event | category | flops | bytes accessed | tf_op | source)
XLA Modules:
  0.0 114.1 jit_solution(14612004073487570168)
XLA Ops:
  7.0 4.9 %collective-permute-start = (f32[10,4,128]{2,1,0:T(4,128)S(1)}, f32[10,4,128]{2,1,0:T(4,128)S(1)}, u32[]{:S(2)}, u32[]{:S(2)}) collective-permute-start(f32[10,4,128]{2,1,0:T(4,128)S(1)} %get-tuple-element.27), channel_id=1, source_target_pairs={{0,8},{8,16},{16,24},{1,9},{9,17},{17,25},{2,10},{10,18},{18,26},{... | collective-permute-start | bytes 61448 | tf_op jit(solution)/shard_map/ppermute | solution.py:438
  14.6 3.0 %collective-permute-done.1.below_ref = f32[10,4,128]{2,1,0:T(4,128)S(1)} collective-permute-done((f32[10,4,128]{2,1,0:T(4,128)S(1)}, f32[10,4,128]{2,1,0:T(4,128)S(1)}, u32[]{:S(2)}, u32[]{:S(2)}) %collective-permute-start.1) | collective-permute-done | bytes 20512 | tf_op jit(solution)/shard_map/ppermute | solution.py:438
  17.8 2.3 %copy-done = f32[8,3,408,128]{3,2,1,0:T(8,128)} copy-done((f32[8,3,408,128]{3,2,1,0:T(8,128)}, f32[8,3,408,128]{3,2,1,0:T(8,128)S(1)}, u32[]{:S(2)}) %copy-start) | copy-done | bytes 5013528
  21.4 3.0 %collective-permute-start.2 = (f32[5,4,512]{2,1,0:T(4,128)S(1)}, f32[5,4,512]{2,1,0:T(4,128)S(1)}, u32[]{:S(2)}, u32[]{:S(2)}) collective-permute-start(f32[5,4,512]{2,1,0:T(4,128)S(1)} %get-tuple-element.31.own_right), channel_id=1, source_target_pairs={{0,1},{1,2},{2,3},{3,4},{4,5},{5,6},{6,7},{8,9},{9,10},{10,11},{11... | collective-permute-start | bytes 122888 | tf_op jit(solution)/shard_map/ppermute | solution.py:438
  24.4 4.8 %all-to-all-start = ((f32[32,1,128]{2,1,0:T(1,128)}), f32[32,1,128]{2,1,0:T(1,128)S(1)}, u32[]{:S(2)}, u32[]{:S(2)}) async-start(f32[32,1,128]{2,1,0:T(1,128)} %get-tuple-element.24), calls=%async_computation | async-start | bytes 32768 | tf_op jit(solution)/shard_map/all_to_all | solution.py:432
  29.3 2.4 %copy-done.1 = f32[8,3,408,128]{3,2,1,0:T(8,128)S(1)} copy-done((f32[8,3,408,128]{3,2,1,0:T(8,128)S(1)}, f32[8,3,408,128]{3,2,1,0:T(8,128)}, u32[]{:S(2)}) %copy-start.1) | copy-done | bytes 5013528
  32.5 3.9 %flux.4.work_in = f32[8,3,408,128]{3,2,1,0:T(8,128)S(1)} custom-call(f32[8,3,408,128]{3,2,1,0:T(8,128)S(1)} %columns.1.work_in), custom_call_target="tpu_custom_call", output_to_operand_aliasing={{}: (0, {})} | custom-call | flops 14745600 | bytes 4718592 | tf_op jit(solution)/shard_map/flux/pallas_call | solution.py:521
  38.7 2.4 %copy-done.3 = f32[8,3,408,128]{3,2,1,0:T(8,128)S(1)} copy-done((f32[8,3,408,128]{3,2,1,0:T(8,128)S(1)}, f32[8,3,408,128]{3,2,1,0:T(8,128)}, u32[]{:S(2)}) %copy-start.3) | copy-done | bytes 5013528
  42.2 2.3 %copy-done.4 = f32[8,3,408,128]{3,2,1,0:T(8,128)} copy-done((f32[8,3,408,128]{3,2,1,0:T(8,128)}, f32[8,3,408,128]{3,2,1,0:T(8,128)S(1)}, u32[]{:S(2)}) %copy-start.4) | copy-done | bytes 5013528
  44.4 5.8 %all-to-all-start.1 = ((f32[32,1,128]{2,1,0:T(1,128)}), f32[32,1,128]{2,1,0:T(1,128)S(1)}, u32[]{:S(2)}, u32[]{:S(2)}) async-start(f32[32,1,128]{2,1,0:T(1,128)} %get-tuple-element.32), calls=%async_computation.1 | async-start | bytes 32768 | tf_op jit(solution)/shard_map/all_to_all | solution.py:432
  50.3 2.4 %copy-done.5 = f32[8,3,408,128]{3,2,1,0:T(8,128)S(1)} copy-done((f32[8,3,408,128]{3,2,1,0:T(8,128)S(1)}, f32[8,3,408,128]{3,2,1,0:T(8,128)}, u32[]{:S(2)}) %copy-start.5) | copy-done | bytes 5013528
  52.7 3.9 %flux.5.work_in = f32[8,3,408,128]{3,2,1,0:T(8,128)S(1)} custom-call(f32[8,3,408,128]{3,2,1,0:T(8,128)S(1)} %copy-done.5), custom_call_target="tpu_custom_call", output_to_operand_aliasing={{}: (0, {})} | custom-call | flops 14745600 | bytes 4718592 | tf_op jit(solution)/shard_map/flux/pallas_call | solution.py:521
  58.9 2.4 %copy-done.7 = f32[8,3,408,128]{3,2,1,0:T(8,128)S(1)} copy-done((f32[8,3,408,128]{3,2,1,0:T(8,128)S(1)}, f32[8,3,408,128]{3,2,1,0:T(8,128)}, u32[]{:S(2)}) %copy-start.7) | copy-done | bytes 5013528
  62.3 2.3 %copy-done.8 = f32[8,3,408,128]{3,2,1,0:T(8,128)} copy-done((f32[8,3,408,128]{3,2,1,0:T(8,128)}, f32[8,3,408,128]{3,2,1,0:T(8,128)S(1)}, u32[]{:S(2)}) %copy-start.8) | copy-done | bytes 5013528
  64.6 5.8 %all-to-all-start.2 = ((f32[32,1,128]{2,1,0:T(1,128)}), f32[32,1,128]{2,1,0:T(1,128)S(1)}, u32[]{:S(2)}, u32[]{:S(2)}) async-start(f32[32,1,128]{2,1,0:T(1,128)} %get-tuple-element.34), calls=%async_computation.2 | async-start | bytes 32768 | tf_op jit(solution)/shard_map/all_to_all | solution.py:432
  70.4 2.4 %copy-done.9 = f32[8,3,408,128]{3,2,1,0:T(8,128)S(1)} copy-done((f32[8,3,408,128]{3,2,1,0:T(8,128)S(1)}, f32[8,3,408,128]{3,2,1,0:T(8,128)}, u32[]{:S(2)}) %copy-start.9) | copy-done | bytes 5013528
  72.8 3.9 %flux.6.work_in = f32[8,3,408,128]{3,2,1,0:T(8,128)S(1)} custom-call(f32[8,3,408,128]{3,2,1,0:T(8,128)S(1)} %copy-done.9), custom_call_target="tpu_custom_call", output_to_operand_aliasing={{}: (0, {})} | custom-call | flops 14745600 | bytes 4718592 | tf_op jit(solution)/shard_map/flux/pallas_call | solution.py:521
  79.0 2.4 %copy-done.11 = f32[8,3,408,128]{3,2,1,0:T(8,128)S(1)} copy-done((f32[8,3,408,128]{3,2,1,0:T(8,128)S(1)}, f32[8,3,408,128]{3,2,1,0:T(8,128)}, u32[]{:S(2)}) %copy-start.11) | copy-done | bytes 5013528
  84.7 5.8 %all-to-all-start.3 = ((f32[32,1,128]{2,1,0:T(1,128)}), f32[32,1,128]{2,1,0:T(1,128)S(1)}, u32[]{:S(2)}, u32[]{:S(2)}) async-start(f32[32,1,128]{2,1,0:T(1,128)} %get-tuple-element.36), calls=%async_computation.3 | async-start | bytes 32768 | tf_op jit(solution)/shard_map/all_to_all | solution.py:432
  90.6 2.4 %copy-done.13 = f32[8,3,408,128]{3,2,1,0:T(8,128)S(1)} copy-done((f32[8,3,408,128]{3,2,1,0:T(8,128)S(1)}, f32[8,3,408,128]{3,2,1,0:T(8,128)}, u32[]{:S(2)}) %copy-start.13) | copy-done | bytes 5013528
  93.0 3.9 %flux.7.work_in = f32[8,3,408,128]{3,2,1,0:T(8,128)S(1)} custom-call(f32[8,3,408,128]{3,2,1,0:T(8,128)S(1)} %copy-done.13), custom_call_target="tpu_custom_call", output_to_operand_aliasing={{}: (0, {})} | custom-call | flops 14745600 | bytes 4718592 | tf_op jit(solution)/shard_map/flux/pallas_call | solution.py:521
  99.1 2.4 %copy-done.15 = f32[8,3,408,128]{3,2,1,0:T(8,128)S(1)} copy-done((f32[8,3,408,128]{3,2,1,0:T(8,128)S(1)}, f32[8,3,408,128]{3,2,1,0:T(8,128)}, u32[]{:S(2)}) %copy-start.15) | copy-done | bytes 5013528
  104.9 3.9 %all-to-all-start.4 = ((f32[8,1,128]{2,1,0:T(1,128)}), f32[8,1,128]{2,1,0:T(1,128)S(1)}, u32[]{:S(2)}, u32[]{:S(2)}) async-start(f32[8,1,128]{2,1,0:T(1,128)} %get-tuple-element.42), calls=%async_computation.4 | async-start | bytes 8192 | tf_op jit(solution)/shard_map/all_to_all | solution.py:432
  108.8 2.4 %copy-done.17 = f32[8,3,408,128]{3,2,1,0:T(8,128)S(1)} copy-done((f32[8,3,408,128]{3,2,1,0:T(8,128)S(1)}, f32[8,3,408,128]{3,2,1,0:T(8,128)}, u32[]{:S(2)}) %copy-start.17) | copy-done | bytes 5013528
  (56 shorter events, 31.8 us)
Async XLA Ops:
  7.0 7.6 %collective-permute-start = (f32[10,4,128]{2,1,0:T(4,128)S(1)}, f32[10,4,128]{2,1,0:T(4,128)S(1)}, u32[]{:S(2)}, u32[]{:S(2)}) collective-permute-start(f32[10,4,128]{2,1,0:T(4,128)S(1)} %get-tuple-element.27), channel_id=1, source_target_pairs={{0,8},{8,16},{16,24},{1,9},{9,17},{17,25},{2,10},{10,18},{18,26},{... | collective-permute-start | bytes 61448 | tf_op jit(solution)/shard_map/ppermute | solution.py:438
  11.9 5.7 %collective-permute-start.1 = (f32[10,4,128]{2,1,0:T(4,128)S(1)}, f32[10,4,128]{2,1,0:T(4,128)S(1)}, u32[]{:S(2)}, u32[]{:S(2)}) collective-permute-start(f32[10,4,128]{2,1,0:T(4,128)S(1)} %get-tuple-element.28), channel_id=1, source_target_pairs={{8,0},{16,8},{24,16},{9,1},{17,9},{25,17},{10,2},{18,10},{26,18},{... | collective-permute-start | bytes 61448 | tf_op jit(solution)/shard_map/ppermute | solution.py:438
  17.8 2.3 %copy-start = (f32[8,3,408,128]{3,2,1,0:T(8,128)}, f32[8,3,408,128]{3,2,1,0:T(8,128)S(1)}, u32[]{:S(2)}) copy-start(f32[8,3,408,128]{3,2,1,0:T(8,128)S(1)} %get-tuple-element.29.work_in) | copy-start | bytes 15040516
  20.1 9.2 %collective-permute-start.3 = (f32[5,4,512]{2,1,0:T(4,128)S(1)}, f32[5,4,512]{2,1,0:T(4,128)S(1)}, u32[]{:S(2)}, u32[]{:S(2)}) collective-permute-start(f32[5,4,512]{2,1,0:T(4,128)S(1)} %get-tuple-element.30.own_left), channel_id=1, source_target_pairs={{1,0},{2,1},{3,2},{4,3},{5,4},{6,5},{7,6},{9,8},{10,9},{11,10},{12... | collective-permute-start | bytes 122888 | tf_op jit(solution)/shard_map/ppermute | solution.py:438
  21.4 7.9 %collective-permute-start.2 = (f32[5,4,512]{2,1,0:T(4,128)S(1)}, f32[5,4,512]{2,1,0:T(4,128)S(1)}, u32[]{:S(2)}, u32[]{:S(2)}) collective-permute-start(f32[5,4,512]{2,1,0:T(4,128)S(1)} %get-tuple-element.31.own_right), channel_id=1, source_target_pairs={{0,1},{1,2},{2,3},{3,4},{4,5},{5,6},{6,7},{8,9},{9,10},{10,11},{11... | collective-permute-start | bytes 122888 | tf_op jit(solution)/shard_map/ppermute | solution.py:438
  24.4 14.3 %all-to-all-start = ((f32[32,1,128]{2,1,0:T(1,128)}), f32[32,1,128]{2,1,0:T(1,128)S(1)}, u32[]{:S(2)}, u32[]{:S(2)}) async-start(f32[32,1,128]{2,1,0:T(1,128)} %get-tuple-element.24), calls=%async_computation | async-start | bytes 32768 | tf_op jit(solution)/shard_map/all_to_all | solution.py:432
  29.3 2.4 %copy-start.1 = (f32[8,3,408,128]{3,2,1,0:T(8,128)S(1)}, f32[8,3,408,128]{3,2,1,0:T(8,128)}, u32[]{:S(2)}) copy-start(f32[8,3,408,128]{3,2,1,0:T(8,128)} %copy-done) | copy-start | bytes 15040516
  36.5 2.3 %copy-start.2 = (f32[8,3,408,128]{3,2,1,0:T(8,128)}, f32[8,3,408,128]{3,2,1,0:T(8,128)S(1)}, u32[]{:S(2)}) copy-start(f32[8,3,408,128]{3,2,1,0:T(8,128)S(1)} %flux.4.work_in) | copy-start | bytes 15040516
  38.7 2.4 %copy-start.3 = (f32[8,3,408,128]{3,2,1,0:T(8,128)S(1)}, f32[8,3,408,128]{3,2,1,0:T(8,128)}, u32[]{:S(2)}) copy-start(f32[8,3,408,128]{3,2,1,0:T(8,128)} %copy-done.2) | copy-start | bytes 15040516
  44.4 14.4 %all-to-all-start.1 = ((f32[32,1,128]{2,1,0:T(1,128)}), f32[32,1,128]{2,1,0:T(1,128)S(1)}, u32[]{:S(2)}, u32[]{:S(2)}) async-start(f32[32,1,128]{2,1,0:T(1,128)} %get-tuple-element.32), calls=%async_computation.1 | async-start | bytes 32768 | tf_op jit(solution)/shard_map/all_to_all | solution.py:432
  50.3 2.4 %copy-start.5 = (f32[8,3,408,128]{3,2,1,0:T(8,128)S(1)}, f32[8,3,408,128]{3,2,1,0:T(8,128)}, u32[]{:S(2)}) copy-start(f32[8,3,408,128]{3,2,1,0:T(8,128)} %copy-done.4) | copy-start | bytes 15040516
  56.6 2.3 %copy-start.6 = (f32[8,3,408,128]{3,2,1,0:T(8,128)}, f32[8,3,408,128]{3,2,1,0:T(8,128)S(1)}, u32[]{:S(2)}) copy-start(f32[8,3,408,128]{3,2,1,0:T(8,128)S(1)} %flux.5.work_in) | copy-start | bytes 15040516
  58.9 2.4 %copy-start.7 = (f32[8,3,408,128]{3,2,1,0:T(8,128)S(1)}, f32[8,3,408,128]{3,2,1,0:T(8,128)}, u32[]{:S(2)}) copy-start(f32[8,3,408,128]{3,2,1,0:T(8,128)} %copy-done.6) | copy-start | bytes 15040516
  64.6 14.4 %all-to-all-start.2 = ((f32[32,1,128]{2,1,0:T(1,128)}), f32[32,1,128]{2,1,0:T(1,128)S(1)}, u32[]{:S(2)}, u32[]{:S(2)}) async-start(f32[32,1,128]{2,1,0:T(1,128)} %get-tuple-element.34), calls=%async_computation.2 | async-start | bytes 32768 | tf_op jit(solution)/shard_map/all_to_all | solution.py:432
  70.4 2.4 %copy-start.9 = (f32[8,3,408,128]{3,2,1,0:T(8,128)S(1)}, f32[8,3,408,128]{3,2,1,0:T(8,128)}, u32[]{:S(2)}) copy-start(f32[8,3,408,128]{3,2,1,0:T(8,128)} %copy-done.8) | copy-start | bytes 15040516
  76.7 2.3 %copy-start.10 = (f32[8,3,408,128]{3,2,1,0:T(8,128)}, f32[8,3,408,128]{3,2,1,0:T(8,128)S(1)}, u32[]{:S(2)}) copy-start(f32[8,3,408,128]{3,2,1,0:T(8,128)S(1)} %flux.6.work_in) | copy-start | bytes 15040516
  79.0 2.4 %copy-start.11 = (f32[8,3,408,128]{3,2,1,0:T(8,128)S(1)}, f32[8,3,408,128]{3,2,1,0:T(8,128)}, u32[]{:S(2)}) copy-start(f32[8,3,408,128]{3,2,1,0:T(8,128)} %copy-done.10) | copy-start | bytes 15040516
  82.4 2.3 %copy-start.12 = (f32[8,3,408,128]{3,2,1,0:T(8,128)}, f32[8,3,408,128]{3,2,1,0:T(8,128)S(1)}, u32[]{:S(2)}) copy-start(f32[8,3,408,128]{3,2,1,0:T(8,128)S(1)} %get-tuple-element.38.work_in) | copy-start | bytes 15040516
  84.7 14.4 %all-to-all-start.3 = ((f32[32,1,128]{2,1,0:T(1,128)}), f32[32,1,128]{2,1,0:T(1,128)S(1)}, u32[]{:S(2)}, u32[]{:S(2)}) async-start(f32[32,1,128]{2,1,0:T(1,128)} %get-tuple-element.36), calls=%async_computation.3 | async-start | bytes 32768 | tf_op jit(solution)/shard_map/all_to_all | solution.py:432
  90.5 2.4 %copy-start.13 = (f32[8,3,408,128]{3,2,1,0:T(8,128)S(1)}, f32[8,3,408,128]{3,2,1,0:T(8,128)}, u32[]{:S(2)}) copy-start(f32[8,3,408,128]{3,2,1,0:T(8,128)} %copy-done.12) | copy-start | bytes 15040516
  96.9 2.3 %copy-start.14 = (f32[8,3,408,128]{3,2,1,0:T(8,128)}, f32[8,3,408,128]{3,2,1,0:T(8,128)S(1)}, u32[]{:S(2)}) copy-start(f32[8,3,408,128]{3,2,1,0:T(8,128)S(1)} %flux.7.work_in) | copy-start | bytes 15040516
  99.1 2.4 %copy-start.15 = (f32[8,3,408,128]{3,2,1,0:T(8,128)S(1)}, f32[8,3,408,128]{3,2,1,0:T(8,128)}, u32[]{:S(2)}) copy-start(f32[8,3,408,128]{3,2,1,0:T(8,128)} %copy-done.14) | copy-start | bytes 15040516
  104.9 8.6 %all-to-all-start.4 = ((f32[8,1,128]{2,1,0:T(1,128)}), f32[8,1,128]{2,1,0:T(1,128)S(1)}, u32[]{:S(2)}, u32[]{:S(2)}) async-start(f32[8,1,128]{2,1,0:T(1,128)} %get-tuple-element.42), calls=%async_computation.4 | async-start | bytes 8192 | tf_op jit(solution)/shard_map/all_to_all | solution.py:432
  108.8 2.4 %copy-start.17 = (f32[8,3,408,128]{3,2,1,0:T(8,128)S(1)}, f32[8,3,408,128]{3,2,1,0:T(8,128)}, u32[]{:S(2)}) copy-start(f32[8,3,408,128]{3,2,1,0:T(8,128)} %copy-done.16) | copy-start | bytes 15040516
  (9 other events, 11.5 us)

commit v3 on v2

--- a/solution.py
+++ b/solution.py
@@ -15,11 +15,30 @@
 SPACING = 1.0
 
 VMEM_LIMIT = 20 << 20
-
-
-WORK = 8
+FLUX_UNROLL = 7
+
+
+SOURCE, DIFF, FIELDS = 3, 4, 7
 SEND = 5
-ACTIVE, SOURCE, DIFF = 3, 4, 5
+STRIP_DIFF = 2 * HALO * SEND
+STRIP_END = STRIP_DIFF + 2 * HALO * 3
+
+
+def tiles_of(work):
+    return (work.shape[0] - 2) // FIELDS
+
+
+def active_at(work):
+    return work.shape[0] - 2
+
+
+def strip_at(work):
+    return work.shape[0] - 1
+
+
+def sent_plane(work, k, c):
+    tiles = tiles_of(work)
+    return (k * tiles + c, active_at(work), SOURCE * tiles + c)[max(k - 2, 0)]
 
 
 def vmem_spec():
@@ -83,7 +102,7 @@
 ):
     rows, cols = depth_hbm.shape
     tiles = cols // LANES
-    padded = work.shape[2]
+    padded = work.shape[1]
     blocks = wet_hbm.shape[0]
     block_rows = rows // blocks
     bottom = TOP + rows
@@ -104,20 +123,20 @@
             big.append(
                 pltpu.make_async_copy(
                     src.at[:, pl.ds(c * LANES, LANES)],
-                    work.at[k, c, pl.ds(TOP, rows), :],
+                    work.at[k * tiles + c, pl.ds(TOP, rows), :],
                     big_sem.at[k, c],
                 )
             )
     for copy in small + big:
         copy.start()
     for k in range(SEND):
-        fill = 1.0 if k == 0 else 0.0
         for c in range(tiles):
-            work[k, c, 0:TOP, :] = jnp.full((TOP, LANES), fill, jnp.float32)
-            work[k, c, bottom:padded, :] = jnp.full((padded - bottom, LANES), fill, jnp.float32)
-        work[k, tiles] = jnp.full((padded, LANES), fill, jnp.float32)
+            plane = sent_plane(work, k, c)
+            fill = 1.0 if k == 0 else 0.0
+            work[plane, 0:TOP, :] = jnp.full((TOP, LANES), fill, jnp.float32)
+            work[plane, bottom:padded, :] = jnp.full((padded - bottom, LANES), fill, jnp.float32)
     for c in range(tiles):
-        work[SOURCE, c, TOP:bottom, :] = jnp.zeros((rows, LANES), jnp.float32)
+        work[SOURCE * tiles + c, TOP:bottom, :] = jnp.zeros((rows, LANES), jnp.float32)
     for copy in small:
         copy.wait()
     lane = lane_ids(1)
@@ -128,29 +147,30 @@
         col = cell - row * cols
         c = lax.div(col, LANES)
         at = pl.ds(row + TOP, 1)
-        work[SOURCE, c, at, :] += jnp.where(lane == col - c * LANES, rate_ref[i], 0.0)
+        work[SOURCE * tiles + c, at, :] += jnp.where(lane == col - c * LANES, rate_ref[i], 0.0)
         return carry
 
     lax.fori_loop(0, cell_ref.shape[0], add_cell, 0)
     for b in range(blocks):
         wet = wet_ref[b].astype(jnp.float32)
         at = slice(TOP + b * block_rows, TOP + (b + 1) * block_rows)
-        for c in range(tiles):
-            work[ACTIVE, c, at, :] = jnp.full((block_rows, LANES), wet)
-        plan_ref[b] = jnp.full((8, LANES), plan_smem[b])
+        work[active_at(work), at, :] = jnp.full((block_rows, LANES), wet)
+        plan_ref[b] = jnp.full((1, LANES), plan_smem[b])
     for copy in big:
         copy.wait()
     for k in range(SEND):
         for c in range(tiles):
-            up_ref[k * tiles + c] = work[k, c, TOP : TOP + HALO, :]
-            down_ref[k * tiles + c] = work[k, c, bottom - HALO : bottom, :]
-
-
-def packed(work, at, size, lane):
-    tiles = work.shape[1] - 1
+            plane = sent_plane(work, k, c)
+            up_ref[k * tiles + c] = work[plane, TOP : TOP + HALO, :]
+            down_ref[k * tiles + c] = work[plane, bottom - HALO : bottom, :]
+
+
+def packed(work, at, lane):
+    tiles = tiles_of(work)
     out = None
     for k in range(SEND):
-        ends = jnp.where(lane < HALO, work[k, 0, at, :], work[k, tiles - 1, at, :])
+        first, last = sent_plane(work, k, 0), sent_plane(work, k, tiles - 1)
+        ends = jnp.where(lane < HALO, work[first, at, :], work[last, at, :])
         ends = pltpu.roll(ends, 2 * HALO * k + HALO, 1)
         out = ends if out is None else jnp.where(lane >= 2 * HALO * k, ends, out)
     return out
@@ -164,16 +184,16 @@
 
 
 def pack_kernel(work, peak_ref, left_ref, right_ref, pack):
-    tiles = work.shape[1] - 1
+    tiles = tiles_of(work)
     rows = pack.shape[0]
     lane = lane_ids(8)
 
     def one(r, acc):
         at = aligned(r * 8 + TOP, 8)
-        pack[aligned(r * 8, 8), :] = packed(work, at, 8, lane)
-        active = work[ACTIVE, 0, at, :] > 0.5
+        pack[aligned(r * 8, 8), :] = packed(work, at, lane)
+        active = work[active_at(work), at, :] > 0.5
         for c in range(tiles):
-            speed = speed_of(work[0, c, at, :], work[1, c, at, :], work[2, c, at, :])
+            speed = speed_of(*[work[k * tiles + c, at, :] for k in range(3)])
             acc = jnp.maximum(acc, jnp.where(active, speed, 0.0))
         return acc
 
@@ -187,10 +207,9 @@
 def rows_kernel(
     work_in, left_in, right_in, above_ref, below_ref, work, left_ref, right_ref, pack
 ):
-    tiles = work.shape[1] - 1
-    padded = work.shape[2]
-    bottom = padded - 2 * 8
+    tiles = tiles_of(work)
     own = left_ref.shape[2] - LANES
+    bottom = TOP + own
     is_top = lax.axis_index("region") == 0
     is_bottom = lax.axis_index("region") == lax.axis_size("region") - 1
 
@@ -198,13 +217,14 @@
         for k in range(SEND):
             flip = -1.0 if k == 1 else 1.0
             for c in range(tiles):
+                plane = sent_plane(work, k, c)
                 for j in range(HALO):
-                    work[k, c, to - step * (1 + j), :] = work[k, c, first + step * j, :] * flip
+                    work[plane, to - step * (1 + j), :] = work[plane, first + step * j, :] * flip
 
     def received(ref, lo):
         for k in range(SEND):
             for c in range(tiles):
-                work[k, c, lo : lo + HALO, :] = ref[k * tiles + c]
+                work[sent_plane(work, k, c), lo : lo + HALO, :] = ref[k * tiles + c]
 
     pl.when(is_top)(lambda: mirrored(TOP, 1, TOP))
     pl.when(jnp.logical_not(is_top))(lambda: received(above_ref, TOP - HALO))
@@ -212,15 +232,12 @@
     pl.when(jnp.logical_not(is_bottom))(lambda: received(below_ref, bottom))
     pack[...] = jnp.zeros_like(pack)
     lane = lane_ids(8)
-    pack[0:8, :] = packed(work, slice(0, 8), 8, lane)
-    pack[8:16, :] = packed(work, slice(bottom, bottom + 8), 8, lane)
+    pack[0:8, :] = packed(work, slice(0, 8), lane)
+    pack[8:16, :] = packed(work, slice(bottom, bottom + 8), lane)
     split_packed(pack[...].T, left_ref, right_ref, slice(own, own + LANES))
 
 
-def columns_kernel(
-    work_in, own_left, own_right, from_left, from_right, work, both, turned
-):
-    last = work.shape[1] - 1
+def columns_kernel(work_in, own_left, own_right, from_left, from_right, work, both):
     own = own_left.shape[2] - LANES
     bottom = TOP + own
     is_left = lax.axis_index("tile") == 0
@@ -237,29 +254,18 @@
             at = 2 * HALO * k + to
             both[at : at + HALO, :] = ref[k]
 
-    both[2 * HALO * SEND :, :] = jnp.zeros((LANES - 2 * HALO * SEND, own + LANES), jnp.float32)
+    both[STRIP_DIFF:, :] = jnp.zeros((LANES - STRIP_DIFF, own + LANES), jnp.float32)
     pl.when(is_left)(lambda: mirrored(own_left, 0))
     pl.when(jnp.logical_not(is_left))(lambda: received(from_left, 0))
     pl.when(is_right)(lambda: mirrored(own_right, HALO))
     pl.when(jnp.logical_not(is_right))(lambda: received(from_right, HALO))
-    for q in range(turned.shape[0] // LANES):
+    strip = strip_at(work)
+    for q in range(own // LANES):
         at = slice(q * LANES, (q + 1) * LANES)
-        turned[at, :] = both[:, at].T
-    lane = lane_ids(8)
-    inside = (lane < HALO) | (lane >= LANES - HALO)
-
-    def place(strip, at):
-        for k in range(SEND):
-            moved = pltpu.roll(strip, LANES - HALO - 2 * HALO * k, 1)
-            work[k, last, at, :] = jnp.where(inside, moved, 1.0 if k == 0 else 0.0)
-
-    def one(r, carry):
-        place(turned[aligned(r * 8, 8), :], aligned(r * 8 + TOP, 8))
-        return carry
-
-    lax.fori_loop(0, own // 8, one, 0, unroll=8)
-    place(turned[own : own + 8, :], slice(0, 8))
-    place(turned[own + 8 : own + 16, :], slice(bottom, bottom + 8))
+        work[strip, TOP + q * LANES : TOP + (q + 1) * LANES, :] = both[:, at].T
+    ends = both[:, own : own + LANES].T
+    work[strip, 0:8, :] = ends[0:8, :]
+    work[strip, bottom : bottom + 8, :] = ends[8:16, :]
 
 
 def roe(left, right):
@@ -292,63 +298,89 @@
     return (depth, normal, tangent, root, sn, st, press, sn * st)
 
 
-def flux_kernel(work_in, work, derived, faces):
-    lane_tiles = work.shape[1]
-    padded = work.shape[2]
+def flux_kernel(work_in, work, beside, derived, faces):
+    tiles = tiles_of(work)
+    padded = work.shape[1]
     row_tiles = padded // 8
+    strip, active_rows = strip_at(work), active_at(work)
+    lane = lane_ids(8)
+    inside = (lane < HALO) | (lane >= LANES - HALO)
 
     def derive(r, carry):
-        at = aligned(r * 24, 24)
-        for c in range(lane_tiles):
-            depth = work[0, c, at, :]
-            inverse = lax.rsqrt(depth)
-            derived[0, c, at, :] = depth * inverse
-            derived[1, c, at, :] = work[1, c, at, :] * inverse
-            derived[2, c, at, :] = work[2, c, at, :] * inverse
+        for i in range(5):
+            at = aligned(r * 40 + i * 8, 8)
+            packed_columns = work[strip, at, :]
+            for k in range(SEND):
+                out = pltpu.roll(packed_columns, LANES - HALO - 2 * HALO * k, 1)
+                beside[k, at, :] = jnp.where(inside, out, 1.0) if k == 0 else out
+            for c in range(tiles + 1):
+                state = own_state(c, at)
+                inverse = lax.rsqrt(state[0])
+                derived[c, at, :] = state[0] * inverse
+                derived[tiles + 1 + c, at, :] = state[1] * inverse
+                derived[2 * (tiles + 1) + c, at, :] = state[2] * inverse
         return carry
 
-    lax.fori_loop(0, padded // 24, derive, 0)
-    lane = lane_ids(8)
+    def own_state(c, at):
+        if c == tiles:
+            return [beside[k, at, :] for k in range(3)]
+        return [work[k * tiles + c, at, :] for k in range(3)]
+
+    lax.fori_loop(0, row_tiles // 5, derive, 0)
     for f in range(3):
-        for c in range(lane_tiles):
-            faces[f, c, 0:8, :] = jnp.zeros((8, LANES), jnp.float32)
+        for c in range(tiles + 1):
+            faces[f * (tiles + 1) + c, 0:8, :] = jnp.zeros((8, LANES), jnp.float32)
 
     def load(c, at):
-        return [work[k, c, at, :] for k in range(3)] + [derived[k, c, at, :] for k in range(3)]
+        return own_state(c, at) + [derived[k * (tiles + 1) + c, at, :] for k in range(3)]
 
     def flip(v):
         return (v[0], v[2], v[1], v[3], v[5], v[4])
 
-    def row_faces(r, carry):
-        at = pl.multiple_of(r * 8, 8)
+    def row_faces(at, wrap):
         here, below = pl.ds(at, 8), pl.ds(at + 1, 8)
-        now = [load(c, here) for c in range(lane_tiles)]
+        now = [load(c, here) for c in range(tiles + 1)]
         across = []
-        for c in range(lane_tiles):
-            nxt = now[(c + 1) % lane_tiles]
+        for c in range(tiles + 1):
+            nxt = now[(c + 1) % (tiles + 1)]
             right = [
                 pltpu.roll(jnp.where(lane == 0, b, a), LANES - 1, 1)
                 for a, b in zip(now[c], nxt)
             ]
             f_depth, f_across, f_along = roe(side(*flip(now[c])), side(*flip(right)))
             across.append((f_depth, f_along, f_across))
-            flux = roe(side(*now[c]), side(*load(c, below)))
+            under = [pltpu.roll(v, 7, 0) for v in now[c]] if wrap else load(c, below)
+            flux = roe(side(*now[c]), side(*under))
             for f in range(3):
-                faces[f, c, pl.ds(at + 8, 8), :] = flux[f]
-        for c in range(lane_tiles):
-            prev = across[(c - 1) % lane_tiles]
-            active = work[ACTIVE, c, here, :] > 0.5
+                faces[f * (tiles + 1) + c, pl.ds(at + 8, 8), :] = flux[f]
+        strip_out = work[strip, here, :]
+        for c in range(tiles + 1):
+            prev = across[(c - 1) % (tiles + 1)]
+            own = c < tiles
+            active = (work[active_rows, here, :] if own else beside[3, here, :]) > 0.5
             for f in range(3):
                 left = pltpu.roll(jnp.where(lane == LANES - 1, prev[f], across[c][f]), 1, 1)
+                plane = f * (tiles + 1) + c
                 out = (across[c][f] - left) + (
-                    faces[f, c, pl.ds(at + 8, 8), :] - faces[f, c, pl.ds(at + 7, 8), :]
+                    faces[plane, pl.ds(at + 8, 8), :] - faces[plane, pl.ds(at + 7, 8), :]
                 )
                 if f == 0:
-                    out = out - 2.0 * work[SOURCE, c, here, :]
-                work[DIFF + f, c, here, :] = jnp.where(active, out, 0.0)
+                    source = work[SOURCE * tiles + c, here, :] if own else beside[4, here, :]
+                    out = out - 2.0 * source
+                out = jnp.where(active, out, 0.0)
+                if own:
+                    work[(DIFF + f) * tiles + c, here, :] = out
+                else:
+                    lo = STRIP_DIFF + 2 * HALO * f
+                    strip_out = jnp.where(lane >= lo, pltpu.roll(out, lo + HALO, 1), strip_out)
+        work[strip, here, :] = strip_out
+
+    def one(r, carry):
+        row_faces(pl.multiple_of(r * 8, 8), False)
         return carry
 
-    lax.fori_loop(0, row_tiles - 1, row_faces, 0, unroll=5)
+    lax.fori_loop(0, row_tiles - 1, one, 0, unroll=FLUX_UNROLL)
+    row_faces(padded - 8, True)
 
 
 def step_ratio(peak_ref):
@@ -358,38 +390,49 @@
 
 
 def moved(work, c, at, ratio):
-    new = [work[f, c, at, :] - ratio * work[DIFF + f, c, at, :] for f in range(3)]
+    tiles = tiles_of(work)
+    new = [
+        work[f * tiles + c, at, :] - ratio * work[(DIFF + f) * tiles + c, at, :] for f in range(3)
+    ]
     for f in range(3):
-        work[f, c, at, :] = new[f]
+        work[f * tiles + c, at, :] = new[f]
     return new
 
 
 def update_kernel(peak_ref, work_in, work, next_ref):
-    lane_tiles = work.shape[1]
-    padded = work.shape[2]
+    tiles = tiles_of(work)
+    row_tiles = work.shape[1] // 8
+    strip = strip_at(work)
     ratio = step_ratio(peak_ref)
+    lane = lane_ids(8)
+    strip_ratio = jnp.where(lane < 2 * HALO * 3, ratio, 0.0)
+
+    def move_strip(at):
+        old = work[strip, at, :]
+        work[strip, at, :] = old - strip_ratio * pltpu.roll(old, LANES - STRIP_DIFF, 1)
 
     def one(r, acc):
         at = aligned(r * 8 + TOP, 8)
-        active = work[ACTIVE, 0, at, :] > 0.5
-        for c in range(lane_tiles):
+        active = work[active_at(work), at, :] > 0.5
+        for c in range(tiles):
             new = moved(work, c, at, ratio)
-            if c < lane_tiles - 1:
-                acc = jnp.maximum(acc, jnp.where(active, speed_of(*new), 0.0))
+            acc = jnp.maximum(acc, jnp.where(active, speed_of(*new), 0.0))
+        move_strip(at)
         return acc
 
-    own_tiles = padded // 8 - 3
-    acc = lax.fori_loop(0, own_tiles, one, jnp.zeros((8, LANES), jnp.float32), unroll=8)
-    for at in (slice(0, 8), slice(padded - 16, padded - 8)):
-        for c in range(lane_tiles):
+    zero = jnp.zeros((8, LANES), jnp.float32)
+    acc = lax.fori_loop(0, row_tiles - 2, one, zero, unroll=8)
+    for at in (slice(0, 8), slice(8 * row_tiles - 8, 8 * row_tiles)):
+        for c in range(tiles):
             moved(work, c, at, ratio)
+        move_strip(at)
     spread_peak(acc, next_ref)
 
 
 def last_kernel(peak_ref, plan_ref, work_in, work, next_ref, best):
-    tiles = work.shape[1] - 1
+    tiles = tiles_of(work)
     blocks = plan_ref.shape[0]
-    block_rows = (work.shape[2] - 3 * 8) // blocks
+    block_rows = (work.shape[1] - 2 * 8) // blocks
     ratio = step_ratio(peak_ref)
 
     def one_block(b, carry):
@@ -412,12 +455,13 @@
 
 def store_kernel(work, depth_hbm, mom_hbm, sem):
     rows, cols = depth_hbm.shape
+    tiles = cols // LANES
     copies = []
     for k, dst in enumerate([depth_hbm, mom_hbm.at[0], mom_hbm.at[1]]):
-        for c in range(cols // LANES):
+        for c in range(tiles):
             copies.append(
                 pltpu.make_async_copy(
-                    work.at[k, c, pl.ds(TOP, rows), :],
+                    work.at[k * tiles + c, pl.ds(TOP, rows), :],
                     dst.at[:, pl.ds(c * LANES, LANES)],
                     sem.at[k, c],
                 )
@@ -444,19 +488,19 @@
     everyone = tile_count * lax.axis_size("region")
     blocks = wet_mask.shape[0]
     tiles = cols // LANES
-    padded = rows + 3 * 8
+    padded = rows + 2 * 8
     f32 = jnp.float32
     cells = breach_cells.reshape(-1)
     rates = breach_rate.reshape(-1)
     nbytes = 4 * 3 * rows * cols
-    work_out = vmem_out(WORK, tiles + 1, padded, LANES)
+    work_out = vmem_out(FIELDS * tiles + 2, padded, LANES)
     strip_out = vmem_out(SEND, HALO, rows + LANES)
     edge_out = vmem_out(SEND * tiles, HALO, LANES)
     peak_out = vmem_out(everyone, 1, LANES)
 
     work, plan, up, down = pl.pallas_call(
         start_kernel,
-        out_shape=(work_out, pltpu.VMEM((blocks, 8, LANES), jnp.int32), edge_out, edge_out),
+        out_shape=(work_out, pltpu.VMEM((blocks, 1, LANES), jnp.int32), edge_out, edge_out),
         in_specs=[hbm_spec()] * 6,
         out_specs=(vmem_spec(),) * 4,
         scratch_shapes=[
@@ -470,7 +514,19 @@
         compiler_params=params(),
         cost_estimate=cost(2 * rows * cols, nbytes),
         name="start",
-    )(wet_mask.reshape(-1), helper_plan.reshape(-1), cells, rates, water_depth, momentum)
+    )(
+        *(
+            pltpu.with_memory_space_constraint(x, pltpu.HBM)
+            for x in (
+                wet_mask.reshape(-1),
+                helper_plan.reshape(-1),
+                cells,
+                rates,
+                water_depth,
+                momentum,
+            )
+        )
+    )
 
     above = send(down, "region", True)
     below = send(up, "region", False)
@@ -509,7 +565,6 @@
         out_specs=vmem_spec(),
         scratch_shapes=[
             pltpu.VMEM((LANES, rows + LANES), f32),
-            pltpu.VMEM((rows + LANES, LANES), f32),
         ],
         input_output_aliases={0: 0},
         compiler_params=params(),
@@ -524,8 +579,9 @@
             in_specs=[vmem_spec()],
             out_specs=vmem_spec(),
             scratch_shapes=[
-                pltpu.VMEM((3, tiles + 1, padded, LANES), f32),
-                pltpu.VMEM((3, tiles + 1, padded + 8, LANES), f32),
+                pltpu.VMEM((SEND, padded, LANES), f32),
+                pltpu.VMEM((3 * (tiles + 1), padded, LANES), f32),
+                pltpu.VMEM((3 * (tiles + 1), padded + 8, LANES), f32),
             ],
             input_output_aliases={0: 0},
             compiler_params=params(),

time: 115 us -> 75 us (0.65)
  local copies, waits for them, and re-layouts: 46.8 us -> 0 us
  waiting for transfers between devices: 4.24 us -> 15.7 us
  starting transfers between devices: 36.8 us -> 29.4 us
  Pallas kernels: 24.7 us -> 28.2 us
    unnamed x48 -> x0, local copies, waits for them, and re-layouts: 46.8 us -> none
    all_to_all x5, waiting for transfers between devices: 1.19 us -> 12.7 us  [exchange(): return lax.all_to_all(x, axes, 0, 0)]
    all_to_all x5, starting transfers between devices: 26.3 us -> 18.9 us  [exchange(): return lax.all_to_all(x, axes, 0, 0)]
    pallas_call x4, Pallas kernels: 15.6 us -> 19 us  [on_device(): pl.pallas_call(flux_kernel, out_shape=work_out, in_specs=[vmem_spec()], o...]
  transfers between devices with their start and end apart: 9 -> 9, of which waited for: 2 -> 6; matrix products, arithmetic and copies ran while one was open for 0% -> 0% of each run, Pallas kernels for 17% -> 29%
where the time goes in v3:
time: 75 us; the launch traced here: 74.7 us
  starting transfers between devices  29.4 us (39%)
  Pallas kernels  28.2 us (38%)
  waiting for transfers between devices  15.7 us (21%)
    pallas_call x4, Pallas kernels, on_device(): pl.pallas_call(flux_kernel, out_shape=work_out, in_specs=[vmem_spec()], o...  19 us
    all_to_all x5, starting transfers between devices, exchange(): return lax.all_to_all(x, axes, 0, 0)  18.9 us
    all_to_all x5, waiting for transfers between devices, exchange(): return lax.all_to_all(x, axes, 0, 0)  12.7 us
    ppermute x4, starting transfers between devices, send(): return lax.ppermute(x, axis, pairs)  10.5 us
    pallas_call x3, Pallas kernels, on_device(): pl.pallas_call(update_kernel, out_shape=(work_out, peak_out), in_specs=[v...  3.53 us
    ppermute x4, waiting for transfers between devices, send(): return lax.ppermute(x, axis, pairs)  3.05 us
    pallas_call x1, Pallas kernels, on_device(): pl.pallas_call(start_kernel, out_shape=(work_out, pltpu.VMEM((blocks, 1,...  1.86 us
  transfers between devices with their start and end apart: 9, of which 6 were waited for; matrix products, arithmetic and copies ran while one was open for 0% of the time, Pallas kernels for 29%

profile of v3, /device:TPU:0, one launch (start us, length us, event | category | flops | bytes accessed | tf_op | source)
XLA Modules:
  0.0 74.7 jit_solution(2904975809346386805)
XLA Ops:
  0.6 1.9 %start.1 = (f32[16,400,128]{2,1,0:T(8,128)S(1)}, s32[24,1,128]{2,1,0:T(1,128)S(1)}, f32[10,4,128]{2,1,0:T(4,128)S(1)}, f32[10,4,128]{2,1,0:T(4,128)S(1)}) custom-call(s32[24]{0:T(128)} %bitcast.5, s32[24]{0:T(128)} %bitcast.6, s32[64]{0:T(128)} %bitcast.7, f32[64]{0:T(128)} %bitcast.8, f32[384,256]{1,0:T(8,128)} %depth_hbm.1, f32[2,384,256]{2,1,0:T(8,128)} %mom_hbm.1), custom_call_target="tpu_custom_call" | custom-call | flops 196608 | bytes 1179648 | tf_op jit(solution)/shard_map/start/pallas_call | solution.py:501
  2.5 4.9 %collective-permute-start = (f32[10,4,128]{2,1,0:T(4,128)S(1)}, f32[10,4,128]{2,1,0:T(4,128)S(1)}, u32[]{:S(2)}, u32[]{:S(2)}) collective-permute-start(f32[10,4,128]{2,1,0:T(4,128)S(1)} %get-tuple-element.27), channel_id=1, source_target_pairs={{0,8},{8,16},{16,24},{1,9},{9,17},{17,25},{2,10},{10,18},{18,26},{... | collective-permute-start | bytes 61448 | tf_op jit(solution)/shard_map/ppermute | solution.py:482
  7.4 1.3 %collective-permute-start.1 = (f32[10,4,128]{2,1,0:T(4,128)S(1)}, f32[10,4,128]{2,1,0:T(4,128)S(1)}, u32[]{:S(2)}, u32[]{:S(2)}) collective-permute-start(f32[10,4,128]{2,1,0:T(4,128)S(1)} %get-tuple-element.28), channel_id=1, source_target_pairs={{8,0},{16,8},{24,16},{9,1},{17,9},{25,17},{10,2},{18,10},{26,18},{... | collective-permute-start | bytes 61448 | tf_op jit(solution)/shard_map/ppermute | solution.py:482
  8.7 1.3 %pack.1 = (f32[32,1,128]{2,1,0:T(1,128)}, f32[5,4,512]{2,1,0:T(4,128)S(1)}, f32[5,4,512]{2,1,0:T(4,128)S(1)}) custom-call(f32[16,400,128]{2,1,0:T(8,128)S(1)} %get-tuple-element.23.work.work_in), custom_call_target="tpu_custom_call" | custom-call | flops 1966080 | bytes 1179648 | tf_op jit(solution)/shard_map/pack/pallas_call | solution.py:534
  10.1 3.0 %collective-permute-done.1.below_ref = f32[10,4,128]{2,1,0:T(4,128)S(1)} collective-permute-done((f32[10,4,128]{2,1,0:T(4,128)S(1)}, f32[10,4,128]{2,1,0:T(4,128)S(1)}, u32[]{:S(2)}, u32[]{:S(2)}) %collective-permute-start.1) | collective-permute-done | bytes 20512 | tf_op jit(solution)/shard_map/ppermute | solution.py:482
  13.3 1.3 %collective-permute-start.3 = (f32[5,4,512]{2,1,0:T(4,128)S(1)}, f32[5,4,512]{2,1,0:T(4,128)S(1)}, u32[]{:S(2)}, u32[]{:S(2)}) collective-permute-start(f32[5,4,512]{2,1,0:T(4,128)S(1)} %get-tuple-element.30.own_left), channel_id=1, source_target_pairs={{1,0},{2,1},{3,2},{4,3},{5,4},{6,5},{7,6},{9,8},{10,9},{11,10},{12... | collective-permute-start | bytes 122888 | tf_op jit(solution)/shard_map/ppermute | solution.py:482
  14.6 3.0 %collective-permute-start.2 = (f32[5,4,512]{2,1,0:T(4,128)S(1)}, f32[5,4,512]{2,1,0:T(4,128)S(1)}, u32[]{:S(2)}, u32[]{:S(2)}) collective-permute-start(f32[5,4,512]{2,1,0:T(4,128)S(1)} %get-tuple-element.31.own_right), channel_id=1, source_target_pairs={{0,1},{1,2},{2,3},{3,4},{4,5},{5,6},{6,7},{8,9},{9,10},{10,11},{11... | collective-permute-start | bytes 122888 | tf_op jit(solution)/shard_map/ppermute | solution.py:482
  17.6 4.8 %all-to-all-start = ((f32[32,1,128]{2,1,0:T(1,128)}), f32[32,1,128]{2,1,0:T(1,128)S(1)}, u32[]{:S(2)}, u32[]{:S(2)}) async-start(f32[32,1,128]{2,1,0:T(1,128)} %get-tuple-element.24), calls=%async_computation | async-start | bytes 32768 | tf_op jit(solution)/shard_map/all_to_all | solution.py:476
  22.7 4.7 %flux.4.work_in = f32[16,400,128]{2,1,0:T(8,128)S(1)} custom-call(f32[16,400,128]{2,1,0:T(8,128)S(1)} %columns.1.work_in), custom_call_target="tpu_custom_call", output_to_operand_aliasing={{}: (0, {})} | custom-call | flops 14745600 | bytes 4718592 | tf_op jit(solution)/shard_map/flux/pallas_call | solution.py:576
  27.4 2.1 %all-to-all-done.peak_ref = f32[32,1,128]{2,1,0:T(1,128)S(1)} async-done(((f32[32,1,128]{2,1,0:T(1,128)}), f32[32,1,128]{2,1,0:T(1,128)S(1)}, u32[]{:S(2)}, u32[]{:S(2)}) %all-to-all-start) | async-done | bytes 16416 | tf_op jit(solution)/shard_map/all_to_all | solution.py:476
  29.5 1.2 %update.3 = (f32[16,400,128]{2,1,0:T(8,128)S(1)}, f32[32,1,128]{2,1,0:T(1,128)}) custom-call(f32[32,1,128]{2,1,0:T(1,128)S(1)} %all-to-all-done.peak_ref, f32[16,400,128]{2,1,0:T(8,128)S(1)} %flux.4.work_in), custom_call_target="tpu_custom_call", output_to_operand_aliasing={{0}: (1, {})} | custom-call | flops 1966080 | bytes 1179648 | tf_op jit(solution)/shard_map/update/pallas_call | solution.py:592
  30.7 3.7 %all-to-all-start.1 = ((f32[32,1,128]{2,1,0:T(1,128)}), f32[32,1,128]{2,1,0:T(1,128)S(1)}, u32[]{:S(2)}, u32[]{:S(2)}) async-start(f32[32,1,128]{2,1,0:T(1,128)} %get-tuple-element.32), calls=%async_computation.1 | async-start | bytes 32768 | tf_op jit(solution)/shard_map/all_to_all | solution.py:476
  34.4 4.7 %flux.5.work_in = f32[16,400,128]{2,1,0:T(8,128)S(1)} custom-call(f32[16,400,128]{2,1,0:T(8,128)S(1)} %get-tuple-element.33.work_in), custom_call_target="tpu_custom_call", output_to_operand_aliasing={{}: (0, {})} | custom-call | flops 14745600 | bytes 4718592 | tf_op jit(solution)/shard_map/flux/pallas_call | solution.py:576
  39.2 2.3 %all-to-all-done.1.peak_ref = f32[32,1,128]{2,1,0:T(1,128)S(1)} async-done(((f32[32,1,128]{2,1,0:T(1,128)}), f32[32,1,128]{2,1,0:T(1,128)S(1)}, u32[]{:S(2)}, u32[]{:S(2)}) %all-to-all-start.1) | async-done | bytes 16416 | tf_op jit(solution)/shard_map/all_to_all | solution.py:476
  41.5 1.2 %update.4 = (f32[16,400,128]{2,1,0:T(8,128)S(1)}, f32[32,1,128]{2,1,0:T(1,128)}) custom-call(f32[32,1,128]{2,1,0:T(1,128)S(1)} %all-to-all-done.1.peak_ref, f32[16,400,128]{2,1,0:T(8,128)S(1)} %flux.5.work_in), custom_call_target="tpu_custom_call", output_to_operand_aliasing={{0}: (1, {})} | custom-call | flops 1966080 | bytes 1179648 | tf_op jit(solution)/shard_map/update/pallas_call | solution.py:592
  42.7 3.5 %all-to-all-start.2 = ((f32[32,1,128]{2,1,0:T(1,128)}), f32[32,1,128]{2,1,0:T(1,128)S(1)}, u32[]{:S(2)}, u32[]{:S(2)}) async-start(f32[32,1,128]{2,1,0:T(1,128)} %get-tuple-element.34), calls=%async_computation.2 | async-start | bytes 32768 | tf_op jit(solution)/shard_map/all_to_all | solution.py:476
  46.2 4.7 %flux.6.work_in = f32[16,400,128]{2,1,0:T(8,128)S(1)} custom-call(f32[16,400,128]{2,1,0:T(8,128)S(1)} %get-tuple-element.35.work_in), custom_call_target="tpu_custom_call", output_to_operand_aliasing={{}: (0, {})} | custom-call | flops 14745600 | bytes 4718592 | tf_op jit(solution)/shard_map/flux/pallas_call | solution.py:576
  50.9 2.3 %all-to-all-done.2.peak_ref = f32[32,1,128]{2,1,0:T(1,128)S(1)} async-done(((f32[32,1,128]{2,1,0:T(1,128)}), f32[32,1,128]{2,1,0:T(1,128)S(1)}, u32[]{:S(2)}, u32[]{:S(2)}) %all-to-all-start.2) | async-done | bytes 16416 | tf_op jit(solution)/shard_map/all_to_all | solution.py:476
  53.3 1.2 %update.5 = (f32[16,400,128]{2,1,0:T(8,128)S(1)}, f32[32,1,128]{2,1,0:T(1,128)}) custom-call(f32[32,1,128]{2,1,0:T(1,128)S(1)} %all-to-all-done.2.peak_ref, f32[16,400,128]{2,1,0:T(8,128)S(1)} %flux.6.work_in), custom_call_target="tpu_custom_call", output_to_operand_aliasing={{0}: (1, {})} | custom-call | flops 1966080 | bytes 1179648 | tf_op jit(solution)/shard_map/update/pallas_call | solution.py:592
  54.4 3.5 %all-to-all-start.3 = ((f32[32,1,128]{2,1,0:T(1,128)}), f32[32,1,128]{2,1,0:T(1,128)S(1)}, u32[]{:S(2)}, u32[]{:S(2)}) async-start(f32[32,1,128]{2,1,0:T(1,128)} %get-tuple-element.36), calls=%async_computation.3 | async-start | bytes 32768 | tf_op jit(solution)/shard_map/all_to_all | solution.py:476
  57.9 4.7 %flux.7.work_in = f32[16,400,128]{2,1,0:T(8,128)S(1)} custom-call(f32[16,400,128]{2,1,0:T(8,128)S(1)} %get-tuple-element.38.work_in), custom_call_target="tpu_custom_call", output_to_operand_aliasing={{}: (0, {})} | custom-call | flops 14745600 | bytes 4718592 | tf_op jit(solution)/shard_map/flux/pallas_call | solution.py:576
  62.7 2.3 %all-to-all-done.3.peak_ref = f32[32,1,128]{2,1,0:T(1,128)S(1)} async-done(((f32[32,1,128]{2,1,0:T(1,128)}), f32[32,1,128]{2,1,0:T(1,128)S(1)}, u32[]{:S(2)}, u32[]{:S(2)}) %all-to-all-start.3) | async-done | bytes 16416 | tf_op jit(solution)/shard_map/all_to_all | solution.py:476
  66.1 3.3 %all-to-all-start.4 = ((f32[8,1,128]{2,1,0:T(1,128)}), f32[8,1,128]{2,1,0:T(1,128)S(1)}, u32[]{:S(2)}, u32[]{:S(2)}) async-start(f32[8,1,128]{2,1,0:T(1,128)} %get-tuple-element.42), calls=%async_computation.4 | async-start | bytes 8192 | tf_op jit(solution)/shard_map/all_to_all | solution.py:476
  70.5 3.5 %all-to-all-done.4 = f32[8,1,128]{2,1,0:T(1,128)S(1)} async-done(((f32[8,1,128]{2,1,0:T(1,128)}), f32[8,1,128]{2,1,0:T(1,128)S(1)}, u32[]{:S(2)}, u32[]{:S(2)}) %all-to-all-start.4) | async-done | bytes 4128 | tf_op jit(solution)/shard_map/all_to_all | solution.py:476
  (8 shorter events, 3.1 us)
Async XLA Ops:
  2.5 7.6 %collective-permute-start = (f32[10,4,128]{2,1,0:T(4,128)S(1)}, f32[10,4,128]{2,1,0:T(4,128)S(1)}, u32[]{:S(2)}, u32[]{:S(2)}) collective-permute-start(f32[10,4,128]{2,1,0:T(4,128)S(1)} %get-tuple-element.27), channel_id=1, source_target_pairs={{0,8},{8,16},{16,24},{1,9},{9,17},{17,25},{2,10},{10,18},{18,26},{... | collective-permute-start | bytes 61448 | tf_op jit(solution)/shard_map/ppermute | solution.py:482
  7.4 5.7 %collective-permute-start.1 = (f32[10,4,128]{2,1,0:T(4,128)S(1)}, f32[10,4,128]{2,1,0:T(4,128)S(1)}, u32[]{:S(2)}, u32[]{:S(2)}) collective-permute-start(f32[10,4,128]{2,1,0:T(4,128)S(1)} %get-tuple-element.28), channel_id=1, source_target_pairs={{8,0},{16,8},{24,16},{9,1},{17,9},{25,17},{10,2},{18,10},{26,18},{... | collective-permute-start | bytes 61448 | tf_op jit(solution)/shard_map/ppermute | solution.py:482
  13.3 9.2 %collective-permute-start.3 = (f32[5,4,512]{2,1,0:T(4,128)S(1)}, f32[5,4,512]{2,1,0:T(4,128)S(1)}, u32[]{:S(2)}, u32[]{:S(2)}) collective-permute-start(f32[5,4,512]{2,1,0:T(4,128)S(1)} %get-tuple-element.30.own_left), channel_id=1, source_target_pairs={{1,0},{2,1},{3,2},{4,3},{5,4},{6,5},{7,6},{9,8},{10,9},{11,10},{12... | collective-permute-start | bytes 122888 | tf_op jit(solution)/shard_map/ppermute | solution.py:482
  14.6 7.9 %collective-permute-start.2 = (f32[5,4,512]{2,1,0:T(4,128)S(1)}, f32[5,4,512]{2,1,0:T(4,128)S(1)}, u32[]{:S(2)}, u32[]{:S(2)}) collective-permute-start(f32[5,4,512]{2,1,0:T(4,128)S(1)} %get-tuple-element.31.own_right), channel_id=1, source_target_pairs={{0,1},{1,2},{2,3},{3,4},{4,5},{5,6},{6,7},{8,9},{9,10},{10,11},{11... | collective-permute-start | bytes 122888 | tf_op jit(solution)/shard_map/ppermute | solution.py:482
  17.6 11.9 %all-to-all-start = ((f32[32,1,128]{2,1,0:T(1,128)}), f32[32,1,128]{2,1,0:T(1,128)S(1)}, u32[]{:S(2)}, u32[]{:S(2)}) async-start(f32[32,1,128]{2,1,0:T(1,128)} %get-tuple-element.24), calls=%async_computation | async-start | bytes 32768 | tf_op jit(solution)/shard_map/all_to_all | solution.py:476
  30.7 10.8 %all-to-all-start.1 = ((f32[32,1,128]{2,1,0:T(1,128)}), f32[32,1,128]{2,1,0:T(1,128)S(1)}, u32[]{:S(2)}, u32[]{:S(2)}) async-start(f32[32,1,128]{2,1,0:T(1,128)} %get-tuple-element.32), calls=%async_computation.1 | async-start | bytes 32768 | tf_op jit(solution)/shard_map/all_to_all | solution.py:476
  42.7 10.6 %all-to-all-start.2 = ((f32[32,1,128]{2,1,0:T(1,128)}), f32[32,1,128]{2,1,0:T(1,128)S(1)}, u32[]{:S(2)}, u32[]{:S(2)}) async-start(f32[32,1,128]{2,1,0:T(1,128)} %get-tuple-element.34), calls=%async_computation.2 | async-start | bytes 32768 | tf_op jit(solution)/shard_map/all_to_all | solution.py:476
  54.4 10.6 %all-to-all-start.3 = ((f32[32,1,128]{2,1,0:T(1,128)}), f32[32,1,128]{2,1,0:T(1,128)S(1)}, u32[]{:S(2)}, u32[]{:S(2)}) async-start(f32[32,1,128]{2,1,0:T(1,128)} %get-tuple-element.36), calls=%async_computation.3 | async-start | bytes 32768 | tf_op jit(solution)/shard_map/all_to_all | solution.py:476
  66.1 7.9 %all-to-all-start.4 = ((f32[8,1,128]{2,1,0:T(1,128)}), f32[8,1,128]{2,1,0:T(1,128)S(1)}, u32[]{:S(2)}, u32[]{:S(2)}) async-start(f32[8,1,128]{2,1,0:T(1,128)} %get-tuple-element.42), calls=%async_computation.4 | async-start | bytes 8192 | tf_op jit(solution)/shard_map/all_to_all | solution.py:476

commit v4 on v3

--- a/solution.py
+++ b/solution.py
@@ -1,3 +1,5 @@
+import functools
+
 import jax
 import jax.numpy as jnp
 from jax import lax
@@ -20,6 +22,7 @@
 
 SOURCE, DIFF, FIELDS = 3, 4, 7
 SEND = 5
+ALL, ROWS, REST = range(3)
 STRIP_DIFF = 2 * HALO * SEND
 STRIP_END = STRIP_DIFF + 2 * HALO * 3
 
@@ -91,6 +94,7 @@
     mom_hbm,
     work,
     plan_ref,
+    peak_ref,
     up_ref,
     down_ref,
     wet_ref,
@@ -164,6 +168,17 @@
             up_ref[k * tiles + c] = work[plane, TOP : TOP + HALO, :]
             down_ref[k * tiles + c] = work[plane, bottom - HALO : bottom, :]
 
+    def one(r, acc):
+        at = aligned(r * 8 + TOP, 8)
+        active = work[active_at(work), at, :] > 0.5
+        for c in range(tiles):
+            speed = speed_of(*[work[k * tiles + c, at, :] for k in range(3)])
+            acc = jnp.maximum(acc, jnp.where(active, speed, 0.0))
+        return acc
+
+    acc = lax.fori_loop(0, rows // 8, one, jnp.zeros((8, LANES), jnp.float32), unroll=8)
+    spread_peak(acc, peak_ref)
+
 
 def packed(work, at, lane):
     tiles = tiles_of(work)
@@ -183,22 +198,15 @@
         left_ref[k, :, at] = turned[lo + HALO : lo + 2 * HALO, :]
 
 
-def pack_kernel(work, peak_ref, left_ref, right_ref, pack):
-    tiles = tiles_of(work)
+def pack_kernel(work, left_ref, right_ref, pack):
     rows = pack.shape[0]
     lane = lane_ids(8)
 
-    def one(r, acc):
-        at = aligned(r * 8 + TOP, 8)
-        pack[aligned(r * 8, 8), :] = packed(work, at, lane)
-        active = work[active_at(work), at, :] > 0.5
-        for c in range(tiles):
-            speed = speed_of(*[work[k * tiles + c, at, :] for k in range(3)])
-            acc = jnp.maximum(acc, jnp.where(active, speed, 0.0))
-        return acc
-
-    acc = lax.fori_loop(0, rows // 8, one, jnp.zeros((8, LANES), jnp.float32), unroll=8)
-    spread_peak(acc, peak_ref)
+    def one(r, carry):
+        pack[aligned(r * 8, 8), :] = packed(work, aligned(r * 8 + TOP, 8), lane)
+        return carry
+
+    lax.fori_loop(0, rows // 8, one, 0, unroll=8)
     for q in range(rows // LANES):
         at = slice(q * LANES, (q + 1) * LANES)
         split_packed(pack[at, :].T, left_ref, right_ref, at)
@@ -298,8 +306,9 @@
     return (depth, normal, tangent, root, sn, st, press, sn * st)
 
 
-def flux_kernel(work_in, work, beside, derived, faces):
+def flux_kernel(part, work_in, work, beside, derived, faces):
     tiles = tiles_of(work)
+    count = tiles if part == ROWS else tiles + 1
     padded = work.shape[1]
     row_tiles = padded // 8
     strip, active_rows = strip_at(work), active_at(work)
@@ -310,10 +319,10 @@
         for i in range(5):
             at = aligned(r * 40 + i * 8, 8)
             packed_columns = work[strip, at, :]
-            for k in range(SEND):
+            for k in range(SEND if part != ROWS else 0):
                 out = pltpu.roll(packed_columns, LANES - HALO - 2 * HALO * k, 1)
                 beside[k, at, :] = jnp.where(inside, out, 1.0) if k == 0 else out
-            for c in range(tiles + 1):
+            for c in range(count):
                 state = own_state(c, at)
                 inverse = lax.rsqrt(state[0])
                 derived[c, at, :] = state[0] * inverse
@@ -337,33 +346,45 @@
     def flip(v):
         return (v[0], v[2], v[1], v[3], v[5], v[4])
 
-    def row_faces(at, wrap):
+    def fluxes(at, wrap):
         here, below = pl.ds(at, 8), pl.ds(at + 1, 8)
-        now = [load(c, here) for c in range(tiles + 1)]
-        across = []
-        for c in range(tiles + 1):
-            nxt = now[(c + 1) % (tiles + 1)]
-            right = [
-                pltpu.roll(jnp.where(lane == 0, b, a), LANES - 1, 1)
-                for a, b in zip(now[c], nxt)
-            ]
-            f_depth, f_across, f_along = roe(side(*flip(now[c])), side(*flip(right)))
-            across.append((f_depth, f_along, f_across))
+        now = [load(c, here) for c in range(count)]
+        for c in range(count):
+            if part == REST and c < tiles:
+                continue
             under = [pltpu.roll(v, 7, 0) for v in now[c]] if wrap else load(c, below)
             flux = roe(side(*now[c]), side(*under))
             for f in range(3):
                 faces[f * (tiles + 1) + c, pl.ds(at + 8, 8), :] = flux[f]
+
+        def along_rows(f, c):
+            plane = f * (tiles + 1) + c
+            return faces[plane, pl.ds(at + 8, 8), :] - faces[plane, pl.ds(at + 7, 8), :]
+
+        if part == ROWS:
+            for f in range(3):
+                for c in range(tiles):
+                    work[(DIFF + f) * tiles + c, here, :] = along_rows(f, c)
+            return
+        across = []
+        for c in range(count):
+            right = [
+                pltpu.roll(jnp.where(lane == 0, b, a), LANES - 1, 1)
+                for a, b in zip(now[c], now[(c + 1) % count])
+            ]
+            f_depth, f_across, f_along = roe(side(*flip(now[c])), side(*flip(right)))
+            across.append((f_depth, f_along, f_across))
         strip_out = work[strip, here, :]
-        for c in range(tiles + 1):
-            prev = across[(c - 1) % (tiles + 1)]
+        for c in range(count):
+            prev = across[(c - 1) % count]
             own = c < tiles
             active = (work[active_rows, here, :] if own else beside[3, here, :]) > 0.5
             for f in range(3):
                 left = pltpu.roll(jnp.where(lane == LANES - 1, prev[f], across[c][f]), 1, 1)
-                plane = f * (tiles + 1) + c
-                out = (across[c][f] - left) + (
-                    faces[plane, pl.ds(at + 8, 8), :] - faces[plane, pl.ds(at + 7, 8), :]
-                )
+                if own and part == REST:
+                    out = (across[c][f] - left) + work[(DIFF + f) * tiles + c, here, :]
+                else:
+                    out = (across[c][f] - left) + along_rows(f, c)
                 if f == 0:
                     source = work[SOURCE * tiles + c, here, :] if own else beside[4, here, :]
                     out = out - 2.0 * source
@@ -376,11 +397,11 @@
         work[strip, here, :] = strip_out
 
     def one(r, carry):
-        row_faces(pl.multiple_of(r * 8, 8), False)
+        fluxes(pl.multiple_of(r * 8, 8), False)
         return carry
 
     lax.fori_loop(0, row_tiles - 1, one, 0, unroll=FLUX_UNROLL)
-    row_faces(padded - 8, True)
+    fluxes(padded - 8, True)
 
 
 def step_ratio(peak_ref):
@@ -497,12 +518,13 @@
     strip_out = vmem_out(SEND, HALO, rows + LANES)
     edge_out = vmem_out(SEND * tiles, HALO, LANES)
     peak_out = vmem_out(everyone, 1, LANES)
-
-    work, plan, up, down = pl.pallas_call(
+    first_out = vmem_out(everyone, 2, LANES)
+
+    work, plan, peak, up, down = pl.pallas_call(
         start_kernel,
-        out_shape=(work_out, pltpu.VMEM((blocks, 1, LANES), jnp.int32), edge_out, edge_out),
+        out_shape=(work_out, pltpu.VMEM((blocks, 1, LANES), jnp.int32), first_out, edge_out, edge_out),
         in_specs=[hbm_spec()] * 6,
-        out_specs=(vmem_spec(),) * 4,
+        out_specs=(vmem_spec(),) * 5,
         scratch_shapes=[
             pltpu.SMEM((blocks,), jnp.int32),
             pltpu.SMEM((blocks,), jnp.int32),
@@ -528,14 +550,15 @@
         )
     )
 
+    peaks = exchange(peak, ("region", "tile"))
     above = send(down, "region", True)
     below = send(up, "region", False)
 
-    peak, left, right = pl.pallas_call(
+    left, right = pl.pallas_call(
         pack_kernel,
-        out_shape=(peak_out, strip_out, strip_out),
+        out_shape=(strip_out, strip_out),
         in_specs=[vmem_spec()],
-        out_specs=(vmem_spec(),) * 3,
+        out_specs=(vmem_spec(),) * 2,
         scratch_shapes=[pltpu.VMEM((rows, LANES), f32)],
         compiler_params=params(),
         cost_estimate=cost(20 * rows * cols, nbytes),
@@ -556,8 +579,26 @@
 
     from_left = send(right, "tile", True)
     from_right = send(left, "tile", False)
-    peaks = exchange(peak, ("region", "tile"))
-
+
+    def flux(part, work):
+        share = (1.0, 0.35, 0.65)[part]
+        return pl.pallas_call(
+            functools.partial(flux_kernel, part),
+            out_shape=work_out,
+            in_specs=[vmem_spec()],
+            out_specs=vmem_spec(),
+            scratch_shapes=[
+                pltpu.VMEM((SEND, padded, LANES), f32),
+                pltpu.VMEM((3 * (tiles + 1), padded, LANES), f32),
+                pltpu.VMEM((3 * (tiles + 1), padded + 8, LANES), f32),
+            ],
+            input_output_aliases={0: 0},
+            compiler_params=params(),
+            cost_estimate=cost(int(share * 150 * rows * cols), int(share * 4 * nbytes)),
+            name="flux",
+        )(work)
+
+    work = flux(ROWS, work)
     work = pl.pallas_call(
         columns_kernel,
         out_shape=work_out,
@@ -573,21 +614,7 @@
     )(work, left, right, from_left, from_right)
 
     for step in range(STEPS):
-        work = pl.pallas_call(
-            flux_kernel,
-            out_shape=work_out,
-            in_specs=[vmem_spec()],
-            out_specs=vmem_spec(),
-            scratch_shapes=[
-                pltpu.VMEM((SEND, padded, LANES), f32),
-                pltpu.VMEM((3 * (tiles + 1), padded, LANES), f32),
-                pltpu.VMEM((3 * (tiles + 1), padded + 8, LANES), f32),
-            ],
-            input_output_aliases={0: 0},
-            compiler_params=params(),
-            cost_estimate=cost(150 * rows * cols, 4 * nbytes),
-            name="flux",
-        )(work)
+        work = flux(ALL if step else REST, work)
         if step < STEPS - 1:
             work, peak = pl.pallas_call(
                 update_kernel,

time: 75 us -> 78.5 us (1.047)
  starting transfers between devices: 29.4 us -> 33.2 us
  waiting for transfers between devices: 15.7 us -> 14.1 us
  Pallas kernels: 28.2 us -> 29.4 us
    all_to_all x5, starting transfers between devices: 18.9 us -> 23.9 us  [exchange(): return lax.all_to_all(x, axes, 0, 0)]
    all_to_all x5, waiting for transfers between devices: 12.7 us -> 10.5 us  [exchange(): return lax.all_to_all(x, axes, 0, 0)]
    ppermute x4, starting transfers between devices: 10.5 us -> 9.29 us  [send(): return lax.ppermute(x, axis, pairs)]
    pallas_call x1, Pallas kernels: 1.86 us -> 2.75 us  [on_device(): pl.pallas_call(start_kernel, out_shape=(work_out, pltpu.VMEM((blocks, 1,...]
    pallas_call x5 -> x6, Pallas kernels: 20.3 us -> 20.6 us  [the longest x5 19.9 us: flux(): pl.pallas_call(functools.partial(flux_kernel, part), out_shape=work_out,...]
  transfers between devices with their start and end apart: 9 -> 9, of which waited for: 6 -> 5; matrix products, arithmetic and copies ran while one was open for 0% -> 0% of each run, Pallas kernels for 29% -> 28%
where the time goes in v4:
time: 78.5 us; the launch traced here: 78.1 us
  starting transfers between devices  33.2 us (42%)
  Pallas kernels  29.4 us (37%)
  waiting for transfers between devices  14.1 us (18%)
    all_to_all x5, starting transfers between devices, exchange(): return lax.all_to_all(x, axes, 0, 0)  23.9 us
    pallas_call x5, Pallas kernels, flux(): pl.pallas_call(functools.partial(flux_kernel, part), out_shape=work_out,...  19.9 us
    all_to_all x5, waiting for transfers between devices, exchange(): return lax.all_to_all(x, axes, 0, 0)  10.5 us
    ppermute x4, starting transfers between devices, send(): return lax.ppermute(x, axis, pairs)  9.29 us
    ppermute x4, waiting for transfers between devices, send(): return lax.ppermute(x, axis, pairs)  3.6 us
    pallas_call x3, Pallas kernels, on_device(): pl.pallas_call(update_kernel, out_shape=(work_out, peak_out), in_specs=[v...  3.54 us
    pallas_call x1, Pallas kernels, on_device(): pl.pallas_call(start_kernel, out_shape=(work_out, pltpu.VMEM((blocks, 1,...  2.75 us
  transfers between devices with their start and end apart: 9, of which 5 were waited for; matrix products, arithmetic and copies ran while one was open for 0% of the time, Pallas kernels for 28%

profile of v4, /device:TPU:0, one launch (start us, length us, event | category | flops | bytes accessed | tf_op | source)
XLA Modules:
  0.0 78.1 jit_solution(4987010371284104135)
XLA Ops:
  0.6 2.8 %start.1 = (f32[16,400,128]{2,1,0:T(8,128)S(1)}, s32[24,1,128]{2,1,0:T(1,128)S(1)}, f32[32,2,128]{2,1,0:T(2,128)}, f32[10,4,128]{2,1,0:T(4,128)S(1)}, f32[10,4,128]{2,1,0:T(4,128)S(1)}) custom-call(s32[24]{0:T(128)} %bitcast.5, s32[24]{0:T(128)} %bitcast.6, s32[64]{0:T(128)} %bitcast.7, f32[64]{0:T(128)} %bitcast.8, f32[384,256]{1,0:T(8,128)} %depth_hbm.1, ...), custom_call_target="tpu_custom_call" | custom-call | flops 196608 | bytes 1179648 | tf_op jit(solution)/shard_map/start/pallas_call | solution.py:523
  3.4 7.3 %all-to-all-start = ((f32[32,2,128]{2,1,0:T(2,128)}), f32[32,2,128]{2,1,0:T(2,128)S(1)}, u32[]{:S(2)}, u32[]{:S(2)}) async-start(f32[32,2,128]{2,1,0:T(2,128)} %get-tuple-element.23), calls=%async_computation | async-start | bytes 65536 | tf_op jit(solution)/shard_map/all_to_all | solution.py:497
  10.7 3.7 %collective-permute-start = (f32[10,4,128]{2,1,0:T(4,128)S(1)}, f32[10,4,128]{2,1,0:T(4,128)S(1)}, u32[]{:S(2)}, u32[]{:S(2)}) collective-permute-start(f32[10,4,128]{2,1,0:T(4,128)S(1)} %get-tuple-element.27), channel_id=1, source_target_pairs={{0,8},{8,16},{16,24},{1,9},{9,17},{17,25},{2,10},{10,18},{18,26},{... | collective-permute-start | bytes 61448 | tf_op jit(solution)/shard_map/ppermute | solution.py:503
  14.4 1.3 %collective-permute-start.1 = (f32[10,4,128]{2,1,0:T(4,128)S(1)}, f32[10,4,128]{2,1,0:T(4,128)S(1)}, u32[]{:S(2)}, u32[]{:S(2)}) collective-permute-start(f32[10,4,128]{2,1,0:T(4,128)S(1)} %get-tuple-element.28), channel_id=1, source_target_pairs={{8,0},{16,8},{24,16},{9,1},{17,9},{25,17},{10,2},{18,10},{26,18},{... | collective-permute-start | bytes 61448 | tf_op jit(solution)/shard_map/ppermute | solution.py:503
  16.5 3.6 %collective-permute-done.1.below_ref = f32[10,4,128]{2,1,0:T(4,128)S(1)} collective-permute-done((f32[10,4,128]{2,1,0:T(4,128)S(1)}, f32[10,4,128]{2,1,0:T(4,128)S(1)}, u32[]{:S(2)}, u32[]{:S(2)}) %collective-permute-start.1) | collective-permute-done | bytes 20512 | tf_op jit(solution)/shard_map/ppermute | solution.py:503
  20.2 1.3 %collective-permute-start.3 = (f32[5,4,512]{2,1,0:T(4,128)S(1)}, f32[5,4,512]{2,1,0:T(4,128)S(1)}, u32[]{:S(2)}, u32[]{:S(2)}) collective-permute-start(f32[5,4,512]{2,1,0:T(4,128)S(1)} %get-tuple-element.30.own_left), channel_id=1, source_target_pairs={{1,0},{2,1},{3,2},{4,3},{5,4},{6,5},{7,6},{9,8},{10,9},{11,10},{12... | collective-permute-start | bytes 122888 | tf_op jit(solution)/shard_map/ppermute | solution.py:503
  21.5 3.0 %collective-permute-start.2 = (f32[5,4,512]{2,1,0:T(4,128)S(1)}, f32[5,4,512]{2,1,0:T(4,128)S(1)}, u32[]{:S(2)}, u32[]{:S(2)}) collective-permute-start(f32[5,4,512]{2,1,0:T(4,128)S(1)} %get-tuple-element.31.own_right), channel_id=1, source_target_pairs={{0,1},{1,2},{2,3},{3,4},{4,5},{5,6},{6,7},{8,9},{9,10},{10,11},{11... | collective-permute-start | bytes 122888 | tf_op jit(solution)/shard_map/ppermute | solution.py:503
  24.6 1.2 %flux.5.work_in = f32[16,400,128]{2,1,0:T(8,128)S(1)} custom-call(f32[16,400,128]{2,1,0:T(8,128)S(1)} %get-tuple-element.29.work_in), custom_call_target="tpu_custom_call", output_to_operand_aliasing={{}: (0, {})} | custom-call | flops 5160960 | bytes 1651507 | tf_op jit(solution)/shard_map/flux/pallas_call | solution.py:585
  26.0 4.4 %flux.6.work_in = f32[16,400,128]{2,1,0:T(8,128)S(1)} custom-call(f32[16,400,128]{2,1,0:T(8,128)S(1)} %columns.1.work_in), custom_call_target="tpu_custom_call", output_to_operand_aliasing={{}: (0, {})} | custom-call | flops 9584640 | bytes 3067084 | tf_op jit(solution)/shard_map/flux/pallas_call | solution.py:585
  30.4 1.2 %update.3 = (f32[16,400,128]{2,1,0:T(8,128)S(1)}, f32[32,1,128]{2,1,0:T(1,128)}) custom-call(f32[32,2,128]{2,1,0:T(2,128)S(1)} %all-to-all-done.peak_ref, f32[16,400,128]{2,1,0:T(8,128)S(1)} %flux.6.work_in), custom_call_target="tpu_custom_call", output_to_operand_aliasing={{0}: (1, {})} | custom-call | flops 1966080 | bytes 1179648 | tf_op jit(solution)/shard_map/update/pallas_call | solution.py:619
  31.6 6.3 %all-to-all-start.1 = ((f32[32,1,128]{2,1,0:T(1,128)}), f32[32,1,128]{2,1,0:T(1,128)S(1)}, u32[]{:S(2)}, u32[]{:S(2)}) async-start(f32[32,1,128]{2,1,0:T(1,128)} %get-tuple-element.32), calls=%async_computation.1 | async-start | bytes 32768 | tf_op jit(solution)/shard_map/all_to_all | solution.py:497
  37.9 4.8 %flux.7.work_in = f32[16,400,128]{2,1,0:T(8,128)S(1)} custom-call(f32[16,400,128]{2,1,0:T(8,128)S(1)} %get-tuple-element.33.work_in), custom_call_target="tpu_custom_call", output_to_operand_aliasing={{}: (0, {})} | custom-call | flops 14745600 | bytes 4718592 | tf_op jit(solution)/shard_map/flux/pallas_call | solution.py:585
  42.6 2.3 %all-to-all-done.1.peak_ref = f32[32,1,128]{2,1,0:T(1,128)S(1)} async-done(((f32[32,1,128]{2,1,0:T(1,128)}), f32[32,1,128]{2,1,0:T(1,128)S(1)}, u32[]{:S(2)}, u32[]{:S(2)}) %all-to-all-start.1) | async-done | bytes 16416 | tf_op jit(solution)/shard_map/all_to_all | solution.py:497
  44.9 1.2 %update.4 = (f32[16,400,128]{2,1,0:T(8,128)S(1)}, f32[32,1,128]{2,1,0:T(1,128)}) custom-call(f32[32,1,128]{2,1,0:T(1,128)S(1)} %all-to-all-done.1.peak_ref, f32[16,400,128]{2,1,0:T(8,128)S(1)} %flux.7.work_in), custom_call_target="tpu_custom_call", output_to_operand_aliasing={{0}: (1, {})} | custom-call | flops 1966080 | bytes 1179648 | tf_op jit(solution)/shard_map/update/pallas_call | solution.py:619
  46.1 3.5 %all-to-all-start.2 = ((f32[32,1,128]{2,1,0:T(1,128)}), f32[32,1,128]{2,1,0:T(1,128)S(1)}, u32[]{:S(2)}, u32[]{:S(2)}) async-start(f32[32,1,128]{2,1,0:T(1,128)} %get-tuple-element.34), calls=%async_computation.2 | async-start | bytes 32768 | tf_op jit(solution)/shard_map/all_to_all | solution.py:497
  49.6 4.8 %flux.8.work_in = f32[16,400,128]{2,1,0:T(8,128)S(1)} custom-call(f32[16,400,128]{2,1,0:T(8,128)S(1)} %get-tuple-element.35.work_in), custom_call_target="tpu_custom_call", output_to_operand_aliasing={{}: (0, {})} | custom-call | flops 14745600 | bytes 4718592 | tf_op jit(solution)/shard_map/flux/pallas_call | solution.py:585
  54.4 2.3 %all-to-all-done.2.peak_ref = f32[32,1,128]{2,1,0:T(1,128)S(1)} async-done(((f32[32,1,128]{2,1,0:T(1,128)}), f32[32,1,128]{2,1,0:T(1,128)S(1)}, u32[]{:S(2)}, u32[]{:S(2)}) %all-to-all-start.2) | async-done | bytes 16416 | tf_op jit(solution)/shard_map/all_to_all | solution.py:497
  56.7 1.2 %update.5 = (f32[16,400,128]{2,1,0:T(8,128)S(1)}, f32[32,1,128]{2,1,0:T(1,128)}) custom-call(f32[32,1,128]{2,1,0:T(1,128)S(1)} %all-to-all-done.2.peak_ref, f32[16,400,128]{2,1,0:T(8,128)S(1)} %flux.8.work_in), custom_call_target="tpu_custom_call", output_to_operand_aliasing={{0}: (1, {})} | custom-call | flops 1966080 | bytes 1179648 | tf_op jit(solution)/shard_map/update/pallas_call | solution.py:619
  57.9 3.5 %all-to-all-start.3 = ((f32[32,1,128]{2,1,0:T(1,128)}), f32[32,1,128]{2,1,0:T(1,128)S(1)}, u32[]{:S(2)}, u32[]{:S(2)}) async-start(f32[32,1,128]{2,1,0:T(1,128)} %get-tuple-element.36), calls=%async_computation.3 | async-start | bytes 32768 | tf_op jit(solution)/shard_map/all_to_all | solution.py:497
  61.4 4.8 %flux.9.work_in = f32[16,400,128]{2,1,0:T(8,128)S(1)} custom-call(f32[16,400,128]{2,1,0:T(8,128)S(1)} %get-tuple-element.38.work_in), custom_call_target="tpu_custom_call", output_to_operand_aliasing={{}: (0, {})} | custom-call | flops 14745600 | bytes 4718592 | tf_op jit(solution)/shard_map/flux/pallas_call | solution.py:585
  66.2 2.3 %all-to-all-done.3.peak_ref = f32[32,1,128]{2,1,0:T(1,128)S(1)} async-done(((f32[32,1,128]{2,1,0:T(1,128)}), f32[32,1,128]{2,1,0:T(1,128)S(1)}, u32[]{:S(2)}, u32[]{:S(2)}) %all-to-all-start.3) | async-done | bytes 16416 | tf_op jit(solution)/shard_map/all_to_all | solution.py:497
  68.5 1.1 %last.1 = (f32[16,400,128]{2,1,0:T(8,128)S(1)}, f32[8,1,128]{2,1,0:T(1,128)}) custom-call(f32[32,1,128]{2,1,0:T(1,128)S(1)} %all-to-all-done.3.peak_ref, s32[24,1,128]{2,1,0:T(1,128)S(1)} %get-tuple-element.37.plan_ref, f32[16,400,128]{2,1,0:T(8,128)S(1)} %flux.9.work_in), custom_call_target="tpu_custom_call", output_to_operand_aliasing={{0}: (2, {})} | custom-call | flops 1966080 | bytes 2359296 | tf_op jit(solution)/shard_map/last/pallas_call | solution.py:631
  69.6 3.3 %all-to-all-start.4 = ((f32[8,1,128]{2,1,0:T(1,128)}), f32[8,1,128]{2,1,0:T(1,128)S(1)}, u32[]{:S(2)}, u32[]{:S(2)}) async-start(f32[8,1,128]{2,1,0:T(1,128)} %get-tuple-element.42), calls=%async_computation.4 | async-start | bytes 8192 | tf_op jit(solution)/shard_map/all_to_all | solution.py:497
  74.0 3.5 %all-to-all-done.4 = f32[8,1,128]{2,1,0:T(1,128)S(1)} async-done(((f32[8,1,128]{2,1,0:T(1,128)}), f32[8,1,128]{2,1,0:T(1,128)S(1)}, u32[]{:S(2)}, u32[]{:S(2)}) %all-to-all-start.4) | async-done | bytes 4128 | tf_op jit(solution)/shard_map/all_to_all | solution.py:497
  (9 shorter events, 2.8 us)
Async XLA Ops:
  3.4 27.0 %all-to-all-start = ((f32[32,2,128]{2,1,0:T(2,128)}), f32[32,2,128]{2,1,0:T(2,128)S(1)}, u32[]{:S(2)}, u32[]{:S(2)}) async-start(f32[32,2,128]{2,1,0:T(2,128)} %get-tuple-element.23), calls=%async_computation | async-start | bytes 65536 | tf_op jit(solution)/shard_map/all_to_all | solution.py:497
  10.7 5.8 %collective-permute-start = (f32[10,4,128]{2,1,0:T(4,128)S(1)}, f32[10,4,128]{2,1,0:T(4,128)S(1)}, u32[]{:S(2)}, u32[]{:S(2)}) collective-permute-start(f32[10,4,128]{2,1,0:T(4,128)S(1)} %get-tuple-element.27), channel_id=1, source_target_pairs={{0,8},{8,16},{16,24},{1,9},{9,17},{17,25},{2,10},{10,18},{18,26},{... | collective-permute-start | bytes 61448 | tf_op jit(solution)/shard_map/ppermute | solution.py:503
  14.4 5.7 %collective-permute-start.1 = (f32[10,4,128]{2,1,0:T(4,128)S(1)}, f32[10,4,128]{2,1,0:T(4,128)S(1)}, u32[]{:S(2)}, u32[]{:S(2)}) collective-permute-start(f32[10,4,128]{2,1,0:T(4,128)S(1)} %get-tuple-element.28), channel_id=1, source_target_pairs={{8,0},{16,8},{24,16},{9,1},{17,9},{25,17},{10,2},{18,10},{26,18},{... | collective-permute-start | bytes 61448 | tf_op jit(solution)/shard_map/ppermute | solution.py:503
  20.2 5.6 %collective-permute-start.3 = (f32[5,4,512]{2,1,0:T(4,128)S(1)}, f32[5,4,512]{2,1,0:T(4,128)S(1)}, u32[]{:S(2)}, u32[]{:S(2)}) collective-permute-start(f32[5,4,512]{2,1,0:T(4,128)S(1)} %get-tuple-element.30.own_left), channel_id=1, source_target_pairs={{1,0},{2,1},{3,2},{4,3},{5,4},{6,5},{7,6},{9,8},{10,9},{11,10},{12... | collective-permute-start | bytes 122888 | tf_op jit(solution)/shard_map/ppermute | solution.py:503
  21.5 4.3 %collective-permute-start.2 = (f32[5,4,512]{2,1,0:T(4,128)S(1)}, f32[5,4,512]{2,1,0:T(4,128)S(1)}, u32[]{:S(2)}, u32[]{:S(2)}) collective-permute-start(f32[5,4,512]{2,1,0:T(4,128)S(1)} %get-tuple-element.31.own_right), channel_id=1, source_target_pairs={{0,1},{1,2},{2,3},{3,4},{4,5},{5,6},{6,7},{8,9},{9,10},{10,11},{11... | collective-permute-start | bytes 122888 | tf_op jit(solution)/shard_map/ppermute | solution.py:503
  31.6 13.3 %all-to-all-start.1 = ((f32[32,1,128]{2,1,0:T(1,128)}), f32[32,1,128]{2,1,0:T(1,128)S(1)}, u32[]{:S(2)}, u32[]{:S(2)}) async-start(f32[32,1,128]{2,1,0:T(1,128)} %get-tuple-element.32), calls=%async_computation.1 | async-start | bytes 32768 | tf_op jit(solution)/shard_map/all_to_all | solution.py:497
  46.1 10.6 %all-to-all-start.2 = ((f32[32,1,128]{2,1,0:T(1,128)}), f32[32,1,128]{2,1,0:T(1,128)S(1)}, u32[]{:S(2)}, u32[]{:S(2)}) async-start(f32[32,1,128]{2,1,0:T(1,128)} %get-tuple-element.34), calls=%async_computation.2 | async-start | bytes 32768 | tf_op jit(solution)/shard_map/all_to_all | solution.py:497
  57.9 10.6 %all-to-all-start.3 = ((f32[32,1,128]{2,1,0:T(1,128)}), f32[32,1,128]{2,1,0:T(1,128)S(1)}, u32[]{:S(2)}, u32[]{:S(2)}) async-start(f32[32,1,128]{2,1,0:T(1,128)} %get-tuple-element.36), calls=%async_computation.3 | async-start | bytes 32768 | tf_op jit(solution)/shard_map/all_to_all | solution.py:497
  69.6 7.9 %all-to-all-start.4 = ((f32[8,1,128]{2,1,0:T(1,128)}), f32[8,1,128]{2,1,0:T(1,128)S(1)}, u32[]{:S(2)}, u32[]{:S(2)}) async-start(f32[8,1,128]{2,1,0:T(1,128)} %get-tuple-element.42), calls=%async_computation.4 | async-start | bytes 8192 | tf_op jit(solution)/shard_map/all_to_all | solution.py:497

commit v5 on v3

--- a/solution.py
+++ b/solution.py
@@ -326,7 +326,7 @@
             return [beside[k, at, :] for k in range(3)]
         return [work[k * tiles + c, at, :] for k in range(3)]
 
-    lax.fori_loop(0, row_tiles // 5, derive, 0)
+    lax.fori_loop(0, row_tiles // 5, derive, 0, unroll=5)
     for f in range(3):
         for c in range(tiles + 1):
             faces[f * (tiles + 1) + c, 0:8, :] = jnp.zeros((8, LANES), jnp.float32)
@@ -391,45 +391,49 @@
 
 def moved(work, c, at, ratio):
     tiles = tiles_of(work)
-    new = [
+    return [
         work[f * tiles + c, at, :] - ratio * work[(DIFF + f) * tiles + c, at, :] for f in range(3)
     ]
-    for f in range(3):
-        work[f * tiles + c, at, :] = new[f]
-    return new
-
-
-def update_kernel(peak_ref, work_in, work, next_ref):
+
+
+def move_own(work, at, ratio):
+    tiles = tiles_of(work)
+    for c in range(tiles):
+        for f, new in enumerate(moved(work, c, at, ratio)):
+            work[f * tiles + c, at, :] = new
+
+
+def update_kernel(peak_ref, work_in, work, next_hbm, spread, sem):
     tiles = tiles_of(work)
     row_tiles = work.shape[1] // 8
     strip = strip_at(work)
     ratio = step_ratio(peak_ref)
-    lane = lane_ids(8)
-    strip_ratio = jnp.where(lane < 2 * HALO * 3, ratio, 0.0)
-
-    def move_strip(at):
-        old = work[strip, at, :]
-        work[strip, at, :] = old - strip_ratio * pltpu.roll(old, LANES - STRIP_DIFF, 1)
-
-    def one(r, acc):
+
+    def find(r, acc):
         at = aligned(r * 8 + TOP, 8)
         active = work[active_at(work), at, :] > 0.5
         for c in range(tiles):
-            new = moved(work, c, at, ratio)
-            acc = jnp.maximum(acc, jnp.where(active, speed_of(*new), 0.0))
-        move_strip(at)
+            acc = jnp.maximum(acc, jnp.where(active, speed_of(*moved(work, c, at, ratio)), 0.0))
         return acc
 
     zero = jnp.zeros((8, LANES), jnp.float32)
-    acc = lax.fori_loop(0, row_tiles - 2, one, zero, unroll=8)
-    for at in (slice(0, 8), slice(8 * row_tiles - 8, 8 * row_tiles)):
-        for c in range(tiles):
-            moved(work, c, at, ratio)
-        move_strip(at)
-    spread_peak(acc, next_ref)
-
-
-def last_kernel(peak_ref, plan_ref, work_in, work, next_ref, best):
+    spread_peak(lax.fori_loop(0, row_tiles - 2, find, zero, unroll=16), spread)
+    copy = pltpu.make_async_copy(spread, next_hbm, sem)
+    copy.start()
+    strip_ratio = jnp.where(lane_ids(8) < 2 * HALO * 3, ratio, 0.0)
+
+    def move(r, carry):
+        at = aligned(r * 8, 8)
+        move_own(work, at, ratio)
+        old = work[strip, at, :]
+        work[strip, at, :] = old - strip_ratio * pltpu.roll(old, LANES - STRIP_DIFF, 1)
+        return carry
+
+    lax.fori_loop(0, row_tiles, move, 0, unroll=10)
+    copy.wait()
+
+
+def last_kernel(peak_ref, plan_ref, work, next_ref, best):
     tiles = tiles_of(work)
     blocks = plan_ref.shape[0]
     block_rows = (work.shape[1] - 2 * 8) // blocks
@@ -444,7 +448,7 @@
         best[b] = acc
         return carry
 
-    lax.fori_loop(0, blocks, one_block, 0, unroll=4)
+    lax.fori_loop(0, blocks, one_block, 0, unroll=8)
     for t in range(next_ref.shape[0]):
         acc = jnp.zeros((8, LANES), jnp.float32)
         for b in range(blocks):
@@ -453,9 +457,16 @@
         next_ref[t] = jnp.broadcast_to(jnp.max(top, axis=1, keepdims=True), (1, LANES))
 
 
-def store_kernel(work, depth_hbm, mom_hbm, sem):
+def store_kernel(peak_ref, work_in, work, depth_hbm, mom_hbm, sem):
     rows, cols = depth_hbm.shape
     tiles = cols // LANES
+    ratio = step_ratio(peak_ref)
+
+    def move(r, carry):
+        move_own(work, aligned(r * 8 + TOP, 8), ratio)
+        return carry
+
+    lax.fori_loop(0, rows // 8, move, 0, unroll=8)
     copies = []
     for k, dst in enumerate([depth_hbm, mom_hbm.at[0], mom_hbm.at[1]]):
         for c in range(tiles):
@@ -478,7 +489,7 @@
 
 def send(x, axis, forward):
     count = lax.axis_size(axis)
-    pairs = [(i, i + 1) if forward else (i + 1, i) for i in range(count - 1)]
+    pairs = [(i, (i + 1) % count) if forward else ((i + 1) % count, i) for i in range(count)]
     return lax.ppermute(x, axis, pairs)
 
 
@@ -591,9 +602,13 @@
         if step < STEPS - 1:
             work, peak = pl.pallas_call(
                 update_kernel,
-                out_shape=(work_out, peak_out),
+                out_shape=(work_out, jax.ShapeDtypeStruct((everyone, 1, LANES), f32)),
                 in_specs=[vmem_spec()] * 2,
-                out_specs=(vmem_spec(),) * 2,
+                out_specs=(vmem_spec(), hbm_spec()),
+                scratch_shapes=[
+                    pltpu.VMEM((everyone, 1, LANES), f32),
+                    pltpu.SemaphoreType.DMA,
+                ],
                 input_output_aliases={1: 0},
                 compiler_params=params(),
                 cost_estimate=cost(20 * rows * cols, nbytes),
@@ -601,31 +616,32 @@
             )(peaks, work)
             peaks = exchange(peak, ("region", "tile"))
 
-    work, best = pl.pallas_call(
+    best = pl.pallas_call(
         last_kernel,
-        out_shape=(work_out, vmem_out(tile_count, 1, LANES)),
+        out_shape=vmem_out(tile_count, 1, LANES),
         in_specs=[vmem_spec()] * 3,
-        out_specs=(vmem_spec(),) * 2,
+        out_specs=vmem_spec(),
         scratch_shapes=[pltpu.VMEM((blocks, 8, LANES), f32)],
-        input_output_aliases={2: 0},
         compiler_params=params(),
         cost_estimate=cost(20 * rows * cols, 2 * nbytes),
         name="last",
     )(peaks, plan, work)
     helpers = exchange(best, "tile")
-    new_depth, new_momentum = pl.pallas_call(
+    work, new_depth, new_momentum = pl.pallas_call(
         store_kernel,
         out_shape=(
+            work_out,
             jax.ShapeDtypeStruct((rows, cols), f32),
             jax.ShapeDtypeStruct((2, rows, cols), f32),
         ),
-        in_specs=[vmem_spec()],
-        out_specs=(hbm_spec(),) * 2,
+        in_specs=[vmem_spec()] * 2,
+        out_specs=(vmem_spec(), hbm_spec(), hbm_spec()),
         scratch_shapes=[pltpu.SemaphoreType.DMA((3, tiles))],
+        input_output_aliases={1: 0},
         compiler_params=params(),
         cost_estimate=cost(10 * rows * cols, 2 * nbytes),
         name="store",
-    )(work)
+    )(peaks, work)
     return new_depth, new_momentum, jnp.max(helpers[:, :, :1], axis=0)
 
 

time: 75 us -> 66.9 us (0.89)
  starting transfers between devices: 29.4 us -> 24.6 us
  Pallas kernels: 28.2 us -> 25.6 us
    ppermute x4, starting transfers between devices: 10.5 us -> 6.22 us  [send(): return lax.ppermute(x, axis, pairs)]
    ppermute x4, waiting for transfers between devices: 3.05 us -> 0.59 us  [send(): return lax.ppermute(x, axis, pairs)]
    pallas_call x4, Pallas kernels: 19 us -> 16.9 us  [on_device(): pl.pallas_call(flux_kernel, out_shape=work_out, in_specs=[vmem_spec()], o...]
    all_to_all x5, waiting for transfers between devices: 12.7 us -> 14.5 us  [exchange(): return lax.all_to_all(x, axes, 0, 0)]
  transfers between devices with their start and end apart: 9 -> 9, of which waited for: 6 -> 7; matrix products, arithmetic and copies ran while one was open for 0% -> 0% of each run, Pallas kernels for 29% -> 29%
where the time goes in v5:
time: 66.9 us; the launch traced here: 66.6 us
  Pallas kernels  25.6 us (38%)
  starting transfers between devices  24.6 us (37%)
  waiting for transfers between devices  15.1 us (23%)
  between operations  0.74 us (1%)
    all_to_all x5, starting transfers between devices, exchange(): return lax.all_to_all(x, axes, 0, 0)  18.3 us
    pallas_call x4, Pallas kernels, on_device(): pl.pallas_call(flux_kernel, out_shape=work_out, in_specs=[vmem_spec()], o...  16.9 us
    all_to_all x5, waiting for transfers between devices, exchange(): return lax.all_to_all(x, axes, 0, 0)  14.5 us
    ppermute x4, starting transfers between devices, send(): return lax.ppermute(x, axis, pairs)  6.22 us
    pallas_call x3, Pallas kernels, on_device(): pl.pallas_call(update_kernel, out_shape=(work_out, jax.ShapeDtypeStruct((...  2.87 us
    pallas_call x1, Pallas kernels, on_device(): pl.pallas_call(start_kernel, out_shape=(work_out, pltpu.VMEM((blocks, 1,...  1.86 us
  transfers between devices with their start and end apart: 9, of which 7 were waited for; matrix products, arithmetic and copies ran while one was open for 0% of the time, Pallas kernels for 29%

profile of v5, /device:TPU:0, one launch (start us, length us, event | category | flops | bytes accessed | tf_op | source)
XLA Modules:
  0.0 66.6 jit_solution(12143443859230321600)
XLA Ops:
  0.6 1.9 %start.1 = (f32[16,400,128]{2,1,0:T(8,128)S(1)}, s32[24,1,128]{2,1,0:T(1,128)S(1)}, f32[10,4,128]{2,1,0:T(4,128)S(1)}, f32[10,4,128]{2,1,0:T(4,128)S(1)}) custom-call(s32[24]{0:T(128)} %bitcast.5, s32[24]{0:T(128)} %bitcast.6, s32[64]{0:T(128)} %bitcast.7, f32[64]{0:T(128)} %bitcast.8, f32[384,256]{1,0:T(8,128)} %depth_hbm.1, f32[2,384,256]{2,1,0:T(8,128)} %mom_hbm.1), custom_call_target="tpu_custom_call" | custom-call | flops 196608 | bytes 1179648 | tf_op jit(solution)/shard_map/start/pallas_call | solution.py:512
  2.5 3.1 %collective-permute-start = (f32[10,4,128]{2,1,0:T(4,128)S(1)}, f32[10,4,128]{2,1,0:T(4,128)S(1)}, u32[]{:S(2)}, u32[]{:S(2)}) collective-permute-start(f32[10,4,128]{2,1,0:T(4,128)S(1)} %get-tuple-element.25), channel_id=1, source_target_pairs={{0,8},{8,16},{16,24},{24,0},{1,9},{9,17},{17,25},{25,1},{2,10},{10... | collective-permute-start | bytes 61448 | tf_op jit(solution)/shard_map/ppermute | solution.py:493
  5.6 2.1 %collective-permute-start.1 = (f32[10,4,128]{2,1,0:T(4,128)S(1)}, f32[10,4,128]{2,1,0:T(4,128)S(1)}, u32[]{:S(2)}, u32[]{:S(2)}) collective-permute-start(f32[10,4,128]{2,1,0:T(4,128)S(1)} %get-tuple-element.26), channel_id=1, source_target_pairs={{8,0},{16,8},{24,16},{0,24},{9,1},{17,9},{25,17},{1,25},{10,2},{18... | collective-permute-start | bytes 61448 | tf_op jit(solution)/shard_map/ppermute | solution.py:493
  7.7 1.3 %pack.1 = (f32[32,1,128]{2,1,0:T(1,128)}, f32[5,4,512]{2,1,0:T(4,128)S(1)}, f32[5,4,512]{2,1,0:T(4,128)S(1)}) custom-call(f32[16,400,128]{2,1,0:T(8,128)S(1)} %get-tuple-element.21.work.work_in), custom_call_target="tpu_custom_call" | custom-call | flops 1966080 | bytes 1179648 | tf_op jit(solution)/shard_map/pack/pallas_call | solution.py:545
  9.7 1.0 %collective-permute-start.3 = (f32[5,4,512]{2,1,0:T(4,128)S(1)}, f32[5,4,512]{2,1,0:T(4,128)S(1)}, u32[]{:S(2)}, u32[]{:S(2)}) collective-permute-start(f32[5,4,512]{2,1,0:T(4,128)S(1)} %get-tuple-element.28.own_left), channel_id=1, source_target_pairs={{1,0},{2,1},{3,2},{4,3},{5,4},{6,5},{7,6},{0,7},{9,8},{10,9},{11,1... | collective-permute-start | bytes 122888 | tf_op jit(solution)/shard_map/ppermute | solution.py:493
  10.8 5.8 %all-to-all-start = ((f32[32,1,128]{2,1,0:T(1,128)}), f32[32,1,128]{2,1,0:T(1,128)S(1)}, u32[]{:S(2)}, u32[]{:S(2)}) async-start(f32[32,1,128]{2,1,0:T(1,128)} %get-tuple-element.22), calls=%async_computation | async-start | bytes 32768 | tf_op jit(solution)/shard_map/all_to_all | solution.py:487
  16.8 4.2 %flux.4.work_in = f32[16,400,128]{2,1,0:T(8,128)S(1)} custom-call(f32[16,400,128]{2,1,0:T(8,128)S(1)} %columns.1.work_in), custom_call_target="tpu_custom_call", output_to_operand_aliasing={{}: (0, {})} | custom-call | flops 14745600 | bytes 4718592 | tf_op jit(solution)/shard_map/flux/pallas_call | solution.py:587
  21.0 2.6 %all-to-all-done.peak_ref = f32[32,1,128]{2,1,0:T(1,128)S(1)} async-done(((f32[32,1,128]{2,1,0:T(1,128)}), f32[32,1,128]{2,1,0:T(1,128)S(1)}, u32[]{:S(2)}, u32[]{:S(2)}) %all-to-all-start) | async-done | bytes 16416 | tf_op jit(solution)/shard_map/all_to_all | solution.py:487
  23.7 1.0 %update.3 = (f32[16,400,128]{2,1,0:T(8,128)S(1)}, f32[32,1,128]{2,1,0:T(1,128)}) custom-call(f32[32,1,128]{2,1,0:T(1,128)S(1)} %all-to-all-done.peak_ref, f32[16,400,128]{2,1,0:T(8,128)S(1)} %flux.4.work_in), custom_call_target="tpu_custom_call", output_to_operand_aliasing={{0}: (1, {})} | custom-call | flops 1966080 | bytes 1179648 | tf_op jit(solution)/shard_map/update/pallas_call | solution.py:603
  24.7 3.2 %all-to-all-start.1 = ((f32[32,1,128]{2,1,0:T(1,128)}), f32[32,1,128]{2,1,0:T(1,128)S(1)}, u32[]{:S(2)}, u32[]{:S(2)}) async-start(f32[32,1,128]{2,1,0:T(1,128)} %get-tuple-element.30), calls=%async_computation.1 | async-start | bytes 32768 | tf_op jit(solution)/shard_map/all_to_all | solution.py:487
  27.9 4.2 %flux.5.work_in = f32[16,400,128]{2,1,0:T(8,128)S(1)} custom-call(f32[16,400,128]{2,1,0:T(8,128)S(1)} %get-tuple-element.31.work_in), custom_call_target="tpu_custom_call", output_to_operand_aliasing={{}: (0, {})} | custom-call | flops 14745600 | bytes 4718592 | tf_op jit(solution)/shard_map/flux/pallas_call | solution.py:587
  32.1 2.8 %all-to-all-done.1.peak_ref = f32[32,1,128]{2,1,0:T(1,128)S(1)} async-done(((f32[32,1,128]{2,1,0:T(1,128)}), f32[32,1,128]{2,1,0:T(1,128)S(1)}, u32[]{:S(2)}, u32[]{:S(2)}) %all-to-all-start.1) | async-done | bytes 16416 | tf_op jit(solution)/shard_map/all_to_all | solution.py:487
  34.9 1.0 %update.4 = (f32[16,400,128]{2,1,0:T(8,128)S(1)}, f32[32,1,128]{2,1,0:T(1,128)}) custom-call(f32[32,1,128]{2,1,0:T(1,128)S(1)} %all-to-all-done.1.peak_ref, f32[16,400,128]{2,1,0:T(8,128)S(1)} %flux.5.work_in), custom_call_target="tpu_custom_call", output_to_operand_aliasing={{0}: (1, {})} | custom-call | flops 1966080 | bytes 1179648 | tf_op jit(solution)/shard_map/update/pallas_call | solution.py:603
  35.9 3.0 %all-to-all-start.2 = ((f32[32,1,128]{2,1,0:T(1,128)}), f32[32,1,128]{2,1,0:T(1,128)S(1)}, u32[]{:S(2)}, u32[]{:S(2)}) async-start(f32[32,1,128]{2,1,0:T(1,128)} %get-tuple-element.32), calls=%async_computation.2 | async-start | bytes 32768 | tf_op jit(solution)/shard_map/all_to_all | solution.py:487
  38.9 4.2 %flux.6.work_in = f32[16,400,128]{2,1,0:T(8,128)S(1)} custom-call(f32[16,400,128]{2,1,0:T(8,128)S(1)} %get-tuple-element.33.work_in), custom_call_target="tpu_custom_call", output_to_operand_aliasing={{}: (0, {})} | custom-call | flops 14745600 | bytes 4718592 | tf_op jit(solution)/shard_map/flux/pallas_call | solution.py:587
  43.1 2.8 %all-to-all-done.2.peak_ref = f32[32,1,128]{2,1,0:T(1,128)S(1)} async-done(((f32[32,1,128]{2,1,0:T(1,128)}), f32[32,1,128]{2,1,0:T(1,128)S(1)}, u32[]{:S(2)}, u32[]{:S(2)}) %all-to-all-start.2) | async-done | bytes 16416 | tf_op jit(solution)/shard_map/all_to_all | solution.py:487
  46.0 1.0 %update.5 = (f32[16,400,128]{2,1,0:T(8,128)S(1)}, f32[32,1,128]{2,1,0:T(1,128)}) custom-call(f32[32,1,128]{2,1,0:T(1,128)S(1)} %all-to-all-done.2.peak_ref, f32[16,400,128]{2,1,0:T(8,128)S(1)} %flux.6.work_in), custom_call_target="tpu_custom_call", output_to_operand_aliasing={{0}: (1, {})} | custom-call | flops 1966080 | bytes 1179648 | tf_op jit(solution)/shard_map/update/pallas_call | solution.py:603
  46.9 3.0 %all-to-all-start.3 = ((f32[32,1,128]{2,1,0:T(1,128)}), f32[32,1,128]{2,1,0:T(1,128)S(1)}, u32[]{:S(2)}, u32[]{:S(2)}) async-start(f32[32,1,128]{2,1,0:T(1,128)} %get-tuple-element.34), calls=%async_computation.3 | async-start | bytes 32768 | tf_op jit(solution)/shard_map/all_to_all | solution.py:487
  50.0 4.2 %flux.7.work_in.work = f32[16,400,128]{2,1,0:T(8,128)S(1)} custom-call(f32[16,400,128]{2,1,0:T(8,128)S(1)} %get-tuple-element.35.work_in), custom_call_target="tpu_custom_call", output_to_operand_aliasing={{}: (0, {})} | custom-call | flops 14745600 | bytes 4718592 | tf_op jit(solution)/shard_map/flux/pallas_call | solution.py:587
  54.2 2.8 %all-to-all-done.3.peak_ref = f32[32,1,128]{2,1,0:T(1,128)S(1)} async-done(((f32[32,1,128]{2,1,0:T(1,128)}), f32[32,1,128]{2,1,0:T(1,128)S(1)}, u32[]{:S(2)}, u32[]{:S(2)}) %all-to-all-start.3) | async-done | bytes 16416 | tf_op jit(solution)/shard_map/all_to_all | solution.py:487
  57.0 1.1 %last.1 = f32[8,1,128]{2,1,0:T(1,128)} custom-call(f32[32,1,128]{2,1,0:T(1,128)S(1)} %all-to-all-done.3.peak_ref, s32[24,1,128]{2,1,0:T(1,128)S(1)} %get-tuple-element.38.plan_ref, f32[16,400,128]{2,1,0:T(8,128)S(1)} %flux.7.work_in.work), custom_call_target="tpu_custom_call" | custom-call | flops 1966080 | bytes 2359296 | tf_op jit(solution)/shard_map/last/pallas_call | solution.py:619
  58.1 3.3 %all-to-all-start.4 = ((f32[8,1,128]{2,1,0:T(1,128)}), f32[8,1,128]{2,1,0:T(1,128)S(1)}, u32[]{:S(2)}, u32[]{:S(2)}) async-start(f32[8,1,128]{2,1,0:T(1,128)} %last.1), calls=%async_computation.4 | async-start | bytes 8192 | tf_op jit(solution)/shard_map/all_to_all | solution.py:487
  61.4 1.2 %store.1 = (f32[16,400,128]{2,1,0:T(8,128)S(1)}, f32[384,256]{1,0:T(8,128)}, f32[2,384,256]{2,1,0:T(8,128)}) custom-call(f32[32,1,128]{2,1,0:T(1,128)S(1)} %all-to-all-done.3.peak_ref, f32[16,400,128]{2,1,0:T(8,128)S(1)} %flux.7.work_in.work), custom_call_target="tpu_custom_call", output_to_operand_aliasing={{0}: (1, {})} | custom-call | flops 983040 | bytes 2359296 | tf_op jit(solution)/shard_map/store/pallas_call | solution.py:630
  62.7 3.4 %all-to-all-done.4 = f32[8,1,128]{2,1,0:T(1,128)S(1)} async-done(((f32[8,1,128]{2,1,0:T(1,128)}), f32[8,1,128]{2,1,0:T(1,128)S(1)}, u32[]{:S(2)}, u32[]{:S(2)}) %all-to-all-start.4) | async-done | bytes 4128 | tf_op jit(solution)/shard_map/all_to_all | solution.py:487
  (8 shorter events, 1.5 us)
Async XLA Ops:
  2.5 7.0 %collective-permute-start = (f32[10,4,128]{2,1,0:T(4,128)S(1)}, f32[10,4,128]{2,1,0:T(4,128)S(1)}, u32[]{:S(2)}, u32[]{:S(2)}) collective-permute-start(f32[10,4,128]{2,1,0:T(4,128)S(1)} %get-tuple-element.25), channel_id=1, source_target_pairs={{0,8},{8,16},{16,24},{24,0},{1,9},{9,17},{17,25},{25,1},{2,10},{10... | collective-permute-start | bytes 61448 | tf_op jit(solution)/shard_map/ppermute | solution.py:493
  5.6 4.0 %collective-permute-start.1 = (f32[10,4,128]{2,1,0:T(4,128)S(1)}, f32[10,4,128]{2,1,0:T(4,128)S(1)}, u32[]{:S(2)}, u32[]{:S(2)}) collective-permute-start(f32[10,4,128]{2,1,0:T(4,128)S(1)} %get-tuple-element.26), channel_id=1, source_target_pairs={{8,0},{16,8},{24,16},{0,24},{9,1},{17,9},{25,17},{1,25},{10,2},{18... | collective-permute-start | bytes 61448 | tf_op jit(solution)/shard_map/ppermute | solution.py:493
  9.7 6.9 %collective-permute-start.3 = (f32[5,4,512]{2,1,0:T(4,128)S(1)}, f32[5,4,512]{2,1,0:T(4,128)S(1)}, u32[]{:S(2)}, u32[]{:S(2)}) collective-permute-start(f32[5,4,512]{2,1,0:T(4,128)S(1)} %get-tuple-element.28.own_left), channel_id=1, source_target_pairs={{1,0},{2,1},{3,2},{4,3},{5,4},{6,5},{7,6},{0,7},{9,8},{10,9},{11,1... | collective-permute-start | bytes 122888 | tf_op jit(solution)/shard_map/ppermute | solution.py:493
  10.8 5.8 %collective-permute-start.2 = (f32[5,4,512]{2,1,0:T(4,128)S(1)}, f32[5,4,512]{2,1,0:T(4,128)S(1)}, u32[]{:S(2)}, u32[]{:S(2)}) collective-permute-start(f32[5,4,512]{2,1,0:T(4,128)S(1)} %get-tuple-element.29.own_right), channel_id=1, source_target_pairs={{0,1},{1,2},{2,3},{3,4},{4,5},{5,6},{6,7},{7,0},{8,9},{9,10},{10,1... | collective-permute-start | bytes 122888 | tf_op jit(solution)/shard_map/ppermute | solution.py:493
  10.8 12.9 %all-to-all-start = ((f32[32,1,128]{2,1,0:T(1,128)}), f32[32,1,128]{2,1,0:T(1,128)S(1)}, u32[]{:S(2)}, u32[]{:S(2)}) async-start(f32[32,1,128]{2,1,0:T(1,128)} %get-tuple-element.22), calls=%async_computation | async-start | bytes 32768 | tf_op jit(solution)/shard_map/all_to_all | solution.py:487
  24.7 10.3 %all-to-all-start.1 = ((f32[32,1,128]{2,1,0:T(1,128)}), f32[32,1,128]{2,1,0:T(1,128)S(1)}, u32[]{:S(2)}, u32[]{:S(2)}) async-start(f32[32,1,128]{2,1,0:T(1,128)} %get-tuple-element.30), calls=%async_computation.1 | async-start | bytes 32768 | tf_op jit(solution)/shard_map/all_to_all | solution.py:487
  35.9 10.1 %all-to-all-start.2 = ((f32[32,1,128]{2,1,0:T(1,128)}), f32[32,1,128]{2,1,0:T(1,128)S(1)}, u32[]{:S(2)}, u32[]{:S(2)}) async-start(f32[32,1,128]{2,1,0:T(1,128)} %get-tuple-element.32), calls=%async_computation.2 | async-start | bytes 32768 | tf_op jit(solution)/shard_map/all_to_all | solution.py:487
  46.9 10.1 %all-to-all-start.3 = ((f32[32,1,128]{2,1,0:T(1,128)}), f32[32,1,128]{2,1,0:T(1,128)S(1)}, u32[]{:S(2)}, u32[]{:S(2)}) async-start(f32[32,1,128]{2,1,0:T(1,128)} %get-tuple-element.34), calls=%async_computation.3 | async-start | bytes 32768 | tf_op jit(solution)/shard_map/all_to_all | solution.py:487
  58.1 7.9 %all-to-all-start.4 = ((f32[8,1,128]{2,1,0:T(1,128)}), f32[8,1,128]{2,1,0:T(1,128)S(1)}, u32[]{:S(2)}, u32[]{:S(2)}) async-start(f32[8,1,128]{2,1,0:T(1,128)} %last.1), calls=%async_computation.4 | async-start | bytes 8192 | tf_op jit(solution)/shard_map/all_to_all | solution.py:487

commit v6 on v5

--- a/solution.py
+++ b/solution.py
@@ -1,3 +1,5 @@
+import functools
+
 import jax
 import jax.numpy as jnp
 from jax import lax
@@ -16,23 +18,20 @@
 
 VMEM_LIMIT = 20 << 20
 FLUX_UNROLL = 7
+FLUX_COST = ((150, 4), (150, 4), (20, 1))
 
 
 SOURCE, DIFF, FIELDS = 3, 4, 7
 SEND = 5
-STRIP_DIFF = 2 * HALO * SEND
-STRIP_END = STRIP_DIFF + 2 * HALO * 3
+STRIP_DIFF, STRIP_FIELDS = 5, 8
+ALL, MAIN, EDGE = range(3)
 
 
 def tiles_of(work):
-    return (work.shape[0] - 2) // FIELDS
+    return (work.shape[0] - 1) // FIELDS
 
 
 def active_at(work):
-    return work.shape[0] - 2
-
-
-def strip_at(work):
     return work.shape[0] - 1
 
 
@@ -232,40 +231,31 @@
     pl.when(jnp.logical_not(is_bottom))(lambda: received(below_ref, bottom))
     pack[...] = jnp.zeros_like(pack)
     lane = lane_ids(8)
-    pack[0:8, :] = packed(work, slice(0, 8), lane)
-    pack[8:16, :] = packed(work, slice(bottom, bottom + 8), lane)
+    pack[0:8, :] = packed(work, slice(bottom, bottom + 8), lane)
+    pack[LANES - 8 :, :] = packed(work, slice(0, 8), lane)
     split_packed(pack[...].T, left_ref, right_ref, slice(own, own + LANES))
 
 
-def columns_kernel(work_in, own_left, own_right, from_left, from_right, work, both):
-    own = own_left.shape[2] - LANES
-    bottom = TOP + own
+def columns_kernel(own_left, own_right, from_left, from_right, strips):
     is_left = lax.axis_index("tile") == 0
     is_right = lax.axis_index("tile") == lax.axis_size("tile") - 1
 
-    def mirrored(ref, to):
+    def mirrored(ref, side, to):
         for k in range(SEND):
             flip = -1.0 if k == 2 else 1.0
             for j in range(HALO):
-                both[2 * HALO * k + to + HALO - 1 - j, :] = ref[k, j, :] * flip
-
-    def received(ref, to):
+                strips[side, k, to + HALO - 1 - j, :] = ref[k, j, :] * flip
+
+    def received(ref, side, to):
         for k in range(SEND):
-            at = 2 * HALO * k + to
-            both[at : at + HALO, :] = ref[k]
-
-    both[STRIP_DIFF:, :] = jnp.zeros((LANES - STRIP_DIFF, own + LANES), jnp.float32)
-    pl.when(is_left)(lambda: mirrored(own_left, 0))
-    pl.when(jnp.logical_not(is_left))(lambda: received(from_left, 0))
-    pl.when(is_right)(lambda: mirrored(own_right, HALO))
-    pl.when(jnp.logical_not(is_right))(lambda: received(from_right, HALO))
-    strip = strip_at(work)
-    for q in range(own // LANES):
-        at = slice(q * LANES, (q + 1) * LANES)
-        work[strip, TOP + q * LANES : TOP + (q + 1) * LANES, :] = both[:, at].T
-    ends = both[:, own : own + LANES].T
-    work[strip, 0:8, :] = ends[0:8, :]
-    work[strip, bottom : bottom + 8, :] = ends[8:16, :]
+            strips[side, k, to : to + HALO, :] = ref[k]
+
+    received(own_left, 0, HALO)
+    received(own_right, 1, 0)
+    pl.when(is_left)(lambda: mirrored(own_left, 0, 0))
+    pl.when(jnp.logical_not(is_left))(lambda: received(from_left, 0, 0))
+    pl.when(is_right)(lambda: mirrored(own_right, 1, HALO))
+    pl.when(jnp.logical_not(is_right))(lambda: received(from_right, 1, HALO))
 
 
 def roe(left, right):
@@ -298,89 +288,145 @@
     return (depth, normal, tangent, root, sn, st, press, sn * st)
 
 
-def flux_kernel(work_in, work, beside, derived, faces):
+def flip(v):
+    return (v[0], v[2], v[1], v[3], v[5], v[4])
+
+
+def with_roots(depth, along, across):
+    inverse = lax.rsqrt(depth)
+    return [depth, along, across, depth * inverse, along * inverse, across * inverse]
+
+
+def strip_fluxes(strips, ghost_rows):
+    chunks = strips.shape[3] // LANES
+    lane = lane_ids(8)
+    for s in range(2):
+        spans = [slice(q * LANES, (q + 1) * LANES) for q in range(chunks)]
+        now = [with_roots(*[strips[s, k, :, at] for k in range(3)]) for at in spans]
+        rows = []
+        for q in range(chunks):
+            below = [
+                pltpu.roll(jnp.where(lane == 0, b, a), LANES - 1, 1)
+                for a, b in zip(now[q], now[(q + 1) % chunks])
+            ]
+            rows.append(roe(side(*now[q]), side(*below)))
+        for q, at in enumerate(spans):
+            right = [pltpu.roll(v, 7, 0) for v in now[q]]
+            f_depth, f_across, f_along = roe(side(*flip(now[q])), side(*flip(right)))
+            active = strips[s, 3, :, at] > 0.5
+            for f, flux in enumerate((f_depth, f_along, f_across)):
+                above = jnp.where(lane == LANES - 1, rows[q - 1][f], rows[q][f])
+                out = (flux - pltpu.roll(flux, 1, 0)) + (rows[q][f] - pltpu.roll(above, 1, 1))
+                if f == 0:
+                    out = out - 2.0 * strips[s, 4, :, at]
+                strips[s, STRIP_DIFF + f, :, at] = jnp.where(active, out, 0.0)
+                ghost_rows[3 * s + f, at] = flux[HALO - 1, :]
+
+
+def turn_ghosts(ghost_rows, ghost):
+    own = ghost_rows.shape[1] - LANES
+    for q in range(own // LANES):
+        at = slice(q * LANES, (q + 1) * LANES)
+        ghost[TOP + q * LANES : TOP + (q + 1) * LANES, :] = ghost_rows[:, at].T
+    ends = ghost_rows[:, own : own + LANES].T
+    ghost[TOP + own : TOP + own + 8, :] = ends[0:8, :]
+    ghost[0:8, :] = ends[LANES - 8 :, :]
+
+
+def flux_kernel(part, *refs):
+    if part == MAIN:
+        work_in, work, derived, faces = refs
+    elif part == EDGE:
+        work_in, strips_in, work, strips, ghost_rows, ghost = refs
+    else:
+        work_in, strips_in, work, strips, derived, faces, ghost_rows, ghost = refs
     tiles = tiles_of(work)
     padded = work.shape[1]
     row_tiles = padded // 8
-    strip, active_rows = strip_at(work), active_at(work)
+    active_rows = active_at(work)
     lane = lane_ids(8)
-    inside = (lane < HALO) | (lane >= LANES - HALO)
+    first, last = lane == 0, lane == LANES - 1
+    if part != MAIN:
+        strip_fluxes(strips, ghost_rows)
+        turn_ghosts(ghost_rows, ghost)
+
+    def edge_fluxes(at):
+        values = ghost[at, :]
+        return [pltpu.roll(values, LANES - 1 - i, 1) for i in range(6)]
+
+    if part == EDGE:
+
+        def fix(r, carry):
+            at = aligned(r * 8, 8)
+            edges = edge_fluxes(at)
+            active = work[active_rows, at, :] > 0.5
+            for f in range(3):
+                left, right = DIFF * tiles + f * tiles, DIFF * tiles + f * tiles + tiles - 1
+                gone = jnp.where(active & first, pltpu.roll(edges[f], 1, 1), 0.0)
+                work[left, at, :] = work[left, at, :] - gone
+                gone = jnp.where(active & last, edges[3 + f], 0.0)
+                work[right, at, :] = work[right, at, :] + gone
+            return carry
+
+        lax.fori_loop(0, row_tiles, fix, 0, unroll=10)
+        return
 
     def derive(r, carry):
         for i in range(5):
             at = aligned(r * 40 + i * 8, 8)
-            packed_columns = work[strip, at, :]
-            for k in range(SEND):
-                out = pltpu.roll(packed_columns, LANES - HALO - 2 * HALO * k, 1)
-                beside[k, at, :] = jnp.where(inside, out, 1.0) if k == 0 else out
-            for c in range(tiles + 1):
-                state = own_state(c, at)
-                inverse = lax.rsqrt(state[0])
-                derived[c, at, :] = state[0] * inverse
-                derived[tiles + 1 + c, at, :] = state[1] * inverse
-                derived[2 * (tiles + 1) + c, at, :] = state[2] * inverse
+            for c in range(tiles):
+                roots = with_roots(*[work[k * tiles + c, at, :] for k in range(3)])
+                for k in range(3):
+                    derived[k * tiles + c, at, :] = roots[3 + k]
         return carry
 
-    def own_state(c, at):
-        if c == tiles:
-            return [beside[k, at, :] for k in range(3)]
-        return [work[k * tiles + c, at, :] for k in range(3)]
-
-    lax.fori_loop(0, row_tiles // 5, derive, 0, unroll=5)
-    for f in range(3):
-        for c in range(tiles + 1):
-            faces[f * (tiles + 1) + c, 0:8, :] = jnp.zeros((8, LANES), jnp.float32)
+    lax.fori_loop(0, row_tiles // 5, derive, 0, unroll=2)
+    for p in range(3 * tiles):
+        faces[p, 0:8, :] = jnp.zeros((8, LANES), jnp.float32)
 
     def load(c, at):
-        return own_state(c, at) + [derived[k * (tiles + 1) + c, at, :] for k in range(3)]
-
-    def flip(v):
-        return (v[0], v[2], v[1], v[3], v[5], v[4])
-
-    def row_faces(at, wrap):
+        return [ref[k * tiles + c, at, :] for ref in (work, derived) for k in range(3)]
+
+    def fluxes(at, wrap):
         here, below = pl.ds(at, 8), pl.ds(at + 1, 8)
-        now = [load(c, here) for c in range(tiles + 1)]
+        now = [load(c, here) for c in range(tiles)]
         across = []
-        for c in range(tiles + 1):
-            nxt = now[(c + 1) % (tiles + 1)]
+        for c in range(tiles):
             right = [
-                pltpu.roll(jnp.where(lane == 0, b, a), LANES - 1, 1)
-                for a, b in zip(now[c], nxt)
+                pltpu.roll(jnp.where(first, b, a), LANES - 1, 1)
+                for a, b in zip(now[c], now[(c + 1) % tiles])
             ]
             f_depth, f_across, f_along = roe(side(*flip(now[c])), side(*flip(right)))
-            across.append((f_depth, f_along, f_across))
+            across.append([f_depth, f_along, f_across])
             under = [pltpu.roll(v, 7, 0) for v in now[c]] if wrap else load(c, below)
             flux = roe(side(*now[c]), side(*under))
             for f in range(3):
-                faces[f * (tiles + 1) + c, pl.ds(at + 8, 8), :] = flux[f]
-        strip_out = work[strip, here, :]
-        for c in range(tiles + 1):
-            prev = across[(c - 1) % (tiles + 1)]
-            own = c < tiles
-            active = (work[active_rows, here, :] if own else beside[3, here, :]) > 0.5
+                faces[f * tiles + c, pl.ds(at + 8, 8), :] = flux[f]
+        if part == ALL:
+            edges = edge_fluxes(here)
+        else:
+            edges = [jnp.zeros((8, LANES), jnp.float32)] * 6
+        for f in range(3):
+            across[-1][f] = jnp.where(last, edges[3 + f], across[-1][f])
+        active = work[active_rows, here, :] > 0.5
+        for c in range(tiles):
+            prev = across[c - 1] if c else edges
             for f in range(3):
-                left = pltpu.roll(jnp.where(lane == LANES - 1, prev[f], across[c][f]), 1, 1)
-                plane = f * (tiles + 1) + c
+                left = pltpu.roll(jnp.where(last, prev[f], across[c][f]), 1, 1)
+                plane = f * tiles + c
                 out = (across[c][f] - left) + (
                     faces[plane, pl.ds(at + 8, 8), :] - faces[plane, pl.ds(at + 7, 8), :]
                 )
                 if f == 0:
-                    source = work[SOURCE * tiles + c, here, :] if own else beside[4, here, :]
-                    out = out - 2.0 * source
-                out = jnp.where(active, out, 0.0)
-                if own:
-                    work[(DIFF + f) * tiles + c, here, :] = out
-                else:
-                    lo = STRIP_DIFF + 2 * HALO * f
-                    strip_out = jnp.where(lane >= lo, pltpu.roll(out, lo + HALO, 1), strip_out)
-        work[strip, here, :] = strip_out
+                    out = out - 2.0 * work[SOURCE * tiles + c, here, :]
+                work[(DIFF + f) * tiles + c, here, :] = jnp.where(active, out, 0.0)
 
     def one(r, carry):
-        row_faces(pl.multiple_of(r * 8, 8), False)
+        fluxes(pl.multiple_of(r * 8, 8), False)
         return carry
 
     lax.fori_loop(0, row_tiles - 1, one, 0, unroll=FLUX_UNROLL)
-    row_faces(padded - 8, True)
+    fluxes(padded - 8, True)
 
 
 def step_ratio(peak_ref):
@@ -403,10 +449,9 @@
             work[f * tiles + c, at, :] = new
 
 
-def update_kernel(peak_ref, work_in, work, next_hbm, spread, sem):
+def update_kernel(peak_ref, work_in, strips_in, work, strips, next_hbm, spread, sem):
     tiles = tiles_of(work)
     row_tiles = work.shape[1] // 8
-    strip = strip_at(work)
     ratio = step_ratio(peak_ref)
 
     def find(r, acc):
@@ -420,13 +465,14 @@
     spread_peak(lax.fori_loop(0, row_tiles - 2, find, zero, unroll=16), spread)
     copy = pltpu.make_async_copy(spread, next_hbm, sem)
     copy.start()
-    strip_ratio = jnp.where(lane_ids(8) < 2 * HALO * 3, ratio, 0.0)
+    for q in range(strips.shape[3] // LANES):
+        span = slice(q * LANES, (q + 1) * LANES)
+        for k in range(3):
+            for s in range(2):
+                strips[s, k, :, span] -= ratio * strips[s, STRIP_DIFF + k, :, span]
 
     def move(r, carry):
-        at = aligned(r * 8, 8)
-        move_own(work, at, ratio)
-        old = work[strip, at, :]
-        work[strip, at, :] = old - strip_ratio * pltpu.roll(old, LANES - STRIP_DIFF, 1)
+        move_own(work, aligned(r * 8, 8), ratio)
         return carry
 
     lax.fori_loop(0, row_tiles, move, 0, unroll=10)
@@ -504,7 +550,8 @@
     cells = breach_cells.reshape(-1)
     rates = breach_rate.reshape(-1)
     nbytes = 4 * 3 * rows * cols
-    work_out = vmem_out(FIELDS * tiles + 2, padded, LANES)
+    work_out = vmem_out(FIELDS * tiles + 1, padded, LANES)
+    strips_out = vmem_out(2, STRIP_FIELDS, 2 * HALO, rows + LANES)
     strip_out = vmem_out(SEND, HALO, rows + LANES)
     edge_out = vmem_out(SEND * tiles, HALO, LANES)
     peak_out = vmem_out(everyone, 1, LANES)
@@ -569,51 +616,58 @@
     from_right = send(left, "tile", False)
     peaks = exchange(peak, ("region", "tile"))
 
-    work = pl.pallas_call(
+    def flux(part, work, *strips):
+        outs = (work_out, strips_out)[: 1 + len(strips)]
+        main = [
+            pltpu.VMEM((3 * tiles, padded, LANES), f32),
+            pltpu.VMEM((3 * tiles, padded + 8, LANES), f32),
+        ]
+        edge = [pltpu.VMEM((LANES, rows + LANES), f32), pltpu.VMEM((padded, LANES), f32)]
+        flops, moved_bytes = FLUX_COST[part]
+        return pl.pallas_call(
+            functools.partial(flux_kernel, part),
+            out_shape=outs,
+            in_specs=[vmem_spec()] * len(outs),
+            out_specs=(vmem_spec(),) * len(outs),
+            scratch_shapes=(main + edge, main, edge)[part],
+            input_output_aliases={i: i for i in range(len(outs))},
+            compiler_params=params(),
+            cost_estimate=cost(int(flops * rows * cols), int(moved_bytes * nbytes)),
+            name=("flux", "main", "edge")[part],
+        )(work, *strips)
+
+    (work,) = flux(MAIN, work)
+    strips = pl.pallas_call(
         columns_kernel,
-        out_shape=work_out,
-        in_specs=[vmem_spec()] * 5,
+        out_shape=strips_out,
+        in_specs=[vmem_spec()] * 4,
         out_specs=vmem_spec(),
-        scratch_shapes=[
-            pltpu.VMEM((LANES, rows + LANES), f32),
-        ],
-        input_output_aliases={0: 0},
         compiler_params=params(),
-        cost_estimate=cost(10 * rows * cols, nbytes),
+        cost_estimate=cost(rows * cols, nbytes // 8),
         name="columns",
-    )(work, left, right, from_left, from_right)
+    )(left, right, from_left, from_right)
 
     for step in range(STEPS):
-        work = pl.pallas_call(
-            flux_kernel,
-            out_shape=work_out,
-            in_specs=[vmem_spec()],
-            out_specs=vmem_spec(),
-            scratch_shapes=[
-                pltpu.VMEM((SEND, padded, LANES), f32),
-                pltpu.VMEM((3 * (tiles + 1), padded, LANES), f32),
-                pltpu.VMEM((3 * (tiles + 1), padded + 8, LANES), f32),
-            ],
-            input_output_aliases={0: 0},
-            compiler_params=params(),
-            cost_estimate=cost(150 * rows * cols, 4 * nbytes),
-            name="flux",
-        )(work)
+        work, strips = flux(ALL if step else EDGE, work, strips)
         if step < STEPS - 1:
-            work, peak = pl.pallas_call(
+            work, strips, peak = pl.pallas_call(
                 update_kernel,
-                out_shape=(work_out, jax.ShapeDtypeStruct((everyone, 1, LANES), f32)),
-                in_specs=[vmem_spec()] * 2,
-                out_specs=(vmem_spec(), hbm_spec()),
+                out_shape=(
+                    work_out,
+                    strips_out,
+                    jax.ShapeDtypeStruct((everyone, 1, LANES), f32),
+                ),
+                in_specs=[vmem_spec()] * 3,
+                out_specs=(vmem_spec(), vmem_spec(), hbm_spec()),
                 scratch_shapes=[
                     pltpu.VMEM((everyone, 1, LANES), f32),
                     pltpu.SemaphoreType.DMA,
                 ],
-                input_output_aliases={1: 0},
+                input_output_aliases={1: 0, 2: 1},
                 compiler_params=params(),
                 cost_estimate=cost(20 * rows * cols, nbytes),
                 name="update",
-            )(peaks, work)
+            )(peaks, work, strips)
             peaks = exchange(peak, ("region", "tile"))
 
     best = pl.pallas_call(

time: 66.9 us -> 65.7 us (0.982)
  Pallas kernels: 25.6 us -> 22 us
  waiting for transfers between devices: 15.1 us -> 18.7 us
  starting transfers between devices: 24.6 us -> 23.3 us
    pallas_call x8 -> x9, Pallas kernels: 20 us -> 16.4 us  [the longest x5 13.5 us: flux(): pl.pallas_call(functools.partial(flux_kernel, part), out_shape=outs, in_s...]
    all_to_all x5, waiting for transfers between devices: 14.5 us -> 18.1 us  [exchange(): return lax.all_to_all(x, axes, 0, 0)]
    all_to_all x5, starting transfers between devices: 18.3 us -> 17.1 us  [exchange(): return lax.all_to_all(x, axes, 0, 0)]
  transfers between devices with their start and end apart: 9 -> 9, of which waited for: 7 -> 7; matrix products, arithmetic and copies ran while one was open for 0% -> 0% of each run, Pallas kernels for 29% -> 25%
where the time goes in v6:
time: 65.7 us; the launch traced here: 65.4 us
  starting transfers between devices  23.3 us (35%)
  Pallas kernels  22 us (33%)
  waiting for transfers between devices  18.7 us (28%)
  between operations  0.75 us (1%)
    all_to_all x5, waiting for transfers between devices, exchange(): return lax.all_to_all(x, axes, 0, 0)  18.1 us
    all_to_all x5, starting transfers between devices, exchange(): return lax.all_to_all(x, axes, 0, 0)  17.1 us
    pallas_call x5, Pallas kernels, flux(): pl.pallas_call(functools.partial(flux_kernel, part), out_shape=outs, in_s...  13.5 us
    ppermute x4, starting transfers between devices, send(): return lax.ppermute(x, axis, pairs)  6.25 us
    pallas_call x3, Pallas kernels, on_device(): pl.pallas_call(update_kernel, out_shape=(work_out, strips_out, jax.ShapeD...  2.87 us
    pallas_call x1, Pallas kernels, on_device(): pl.pallas_call(start_kernel, out_shape=(work_out, pltpu.VMEM((blocks, 1,...  1.86 us
    pallas_call x1, Pallas kernels, on_device(): pl.pallas_call(pack_kernel, out_shape=(peak_out, strip_out, strip_out), i...  1.33 us
  transfers between devices with their start and end apart: 9, of which 7 were waited for; matrix products, arithmetic and copies ran while one was open for 0% of the time, Pallas kernels for 25%

profile of v6, /device:TPU:0, one launch (start us, length us, event | category | flops | bytes accessed | tf_op | source)
XLA Modules:
  0.0 65.4 jit_solution(2031762466110436320)
XLA Ops:
  0.6 1.9 %start.1 = (f32[15,400,128]{2,1,0:T(8,128)S(1)}, s32[24,1,128]{2,1,0:T(1,128)S(1)}, f32[10,4,128]{2,1,0:T(4,128)S(1)}, f32[10,4,128]{2,1,0:T(4,128)S(1)}) custom-call(s32[24]{0:T(128)} %bitcast.5, s32[24]{0:T(128)} %bitcast.6, s32[64]{0:T(128)} %bitcast.7, f32[64]{0:T(128)} %bitcast.8, f32[384,256]{1,0:T(8,128)} %depth_hbm.1, f32[2,384,256]{2,1,0:T(8,128)} %mom_hbm.1), custom_call_target="tpu_custom_call" | custom-call | flops 196608 | bytes 1179648 | tf_op jit(solution)/shard_map/start/pallas_call | solution.py:559
  2.5 3.1 %collective-permute-start = (f32[10,4,128]{2,1,0:T(4,128)S(1)}, f32[10,4,128]{2,1,0:T(4,128)S(1)}, u32[]{:S(2)}, u32[]{:S(2)}) collective-permute-start(f32[10,4,128]{2,1,0:T(4,128)S(1)} %get-tuple-element.35), channel_id=1, source_target_pairs={{0,8},{8,16},{16,24},{24,0},{1,9},{9,17},{17,25},{25,1},{2,10},{10... | collective-permute-start | bytes 61448 | tf_op jit(solution)/shard_map/ppermute | solution.py:539
  5.6 2.1 %collective-permute-start.1 = (f32[10,4,128]{2,1,0:T(4,128)S(1)}, f32[10,4,128]{2,1,0:T(4,128)S(1)}, u32[]{:S(2)}, u32[]{:S(2)}) collective-permute-start(f32[10,4,128]{2,1,0:T(4,128)S(1)} %get-tuple-element.36), channel_id=1, source_target_pairs={{8,0},{16,8},{24,16},{0,24},{9,1},{17,9},{25,17},{1,25},{10,2},{18... | collective-permute-start | bytes 61448 | tf_op jit(solution)/shard_map/ppermute | solution.py:539
  7.7 1.3 %pack.1 = (f32[32,1,128]{2,1,0:T(1,128)}, f32[5,4,512]{2,1,0:T(4,128)S(1)}, f32[5,4,512]{2,1,0:T(4,128)S(1)}) custom-call(f32[15,400,128]{2,1,0:T(8,128)S(1)} %get-tuple-element.31.work.work_in), custom_call_target="tpu_custom_call" | custom-call | flops 1966080 | bytes 1179648 | tf_op jit(solution)/shard_map/pack/pallas_call | solution.py:592
  9.7 1.1 %collective-permute-start.3 = (f32[5,4,512]{2,1,0:T(4,128)S(1)}, f32[5,4,512]{2,1,0:T(4,128)S(1)}, u32[]{:S(2)}, u32[]{:S(2)}) collective-permute-start(f32[5,4,512]{2,1,0:T(4,128)S(1)} %get-tuple-element.38.own_left), channel_id=1, source_target_pairs={{1,0},{2,1},{3,2},{4,3},{5,4},{6,5},{7,6},{0,7},{9,8},{10,9},{11,1... | collective-permute-start | bytes 122888 | tf_op jit(solution)/shard_map/ppermute | solution.py:539
  10.8 5.8 %all-to-all-start = ((f32[32,1,128]{2,1,0:T(1,128)}), f32[32,1,128]{2,1,0:T(1,128)S(1)}, u32[]{:S(2)}, u32[]{:S(2)}) async-start(f32[32,1,128]{2,1,0:T(1,128)} %get-tuple-element.32), calls=%async_computation | async-start | bytes 32768 | tf_op jit(solution)/shard_map/all_to_all | solution.py:533
  16.6 2.7 %main.1.refs_0_ = f32[15,400,128]{2,1,0:T(8,128)S(1)} custom-call(f32[15,400,128]{2,1,0:T(8,128)S(1)} %get-tuple-element.37.refs_0_), custom_call_target="tpu_custom_call", output_to_operand_aliasing={{}: (0, {})} | custom-call | flops 14745600 | bytes 4718592 | tf_op jit(solution)/shard_map/main/pallas_call | solution.py:627
  19.4 1.3 %edge.1 = (f32[15,400,128]{2,1,0:T(8,128)S(1)}, f32[2,8,8,512]{3,2,1,0:T(8,128)S(1)}) custom-call(f32[15,400,128]{2,1,0:T(8,128)S(1)} %main.1.refs_0_, f32[2,8,8,512]{3,2,1,0:T(8,128)S(1)} %columns.1.refs_1_), custom_call_target="tpu_custom_call", output_to_operand_aliasing={{0}: (0, {}), {1}: (1, {})} | custom-call | flops 1966080 | bytes 1179648 | tf_op jit(solution)/shard_map/edge/pallas_call | solution.py:627
  20.7 3.0 %all-to-all-done.peak_ref = f32[32,1,128]{2,1,0:T(1,128)S(1)} async-done(((f32[32,1,128]{2,1,0:T(1,128)}), f32[32,1,128]{2,1,0:T(1,128)S(1)}, u32[]{:S(2)}, u32[]{:S(2)}) %all-to-all-start) | async-done | bytes 16416 | tf_op jit(solution)/shard_map/all_to_all | solution.py:533
  23.7 1.0 %update.3 = (f32[15,400,128]{2,1,0:T(8,128)S(1)}, f32[2,8,8,512]{3,2,1,0:T(8,128)S(1)}, f32[32,1,128]{2,1,0:T(1,128)}) custom-call(f32[32,1,128]{2,1,0:T(1,128)S(1)} %all-to-all-done.peak_ref, f32[15,400,128]{2,1,0:T(8,128)S(1)} %get-tuple-element.40.work_in, ...), custom_call_target="tpu_custom_call", output_to_operand_aliasing={{0}: (1, {}), {1}: (2, {})} | custom-call | flops 1966080 | bytes 1179648 | tf_op jit(solution)/shard_map/update/pallas_call | solution.py:653
  24.7 2.8 %all-to-all-start.1 = ((f32[32,1,128]{2,1,0:T(1,128)}), f32[32,1,128]{2,1,0:T(1,128)S(1)}, u32[]{:S(2)}, u32[]{:S(2)}) async-start(f32[32,1,128]{2,1,0:T(1,128)} %get-tuple-element.42), calls=%async_computation.1 | async-start | bytes 32768 | tf_op jit(solution)/shard_map/all_to_all | solution.py:533
  27.5 3.2 %flux.3 = (f32[15,400,128]{2,1,0:T(8,128)S(1)}, f32[2,8,8,512]{3,2,1,0:T(8,128)S(1)}) custom-call(f32[15,400,128]{2,1,0:T(8,128)S(1)} %get-tuple-element.43.refs_0_, f32[2,8,8,512]{3,2,1,0:T(8,128)S(1)} %get-tuple-element.44.refs_1_), custom_call_target="tpu_custom_call", output_to_operand_aliasing={{0}: (0, {}), {1}: (1, {})} | custom-call | flops 14745600 | bytes 4718592 | tf_op jit(solution)/shard_map/flux/pallas_call | solution.py:627
  30.7 3.9 %all-to-all-done.1.peak_ref = f32[32,1,128]{2,1,0:T(1,128)S(1)} async-done(((f32[32,1,128]{2,1,0:T(1,128)}), f32[32,1,128]{2,1,0:T(1,128)S(1)}, u32[]{:S(2)}, u32[]{:S(2)}) %all-to-all-start.1) | async-done | bytes 16416 | tf_op jit(solution)/shard_map/all_to_all | solution.py:533
  34.6 1.0 %update.4 = (f32[15,400,128]{2,1,0:T(8,128)S(1)}, f32[2,8,8,512]{3,2,1,0:T(8,128)S(1)}, f32[32,1,128]{2,1,0:T(1,128)}) custom-call(f32[32,1,128]{2,1,0:T(1,128)S(1)} %all-to-all-done.1.peak_ref, f32[15,400,128]{2,1,0:T(8,128)S(1)} %get-tuple-element.45.work_in, ...), custom_call_target="tpu_custom_call", output_to_operand_aliasing={{0}: (1, {}), {1}: (2, {})} | custom-call | flops 1966080 | bytes 1179648 | tf_op jit(solution)/shard_map/update/pallas_call | solution.py:653
  35.6 2.6 %all-to-all-start.2 = ((f32[32,1,128]{2,1,0:T(1,128)}), f32[32,1,128]{2,1,0:T(1,128)S(1)}, u32[]{:S(2)}, u32[]{:S(2)}) async-start(f32[32,1,128]{2,1,0:T(1,128)} %get-tuple-element.47), calls=%async_computation.2 | async-start | bytes 32768 | tf_op jit(solution)/shard_map/all_to_all | solution.py:533
  38.1 3.2 %flux.4 = (f32[15,400,128]{2,1,0:T(8,128)S(1)}, f32[2,8,8,512]{3,2,1,0:T(8,128)S(1)}) custom-call(f32[15,400,128]{2,1,0:T(8,128)S(1)} %get-tuple-element.48.refs_0_, f32[2,8,8,512]{3,2,1,0:T(8,128)S(1)} %get-tuple-element.49.refs_1_), custom_call_target="tpu_custom_call", output_to_operand_aliasing={{0}: (0, {}), {1}: (1, {})} | custom-call | flops 14745600 | bytes 4718592 | tf_op jit(solution)/shard_map/flux/pallas_call | solution.py:627
  41.3 3.9 %all-to-all-done.2.peak_ref = f32[32,1,128]{2,1,0:T(1,128)S(1)} async-done(((f32[32,1,128]{2,1,0:T(1,128)}), f32[32,1,128]{2,1,0:T(1,128)S(1)}, u32[]{:S(2)}, u32[]{:S(2)}) %all-to-all-start.2) | async-done | bytes 16416 | tf_op jit(solution)/shard_map/all_to_all | solution.py:533
  46.2 2.6 %all-to-all-start.3 = ((f32[32,1,128]{2,1,0:T(1,128)}), f32[32,1,128]{2,1,0:T(1,128)S(1)}, u32[]{:S(2)}, u32[]{:S(2)}) async-start(f32[32,1,128]{2,1,0:T(1,128)} %get-tuple-element.52), calls=%async_computation.3 | async-start | bytes 32768 | tf_op jit(solution)/shard_map/all_to_all | solution.py:533
  48.7 3.2 %flux.5 = (f32[15,400,128]{2,1,0:T(8,128)S(1)}, f32[2,8,8,512]{3,2,1,0:T(8,128)S(1)}) custom-call(f32[15,400,128]{2,1,0:T(8,128)S(1)} %get-tuple-element.53.refs_0_, f32[2,8,8,512]{3,2,1,0:T(8,128)S(1)} %get-tuple-element.54.refs_1_), custom_call_target="tpu_custom_call", output_to_operand_aliasing={{0}: (0, {}), {1}: (1, {})} | custom-call | flops 14745600 | bytes 4718592 | tf_op jit(solution)/shard_map/flux/pallas_call | solution.py:627
  51.9 3.9 %all-to-all-done.3.peak_ref = f32[32,1,128]{2,1,0:T(1,128)S(1)} async-done(((f32[32,1,128]{2,1,0:T(1,128)}), f32[32,1,128]{2,1,0:T(1,128)S(1)}, u32[]{:S(2)}, u32[]{:S(2)}) %all-to-all-start.3) | async-done | bytes 16416 | tf_op jit(solution)/shard_map/all_to_all | solution.py:533
  55.8 1.1 %last.1 = f32[8,1,128]{2,1,0:T(1,128)} custom-call(f32[32,1,128]{2,1,0:T(1,128)S(1)} %all-to-all-done.3.peak_ref, s32[24,1,128]{2,1,0:T(1,128)S(1)} %get-tuple-element.58.plan_ref, f32[15,400,128]{2,1,0:T(8,128)S(1)} %get-tuple-element.55.work_in.work), custom_call_target="tpu_custom_call" | custom-call | flops 1966080 | bytes 2359296 | tf_op jit(solution)/shard_map/last/pallas_call | solution.py:673
  56.9 3.3 %all-to-all-start.4 = ((f32[8,1,128]{2,1,0:T(1,128)}), f32[8,1,128]{2,1,0:T(1,128)S(1)}, u32[]{:S(2)}, u32[]{:S(2)}) async-start(f32[8,1,128]{2,1,0:T(1,128)} %last.1), calls=%async_computation.4 | async-start | bytes 8192 | tf_op jit(solution)/shard_map/all_to_all | solution.py:533
  60.2 1.2 %store.1 = (f32[15,400,128]{2,1,0:T(8,128)S(1)}, f32[384,256]{1,0:T(8,128)}, f32[2,384,256]{2,1,0:T(8,128)}) custom-call(f32[32,1,128]{2,1,0:T(1,128)S(1)} %all-to-all-done.3.peak_ref, f32[15,400,128]{2,1,0:T(8,128)S(1)} %get-tuple-element.55.work_in.work), custom_call_target="tpu_custom_call", output_to_operand_aliasing={{0}: (1, {})} | custom-call | flops 983040 | bytes 2359296 | tf_op jit(solution)/shard_map/store/pallas_call | solution.py:684
  61.4 3.4 %all-to-all-done.4 = f32[8,1,128]{2,1,0:T(1,128)S(1)} async-done(((f32[8,1,128]{2,1,0:T(1,128)}), f32[8,1,128]{2,1,0:T(1,128)S(1)}, u32[]{:S(2)}, u32[]{:S(2)}) %all-to-all-start.4) | async-done | bytes 4128 | tf_op jit(solution)/shard_map/all_to_all | solution.py:533
  (9 shorter events, 2.3 us)
Async XLA Ops:
  2.5 7.0 %collective-permute-start = (f32[10,4,128]{2,1,0:T(4,128)S(1)}, f32[10,4,128]{2,1,0:T(4,128)S(1)}, u32[]{:S(2)}, u32[]{:S(2)}) collective-permute-start(f32[10,4,128]{2,1,0:T(4,128)S(1)} %get-tuple-element.35), channel_id=1, source_target_pairs={{0,8},{8,16},{16,24},{24,0},{1,9},{9,17},{17,25},{25,1},{2,10},{10... | collective-permute-start | bytes 61448 | tf_op jit(solution)/shard_map/ppermute | solution.py:539
  5.6 4.0 %collective-permute-start.1 = (f32[10,4,128]{2,1,0:T(4,128)S(1)}, f32[10,4,128]{2,1,0:T(4,128)S(1)}, u32[]{:S(2)}, u32[]{:S(2)}) collective-permute-start(f32[10,4,128]{2,1,0:T(4,128)S(1)} %get-tuple-element.36), channel_id=1, source_target_pairs={{8,0},{16,8},{24,16},{0,24},{9,1},{17,9},{25,17},{1,25},{10,2},{18... | collective-permute-start | bytes 61448 | tf_op jit(solution)/shard_map/ppermute | solution.py:539
  9.7 9.6 %collective-permute-start.3 = (f32[5,4,512]{2,1,0:T(4,128)S(1)}, f32[5,4,512]{2,1,0:T(4,128)S(1)}, u32[]{:S(2)}, u32[]{:S(2)}) collective-permute-start(f32[5,4,512]{2,1,0:T(4,128)S(1)} %get-tuple-element.38.own_left), channel_id=1, source_target_pairs={{1,0},{2,1},{3,2},{4,3},{5,4},{6,5},{7,6},{0,7},{9,8},{10,9},{11,1... | collective-permute-start | bytes 122888 | tf_op jit(solution)/shard_map/ppermute | solution.py:539
  10.8 8.6 %collective-permute-start.2 = (f32[5,4,512]{2,1,0:T(4,128)S(1)}, f32[5,4,512]{2,1,0:T(4,128)S(1)}, u32[]{:S(2)}, u32[]{:S(2)}) collective-permute-start(f32[5,4,512]{2,1,0:T(4,128)S(1)} %get-tuple-element.39.own_right), channel_id=1, source_target_pairs={{0,1},{1,2},{2,3},{3,4},{4,5},{5,6},{6,7},{7,0},{8,9},{9,10},{10,1... | collective-permute-start | bytes 122888 | tf_op jit(solution)/shard_map/ppermute | solution.py:539
  10.8 12.9 %all-to-all-start = ((f32[32,1,128]{2,1,0:T(1,128)}), f32[32,1,128]{2,1,0:T(1,128)S(1)}, u32[]{:S(2)}, u32[]{:S(2)}) async-start(f32[32,1,128]{2,1,0:T(1,128)} %get-tuple-element.32), calls=%async_computation | async-start | bytes 32768 | tf_op jit(solution)/shard_map/all_to_all | solution.py:533
  24.7 9.9 %all-to-all-start.1 = ((f32[32,1,128]{2,1,0:T(1,128)}), f32[32,1,128]{2,1,0:T(1,128)S(1)}, u32[]{:S(2)}, u32[]{:S(2)}) async-start(f32[32,1,128]{2,1,0:T(1,128)} %get-tuple-element.42), calls=%async_computation.1 | async-start | bytes 32768 | tf_op jit(solution)/shard_map/all_to_all | solution.py:533
  35.6 9.6 %all-to-all-start.2 = ((f32[32,1,128]{2,1,0:T(1,128)}), f32[32,1,128]{2,1,0:T(1,128)S(1)}, u32[]{:S(2)}, u32[]{:S(2)}) async-start(f32[32,1,128]{2,1,0:T(1,128)} %get-tuple-element.47), calls=%async_computation.2 | async-start | bytes 32768 | tf_op jit(solution)/shard_map/all_to_all | solution.py:533
  46.2 9.6 %all-to-all-start.3 = ((f32[32,1,128]{2,1,0:T(1,128)}), f32[32,1,128]{2,1,0:T(1,128)S(1)}, u32[]{:S(2)}, u32[]{:S(2)}) async-start(f32[32,1,128]{2,1,0:T(1,128)} %get-tuple-element.52), calls=%async_computation.3 | async-start | bytes 32768 | tf_op jit(solution)/shard_map/all_to_all | solution.py:533
  56.9 7.9 %all-to-all-start.4 = ((f32[8,1,128]{2,1,0:T(1,128)}), f32[8,1,128]{2,1,0:T(1,128)S(1)}, u32[]{:S(2)}, u32[]{:S(2)}) async-start(f32[8,1,128]{2,1,0:T(1,128)} %last.1), calls=%async_computation.4 | async-start | bytes 8192 | tf_op jit(solution)/shard_map/all_to_all | solution.py:533

commit v7 on v6

--- a/solution.py
+++ b/solution.py
@@ -18,7 +18,8 @@
 
 VMEM_LIMIT = 20 << 20
 FLUX_UNROLL = 7
-FLUX_COST = ((150, 4), (150, 4), (20, 1))
+FIRST = 2
+FLUX_COST = ((150, 4), (150, 4), (500, 20))
 
 
 SOURCE, DIFF, FIELDS = 3, 4, 7
@@ -182,25 +183,33 @@
         left_ref[k, :, at] = turned[lo + HALO : lo + 2 * HALO, :]
 
 
-def pack_kernel(work, peak_ref, left_ref, right_ref, pack):
+def pack_kernel(work, peak_hbm, left_ref, right_ref, pack, spread, sem):
     tiles = tiles_of(work)
     rows = pack.shape[0]
     lane = lane_ids(8)
 
-    def one(r, acc):
+    def find(r, acc):
         at = aligned(r * 8 + TOP, 8)
-        pack[aligned(r * 8, 8), :] = packed(work, at, lane)
         active = work[active_at(work), at, :] > 0.5
         for c in range(tiles):
             speed = speed_of(*[work[k * tiles + c, at, :] for k in range(3)])
             acc = jnp.maximum(acc, jnp.where(active, speed, 0.0))
         return acc
 
-    acc = lax.fori_loop(0, rows // 8, one, jnp.zeros((8, LANES), jnp.float32), unroll=8)
-    spread_peak(acc, peak_ref)
+    zero = jnp.zeros((8, LANES), jnp.float32)
+    spread_peak(lax.fori_loop(0, rows // 8, find, zero, unroll=16), spread)
+    copy = pltpu.make_async_copy(spread, peak_hbm, sem)
+    copy.start()
+
+    def one(r, carry):
+        pack[aligned(r * 8, 8), :] = packed(work, aligned(r * 8 + TOP, 8), lane)
+        return carry
+
+    lax.fori_loop(0, rows // 8, one, 0, unroll=8)
     for q in range(rows // LANES):
         at = slice(q * LANES, (q + 1) * LANES)
         split_packed(pack[at, :].T, left_ref, right_ref, at)
+    copy.wait()
 
 
 def rows_kernel(
@@ -320,7 +329,7 @@
                 if f == 0:
                     out = out - 2.0 * strips[s, 4, :, at]
                 strips[s, STRIP_DIFF + f, :, at] = jnp.where(active, out, 0.0)
-                ghost_rows[3 * s + f, at] = flux[HALO - 1, :]
+                ghost_rows[(2 * f - s) % LANES, at] = flux[HALO - 1, :]
 
 
 def turn_ghosts(ghost_rows, ghost):
@@ -352,7 +361,7 @@
 
     def edge_fluxes(at):
         values = ghost[at, :]
-        return [pltpu.roll(values, LANES - 1 - i, 1) for i in range(6)]
+        return [values] + [pltpu.roll(values, LANES - 2 * f, 1) for f in (1, 2)]
 
     if part == EDGE:
 
@@ -362,10 +371,8 @@
             active = work[active_rows, at, :] > 0.5
             for f in range(3):
                 left, right = DIFF * tiles + f * tiles, DIFF * tiles + f * tiles + tiles - 1
-                gone = jnp.where(active & first, pltpu.roll(edges[f], 1, 1), 0.0)
-                work[left, at, :] = work[left, at, :] - gone
-                gone = jnp.where(active & last, edges[3 + f], 0.0)
-                work[right, at, :] = work[right, at, :] + gone
+                work[left, at, :] -= jnp.where(active & first, edges[f], 0.0)
+                work[right, at, :] += jnp.where(active & last, edges[f], 0.0)
             return carry
 
         lax.fori_loop(0, row_tiles, fix, 0, unroll=10)
@@ -405,14 +412,16 @@
         if part == ALL:
             edges = edge_fluxes(here)
         else:
-            edges = [jnp.zeros((8, LANES), jnp.float32)] * 6
+            edges = [jnp.zeros((8, LANES), jnp.float32)] * 3
         for f in range(3):
-            across[-1][f] = jnp.where(last, edges[3 + f], across[-1][f])
+            across[-1][f] = jnp.where(last, edges[f], across[-1][f])
         active = work[active_rows, here, :] > 0.5
         for c in range(tiles):
-            prev = across[c - 1] if c else edges
             for f in range(3):
-                left = pltpu.roll(jnp.where(last, prev[f], across[c][f]), 1, 1)
+                if c:
+                    left = pltpu.roll(jnp.where(last, across[c - 1][f], across[c][f]), 1, 1)
+                else:
+                    left = jnp.where(first, edges[f], pltpu.roll(across[c][f], 1, 1))
                 plane = f * tiles + c
                 out = (across[c][f] - left) + (
                     faces[plane, pl.ds(at + 8, 8), :] - faces[plane, pl.ds(at + 7, 8), :]
@@ -554,7 +563,8 @@
     strips_out = vmem_out(2, STRIP_FIELDS, 2 * HALO, rows + LANES)
     strip_out = vmem_out(SEND, HALO, rows + LANES)
     edge_out = vmem_out(SEND * tiles, HALO, LANES)
-    peak_out = vmem_out(everyone, 1, LANES)
+    peak_out = jax.ShapeDtypeStruct((everyone, 1, LANES), f32)
+    first_out = jax.ShapeDtypeStruct((everyone, FIRST, LANES), f32)
 
     work, plan, up, down = pl.pallas_call(
         start_kernel,
@@ -591,10 +601,14 @@
 
     peak, left, right = pl.pallas_call(
         pack_kernel,
-        out_shape=(peak_out, strip_out, strip_out),
+        out_shape=(first_out, strip_out, strip_out),
         in_specs=[vmem_spec()],
-        out_specs=(vmem_spec(),) * 3,
-        scratch_shapes=[pltpu.VMEM((rows, LANES), f32)],
+        out_specs=(hbm_spec(), vmem_spec(), vmem_spec()),
+        scratch_shapes=[
+            pltpu.VMEM((rows, LANES), f32),
+            pltpu.VMEM(first_out.shape, f32),
+            pltpu.SemaphoreType.DMA,
+        ],
         compiler_params=params(),
         cost_estimate=cost(20 * rows * cols, nbytes),
         name="pack",
@@ -655,7 +669,7 @@
                 out_shape=(
                     work_out,
                     strips_out,
-                    jax.ShapeDtypeStruct((everyone, 1, LANES), f32),
+                    peak_out,
                 ),
                 in_specs=[vmem_spec()] * 3,
                 out_specs=(vmem_spec(), vmem_spec(), hbm_spec()),

time: 65.7 us -> 64 us (0.974)
  waiting for transfers between devices: 18.7 us -> 17.3 us
  Pallas kernels: 22 us -> 20.7 us
  starting transfers between devices: 23.3 us -> 24.4 us
    all_to_all x5, waiting for transfers between devices: 18.1 us -> 15.6 us  [exchange(): return lax.all_to_all(x, axes, 0, 0)]
    ppermute x4, starting transfers between devices: 6.25 us -> 7.64 us  [send(): return lax.ppermute(x, axis, pairs)]
    ppermute x4, waiting for transfers between devices: 0.59 us -> 1.71 us  [send(): return lax.ppermute(x, axis, pairs)]
    pallas_call x5, Pallas kernels: 13.5 us -> 12.4 us  [flux(): pl.pallas_call(functools.partial(flux_kernel, part), out_shape=outs, in_s...]
  transfers between devices with their start and end apart: 9 -> 9, of which waited for: 7 -> 5; matrix products, arithmetic and copies ran while one was open for 0% -> 0% of each run, Pallas kernels for 25% -> 23%
where the time goes in v7:
time: 64 us; the launch traced here: 63.7 us
  starting transfers between devices  24.4 us (38%)
  Pallas kernels  20.7 us (32%)
  waiting for transfers between devices  17.3 us (27%)
  between operations  0.78 us (1%)
    all_to_all x5, starting transfers between devices, exchange(): return lax.all_to_all(x, axes, 0, 0)  16.7 us
    all_to_all x5, waiting for transfers between devices, exchange(): return lax.all_to_all(x, axes, 0, 0)  15.6 us
    pallas_call x5, Pallas kernels, flux(): pl.pallas_call(functools.partial(flux_kernel, part), out_shape=outs, in_s...  12.4 us
    ppermute x4, starting transfers between devices, send(): return lax.ppermute(x, axis, pairs)  7.64 us
    pallas_call x3, Pallas kernels, on_device(): pl.pallas_call(update_kernel, out_shape=(work_out, strips_out, peak_out),...  2.88 us
    pallas_call x1, Pallas kernels, on_device(): pl.pallas_call(start_kernel, out_shape=(work_out, pltpu.VMEM((blocks, 1,...  1.86 us
    ppermute x4, waiting for transfers between devices, send(): return lax.ppermute(x, axis, pairs)  1.71 us
  transfers between devices with their start and end apart: 9, of which 5 were waited for; matrix products, arithmetic and copies ran while one was open for 0% of the time, Pallas kernels for 23%

profile of v7, /device:TPU:0, one launch (start us, length us, event | category | flops | bytes accessed | tf_op | source)
XLA Modules:
  0.0 63.7 jit_solution(2401778504223626818)
XLA Ops:
  0.6 1.9 %start.1 = (f32[15,400,128]{2,1,0:T(8,128)S(1)}, s32[24,1,128]{2,1,0:T(1,128)S(1)}, f32[10,4,128]{2,1,0:T(4,128)S(1)}, f32[10,4,128]{2,1,0:T(4,128)S(1)}) custom-call(s32[24]{0:T(128)} %bitcast.5, s32[24]{0:T(128)} %bitcast.6, s32[64]{0:T(128)} %bitcast.7, f32[64]{0:T(128)} %bitcast.8, f32[384,256]{1,0:T(8,128)} %depth_hbm.1, f32[2,384,256]{2,1,0:T(8,128)} %mom_hbm.1), custom_call_target="tpu_custom_call" | custom-call | flops 196608 | bytes 1179648 | tf_op jit(solution)/shard_map/start/pallas_call | solution.py:569
  2.5 3.1 %collective-permute-start = (f32[10,4,128]{2,1,0:T(4,128)S(1)}, f32[10,4,128]{2,1,0:T(4,128)S(1)}, u32[]{:S(2)}, u32[]{:S(2)}) collective-permute-start(f32[10,4,128]{2,1,0:T(4,128)S(1)} %get-tuple-element.35), channel_id=1, source_target_pairs={{0,8},{8,16},{16,24},{24,0},{1,9},{9,17},{17,25},{25,1},{2,10},{10... | collective-permute-start | bytes 61448 | tf_op jit(solution)/shard_map/ppermute | solution.py:548
  5.6 2.1 %collective-permute-start.1 = (f32[10,4,128]{2,1,0:T(4,128)S(1)}, f32[10,4,128]{2,1,0:T(4,128)S(1)}, u32[]{:S(2)}, u32[]{:S(2)}) collective-permute-start(f32[10,4,128]{2,1,0:T(4,128)S(1)} %get-tuple-element.36), channel_id=1, source_target_pairs={{8,0},{16,8},{24,16},{0,24},{9,1},{17,9},{25,17},{1,25},{10,2},{18... | collective-permute-start | bytes 61448 | tf_op jit(solution)/shard_map/ppermute | solution.py:548
  7.7 1.0 %pack.1 = (f32[32,2,128]{2,1,0:T(2,128)}, f32[5,4,512]{2,1,0:T(4,128)S(1)}, f32[5,4,512]{2,1,0:T(4,128)S(1)}) custom-call(f32[15,400,128]{2,1,0:T(8,128)S(1)} %get-tuple-element.31.work.work_in), custom_call_target="tpu_custom_call" | custom-call | flops 1966080 | bytes 1179648 | tf_op jit(solution)/shard_map/pack/pallas_call | solution.py:602
  8.7 4.2 %all-to-all-start = ((f32[32,2,128]{2,1,0:T(2,128)}), f32[32,2,128]{2,1,0:T(2,128)S(1)}, u32[]{:S(2)}, u32[]{:S(2)}) async-start(f32[32,2,128]{2,1,0:T(2,128)} %get-tuple-element.32), calls=%async_computation | async-start | bytes 65536 | tf_op jit(solution)/shard_map/all_to_all | solution.py:542
  13.1 2.5 %collective-permute-start.3 = (f32[5,4,512]{2,1,0:T(4,128)S(1)}, f32[5,4,512]{2,1,0:T(4,128)S(1)}, u32[]{:S(2)}, u32[]{:S(2)}) collective-permute-start(f32[5,4,512]{2,1,0:T(4,128)S(1)} %get-tuple-element.38.own_left), channel_id=1, source_target_pairs={{1,0},{2,1},{3,2},{4,3},{5,4},{6,5},{7,6},{0,7},{9,8},{10,9},{11,1... | collective-permute-start | bytes 122888 | tf_op jit(solution)/shard_map/ppermute | solution.py:548
  15.6 2.7 %main.1.refs_0_ = f32[15,400,128]{2,1,0:T(8,128)S(1)} custom-call(f32[15,400,128]{2,1,0:T(8,128)S(1)} %get-tuple-element.37.refs_0_), custom_call_target="tpu_custom_call", output_to_operand_aliasing={{}: (0, {})} | custom-call | flops 14745600 | bytes 4718592 | tf_op jit(solution)/shard_map/main/pallas_call | solution.py:641
  18.3 1.7 %collective-permute-done.2.from_left = f32[5,4,512]{2,1,0:T(4,128)S(1)} collective-permute-done((f32[5,4,512]{2,1,0:T(4,128)S(1)}, f32[5,4,512]{2,1,0:T(4,128)S(1)}, u32[]{:S(2)}, u32[]{:S(2)}) %collective-permute-start.2) | collective-permute-done | bytes 40992 | tf_op jit(solution)/shard_map/ppermute | solution.py:548
  20.8 1.0 %update.3 = (f32[15,400,128]{2,1,0:T(8,128)S(1)}, f32[2,8,8,512]{3,2,1,0:T(8,128)S(1)}, f32[32,1,128]{2,1,0:T(1,128)}) custom-call(f32[32,2,128]{2,1,0:T(2,128)S(1)} %all-to-all-done.peak_ref, f32[15,400,128]{2,1,0:T(8,128)S(1)} %get-tuple-element.40.work_in, ...), custom_call_target="tpu_custom_call", output_to_operand_aliasing={{0}: (1, {}), {1}: (2, {})} | custom-call | flops 1966080 | bytes 1179648 | tf_op jit(solution)/shard_map/update/pallas_call | solution.py:667
  21.8 4.1 %all-to-all-start.1 = ((f32[32,1,128]{2,1,0:T(1,128)}), f32[32,1,128]{2,1,0:T(1,128)S(1)}, u32[]{:S(2)}, u32[]{:S(2)}) async-start(f32[32,1,128]{2,1,0:T(1,128)} %get-tuple-element.42), calls=%async_computation.1 | async-start | bytes 32768 | tf_op jit(solution)/shard_map/all_to_all | solution.py:542
  25.9 3.0 %flux.3 = (f32[15,400,128]{2,1,0:T(8,128)S(1)}, f32[2,8,8,512]{3,2,1,0:T(8,128)S(1)}) custom-call(f32[15,400,128]{2,1,0:T(8,128)S(1)} %get-tuple-element.43.refs_0_, f32[2,8,8,512]{3,2,1,0:T(8,128)S(1)} %get-tuple-element.44.refs_1_), custom_call_target="tpu_custom_call", output_to_operand_aliasing={{0}: (0, {}), {1}: (1, {})} | custom-call | flops 14745600 | bytes 4718592 | tf_op jit(solution)/shard_map/flux/pallas_call | solution.py:641
  28.9 4.1 %all-to-all-done.1.peak_ref = f32[32,1,128]{2,1,0:T(1,128)S(1)} async-done(((f32[32,1,128]{2,1,0:T(1,128)}), f32[32,1,128]{2,1,0:T(1,128)S(1)}, u32[]{:S(2)}, u32[]{:S(2)}) %all-to-all-start.1) | async-done | bytes 16416 | tf_op jit(solution)/shard_map/all_to_all | solution.py:542
  33.0 1.0 %update.4 = (f32[15,400,128]{2,1,0:T(8,128)S(1)}, f32[2,8,8,512]{3,2,1,0:T(8,128)S(1)}, f32[32,1,128]{2,1,0:T(1,128)}) custom-call(f32[32,1,128]{2,1,0:T(1,128)S(1)} %all-to-all-done.1.peak_ref, f32[15,400,128]{2,1,0:T(8,128)S(1)} %get-tuple-element.45.work_in, ...), custom_call_target="tpu_custom_call", output_to_operand_aliasing={{0}: (1, {}), {1}: (2, {})} | custom-call | flops 1966080 | bytes 1179648 | tf_op jit(solution)/shard_map/update/pallas_call | solution.py:667
  33.9 2.6 %all-to-all-start.2 = ((f32[32,1,128]{2,1,0:T(1,128)}), f32[32,1,128]{2,1,0:T(1,128)S(1)}, u32[]{:S(2)}, u32[]{:S(2)}) async-start(f32[32,1,128]{2,1,0:T(1,128)} %get-tuple-element.47), calls=%async_computation.2 | async-start | bytes 32768 | tf_op jit(solution)/shard_map/all_to_all | solution.py:542
  36.5 3.0 %flux.4 = (f32[15,400,128]{2,1,0:T(8,128)S(1)}, f32[2,8,8,512]{3,2,1,0:T(8,128)S(1)}) custom-call(f32[15,400,128]{2,1,0:T(8,128)S(1)} %get-tuple-element.48.refs_0_, f32[2,8,8,512]{3,2,1,0:T(8,128)S(1)} %get-tuple-element.49.refs_1_), custom_call_target="tpu_custom_call", output_to_operand_aliasing={{0}: (0, {}), {1}: (1, {})} | custom-call | flops 14745600 | bytes 4718592 | tf_op jit(solution)/shard_map/flux/pallas_call | solution.py:641
  39.5 4.1 %all-to-all-done.2.peak_ref = f32[32,1,128]{2,1,0:T(1,128)S(1)} async-done(((f32[32,1,128]{2,1,0:T(1,128)}), f32[32,1,128]{2,1,0:T(1,128)S(1)}, u32[]{:S(2)}, u32[]{:S(2)}) %all-to-all-start.2) | async-done | bytes 16416 | tf_op jit(solution)/shard_map/all_to_all | solution.py:542
  43.6 1.0 %update.5 = (f32[15,400,128]{2,1,0:T(8,128)S(1)}, f32[2,8,8,512]{3,2,1,0:T(8,128)S(1)}, f32[32,1,128]{2,1,0:T(1,128)}) custom-call(f32[32,1,128]{2,1,0:T(1,128)S(1)} %all-to-all-done.2.peak_ref, f32[15,400,128]{2,1,0:T(8,128)S(1)} %get-tuple-element.50.work_in, ...), custom_call_target="tpu_custom_call", output_to_operand_aliasing={{0}: (1, {}), {1}: (2, {})} | custom-call | flops 1966080 | bytes 1179648 | tf_op jit(solution)/shard_map/update/pallas_call | solution.py:667
  44.5 2.6 %all-to-all-start.3 = ((f32[32,1,128]{2,1,0:T(1,128)}), f32[32,1,128]{2,1,0:T(1,128)S(1)}, u32[]{:S(2)}, u32[]{:S(2)}) async-start(f32[32,1,128]{2,1,0:T(1,128)} %get-tuple-element.52), calls=%async_computation.3 | async-start | bytes 32768 | tf_op jit(solution)/shard_map/all_to_all | solution.py:542
  47.1 3.0 %flux.5 = (f32[15,400,128]{2,1,0:T(8,128)S(1)}, f32[2,8,8,512]{3,2,1,0:T(8,128)S(1)}) custom-call(f32[15,400,128]{2,1,0:T(8,128)S(1)} %get-tuple-element.53.refs_0_, f32[2,8,8,512]{3,2,1,0:T(8,128)S(1)} %get-tuple-element.54.refs_1_), custom_call_target="tpu_custom_call", output_to_operand_aliasing={{0}: (0, {}), {1}: (1, {})} | custom-call | flops 14745600 | bytes 4718592 | tf_op jit(solution)/shard_map/flux/pallas_call | solution.py:641
  50.1 4.1 %all-to-all-done.3.peak_ref = f32[32,1,128]{2,1,0:T(1,128)S(1)} async-done(((f32[32,1,128]{2,1,0:T(1,128)}), f32[32,1,128]{2,1,0:T(1,128)S(1)}, u32[]{:S(2)}, u32[]{:S(2)}) %all-to-all-start.3) | async-done | bytes 16416 | tf_op jit(solution)/shard_map/all_to_all | solution.py:542
  54.2 1.1 %last.1 = f32[8,1,128]{2,1,0:T(1,128)} custom-call(f32[32,1,128]{2,1,0:T(1,128)S(1)} %all-to-all-done.3.peak_ref, s32[24,1,128]{2,1,0:T(1,128)S(1)} %get-tuple-element.58.plan_ref, f32[15,400,128]{2,1,0:T(8,128)S(1)} %get-tuple-element.55.work_in.work), custom_call_target="tpu_custom_call" | custom-call | flops 1966080 | bytes 2359296 | tf_op jit(solution)/shard_map/last/pallas_call | solution.py:687
  55.3 3.3 %all-to-all-start.4 = ((f32[8,1,128]{2,1,0:T(1,128)}), f32[8,1,128]{2,1,0:T(1,128)S(1)}, u32[]{:S(2)}, u32[]{:S(2)}) async-start(f32[8,1,128]{2,1,0:T(1,128)} %last.1), calls=%async_computation.4 | async-start | bytes 8192 | tf_op jit(solution)/shard_map/all_to_all | solution.py:542
  58.6 1.2 %store.1 = (f32[15,400,128]{2,1,0:T(8,128)S(1)}, f32[384,256]{1,0:T(8,128)}, f32[2,384,256]{2,1,0:T(8,128)}) custom-call(f32[32,1,128]{2,1,0:T(1,128)S(1)} %all-to-all-done.3.peak_ref, f32[15,400,128]{2,1,0:T(8,128)S(1)} %get-tuple-element.55.work_in.work), custom_call_target="tpu_custom_call", output_to_operand_aliasing={{0}: (1, {})} | custom-call | flops 983040 | bytes 2359296 | tf_op jit(solution)/shard_map/store/pallas_call | solution.py:698
  59.8 3.4 %all-to-all-done.4 = f32[8,1,128]{2,1,0:T(1,128)S(1)} async-done(((f32[8,1,128]{2,1,0:T(1,128)}), f32[8,1,128]{2,1,0:T(1,128)S(1)}, u32[]{:S(2)}, u32[]{:S(2)}) %all-to-all-start.4) | async-done | bytes 4128 | tf_op jit(solution)/shard_map/all_to_all | solution.py:542
  (9 shorter events, 1.6 us)
Async XLA Ops:
  2.5 10.4 %collective-permute-start = (f32[10,4,128]{2,1,0:T(4,128)S(1)}, f32[10,4,128]{2,1,0:T(4,128)S(1)}, u32[]{:S(2)}, u32[]{:S(2)}) collective-permute-start(f32[10,4,128]{2,1,0:T(4,128)S(1)} %get-tuple-element.35), channel_id=1, source_target_pairs={{0,8},{8,16},{16,24},{24,0},{1,9},{9,17},{17,25},{25,1},{2,10},{10... | collective-permute-start | bytes 61448 | tf_op jit(solution)/shard_map/ppermute | solution.py:548
  5.6 7.4 %collective-permute-start.1 = (f32[10,4,128]{2,1,0:T(4,128)S(1)}, f32[10,4,128]{2,1,0:T(4,128)S(1)}, u32[]{:S(2)}, u32[]{:S(2)}) collective-permute-start(f32[10,4,128]{2,1,0:T(4,128)S(1)} %get-tuple-element.36), channel_id=1, source_target_pairs={{8,0},{16,8},{24,16},{0,24},{9,1},{17,9},{25,17},{1,25},{10,2},{18... | collective-permute-start | bytes 61448 | tf_op jit(solution)/shard_map/ppermute | solution.py:548
  8.7 12.1 %all-to-all-start = ((f32[32,2,128]{2,1,0:T(2,128)}), f32[32,2,128]{2,1,0:T(2,128)S(1)}, u32[]{:S(2)}, u32[]{:S(2)}) async-start(f32[32,2,128]{2,1,0:T(2,128)} %get-tuple-element.32), calls=%async_computation | async-start | bytes 65536 | tf_op jit(solution)/shard_map/all_to_all | solution.py:542
  13.1 5.1 %collective-permute-start.3 = (f32[5,4,512]{2,1,0:T(4,128)S(1)}, f32[5,4,512]{2,1,0:T(4,128)S(1)}, u32[]{:S(2)}, u32[]{:S(2)}) collective-permute-start(f32[5,4,512]{2,1,0:T(4,128)S(1)} %get-tuple-element.38.own_left), channel_id=1, source_target_pairs={{1,0},{2,1},{3,2},{4,3},{5,4},{6,5},{7,6},{0,7},{9,8},{10,9},{11,1... | collective-permute-start | bytes 122888 | tf_op jit(solution)/shard_map/ppermute | solution.py:548
  15.6 4.4 %collective-permute-start.2 = (f32[5,4,512]{2,1,0:T(4,128)S(1)}, f32[5,4,512]{2,1,0:T(4,128)S(1)}, u32[]{:S(2)}, u32[]{:S(2)}) collective-permute-start(f32[5,4,512]{2,1,0:T(4,128)S(1)} %get-tuple-element.39.own_right), channel_id=1, source_target_pairs={{0,1},{1,2},{2,3},{3,4},{4,5},{5,6},{6,7},{7,0},{8,9},{9,10},{10,1... | collective-permute-start | bytes 122888 | tf_op jit(solution)/shard_map/ppermute | solution.py:548
  21.8 11.2 %all-to-all-start.1 = ((f32[32,1,128]{2,1,0:T(1,128)}), f32[32,1,128]{2,1,0:T(1,128)S(1)}, u32[]{:S(2)}, u32[]{:S(2)}) async-start(f32[32,1,128]{2,1,0:T(1,128)} %get-tuple-element.42), calls=%async_computation.1 | async-start | bytes 32768 | tf_op jit(solution)/shard_map/all_to_all | solution.py:542
  33.9 9.6 %all-to-all-start.2 = ((f32[32,1,128]{2,1,0:T(1,128)}), f32[32,1,128]{2,1,0:T(1,128)S(1)}, u32[]{:S(2)}, u32[]{:S(2)}) async-start(f32[32,1,128]{2,1,0:T(1,128)} %get-tuple-element.47), calls=%async_computation.2 | async-start | bytes 32768 | tf_op jit(solution)/shard_map/all_to_all | solution.py:542
  44.5 9.6 %all-to-all-start.3 = ((f32[32,1,128]{2,1,0:T(1,128)}), f32[32,1,128]{2,1,0:T(1,128)S(1)}, u32[]{:S(2)}, u32[]{:S(2)}) async-start(f32[32,1,128]{2,1,0:T(1,128)} %get-tuple-element.52), calls=%async_computation.3 | async-start | bytes 32768 | tf_op jit(solution)/shard_map/all_to_all | solution.py:542
  55.3 7.9 %all-to-all-start.4 = ((f32[8,1,128]{2,1,0:T(1,128)}), f32[8,1,128]{2,1,0:T(1,128)S(1)}, u32[]{:S(2)}, u32[]{:S(2)}) async-start(f32[8,1,128]{2,1,0:T(1,128)} %last.1), calls=%async_computation.4 | async-start | bytes 8192 | tf_op jit(solution)/shard_map/all_to_all | solution.py:542

commit v8 on v7

--- a/solution.py
+++ b/solution.py
@@ -141,16 +141,13 @@
         copy.wait()
     lane = lane_ids(1)
 
-    def add_cell(i, carry):
+    for i in range(cell_ref.shape[0]):
         cell = cell_ref[i]
         row = lax.div(cell, cols)
         col = cell - row * cols
         c = lax.div(col, LANES)
         at = pl.ds(row + TOP, 1)
         work[SOURCE * tiles + c, at, :] += jnp.where(lane == col - c * LANES, rate_ref[i], 0.0)
-        return carry
-
-    lax.fori_loop(0, cell_ref.shape[0], add_cell, 0)
     for b in range(blocks):
         wet = wet_ref[b].astype(jnp.float32)
         at = slice(TOP + b * block_rows, TOP + (b + 1) * block_rows)
@@ -488,7 +485,7 @@
     copy.wait()
 
 
-def last_kernel(peak_ref, plan_ref, work, next_ref, best):
+def last_kernel(peak_ref, plan_ref, work, mine_ref, theirs_ref, best):
     tiles = tiles_of(work)
     blocks = plan_ref.shape[0]
     block_rows = (work.shape[1] - 2 * 8) // blocks
@@ -504,12 +501,31 @@
         return carry
 
     lax.fori_loop(0, blocks, one_block, 0, unroll=8)
-    for t in range(next_ref.shape[0]):
-        acc = jnp.zeros((8, LANES), jnp.float32)
-        for b in range(blocks):
-            acc = jnp.maximum(acc, jnp.where(plan_ref[b] == t, best[b], 0.0))
-        top = jnp.max(acc, axis=0, keepdims=True)
-        next_ref[t] = jnp.broadcast_to(jnp.max(top, axis=1, keepdims=True), (1, LANES))
+    is_odd = lax.rem(lax.axis_index("tile"), 2) == 1
+    for j in range(mine_ref.shape[0]):
+        pair = []
+        for t in (2 * j, 2 * j + 1):
+            acc = jnp.zeros((8, LANES), jnp.float32)
+            for b in range(blocks):
+                acc = jnp.maximum(acc, jnp.where(plan_ref[b] == t, best[b], 0.0))
+            top = jnp.max(acc, axis=0, keepdims=True)
+            pair.append(jnp.broadcast_to(jnp.max(top, axis=1, keepdims=True), (1, LANES)))
+        mine_ref[j] = jnp.where(is_odd, pair[1], pair[0])
+        theirs_ref[j] = jnp.where(is_odd, pair[0], pair[1])
+
+
+def chip_kernel(mine_ref, other_ref, *out_refs):
+    here = lax.div(lax.axis_index("tile"), 2)
+    for x, out_ref in enumerate(out_refs):
+        there = jnp.bitwise_xor(here, x)
+        out_ref[...] = jnp.maximum(mine_ref[there], other_ref[there])
+
+
+def helper_kernel(*refs):
+    value = refs[0][...]
+    for ref in refs[1:-1]:
+        value = jnp.maximum(value, ref[...])
+    refs[-1][...] = value[:, :1]
 
 
 def store_kernel(peak_ref, work_in, work, depth_hbm, mom_hbm, sem):
@@ -540,6 +556,10 @@
 
 def exchange(x, axes):
     return lax.all_to_all(x, axes, 0, 0)
+
+
+def swap(x, axis, apart):
+    return lax.ppermute(x, axis, [(i, i ^ apart) for i in range(lax.axis_size(axis))])
 
 
 def send(x, axis, forward):
@@ -684,17 +704,28 @@
             )(peaks, work, strips)
             peaks = exchange(peak, ("region", "tile"))
 
-    best = pl.pallas_call(
+    chips = tile_count // 2
+    mine, theirs = pl.pallas_call(
         last_kernel,
-        out_shape=vmem_out(tile_count, 1, LANES),
+        out_shape=(vmem_out(chips, 1, LANES),) * 2,
         in_specs=[vmem_spec()] * 3,
-        out_specs=vmem_spec(),
+        out_specs=(vmem_spec(),) * 2,
         scratch_shapes=[pltpu.VMEM((blocks, 8, LANES), f32)],
         compiler_params=params(),
         cost_estimate=cost(20 * rows * cols, 2 * nbytes),
         name="last",
     )(peaks, plan, work)
-    helpers = exchange(best, "tile")
+    other = swap(theirs, "tile", 1)
+    known = pl.pallas_call(
+        chip_kernel,
+        out_shape=(vmem_out(1, LANES),) * chips,
+        in_specs=[vmem_spec()] * 2,
+        out_specs=(vmem_spec(),) * chips,
+        compiler_params=params(),
+        cost_estimate=cost(tile_count, 4 * LANES * tile_count),
+        name="chip",
+    )(mine, other)
+    known = [known[0]] + [swap(known[x], "tile", 2 * x) for x in range(1, chips)]
     work, new_depth, new_momentum = pl.pallas_call(
         store_kernel,
         out_shape=(
@@ -710,7 +741,16 @@
         cost_estimate=cost(10 * rows * cols, 2 * nbytes),
         name="store",
     )(peaks, work)
-    return new_depth, new_momentum, jnp.max(helpers[:, :, :1], axis=0)
+    helper = pl.pallas_call(
+        helper_kernel,
+        out_shape=jax.ShapeDtypeStruct((1, 1), f32),
+        in_specs=[vmem_spec()] * chips,
+        out_specs=vmem_spec(),
+        compiler_params=params(),
+        cost_estimate=cost(tile_count, 4 * LANES * tile_count),
+        name="helper",
+    )(*known)
+    return new_depth, new_momentum, helper
 
 
 def solution(mesh):

time: 64 us -> 61.8 us (0.966)
  waiting for transfers between devices: 17.3 us -> 15.9 us
    ppermute x0 -> x4, starting transfers between devices: none -> 3.52 us  [swap(): lax.ppermute(x, axis, [(i, i ^ apart) for i in range(lax.axis_size(axis))])]
    all_to_all x5 -> x4, waiting for transfers between devices: 15.6 us -> 12.2 us  [exchange(): return lax.all_to_all(x, axes, 0, 0)]
    all_to_all x5 -> x4, starting transfers between devices: 16.7 us -> 13.5 us  [exchange(): return lax.all_to_all(x, axes, 0, 0)]
    ppermute x0 -> x4, waiting for transfers between devices: none -> 2.03 us  [swap(): lax.ppermute(x, axis, [(i, i ^ apart) for i in range(lax.axis_size(axis))])]
  transfers between devices with their start and end apart: 9 -> 12, of which waited for: 5 -> 6; matrix products, arithmetic and copies ran while one was open for 0% -> 0% of each run, Pallas kernels for 23% -> 24%
where the time goes in v8:
time: 61.8 us; the launch traced here: 61.5 us
  starting transfers between devices  24.6 us (40%)
  Pallas kernels  20.2 us (33%)
  waiting for transfers between devices  15.9 us (26%)
  between operations  0.79 us (1%)
    all_to_all x4, starting transfers between devices, exchange(): return lax.all_to_all(x, axes, 0, 0)  13.5 us
    pallas_call x5, Pallas kernels, flux(): pl.pallas_call(functools.partial(flux_kernel, part), out_shape=outs, in_s...  12.4 us
    all_to_all x4, waiting for transfers between devices, exchange(): return lax.all_to_all(x, axes, 0, 0)  12.2 us
    ppermute x4, starting transfers between devices, send(): return lax.ppermute(x, axis, pairs)  7.64 us
    ppermute x4, starting transfers between devices, swap(): lax.ppermute(x, axis, [(i, i ^ apart) for i in range(lax.axis_size(axis))])  3.52 us
    pallas_call x3, Pallas kernels, on_device(): pl.pallas_call(update_kernel, out_shape=(work_out, strips_out, peak_out),...  2.88 us
    ppermute x4, waiting for transfers between devices, swap(): lax.ppermute(x, axis, [(i, i ^ apart) for i in range(lax.axis_size(axis))])  2.03 us
    ppermute x4, waiting for transfers between devices, send(): return lax.ppermute(x, axis, pairs)  1.71 us
  transfers between devices with their start and end apart: 12, of which 6 were waited for; matrix products, arithmetic and copies ran while one was open for 0% of the time, Pallas kernels for 24%

profile of v8, /device:TPU:0, one launch (start us, length us, event | category | flops | bytes accessed | tf_op | source)
XLA Modules:
  0.0 61.5 jit_solution(15106764753755292953)
XLA Ops:
  0.6 1.4 %start.1 = (f32[15,400,128]{2,1,0:T(8,128)S(1)}, s32[24,1,128]{2,1,0:T(1,128)S(1)}, f32[10,4,128]{2,1,0:T(4,128)S(1)}, f32[10,4,128]{2,1,0:T(4,128)S(1)}) custom-call(s32[24]{0:T(128)} %bitcast.4, s32[24]{0:T(128)} %bitcast.5, s32[64]{0:T(128)} %bitcast.6, f32[64]{0:T(128)} %bitcast.7, f32[384,256]{1,0:T(8,128)} %depth_hbm.1, f32[2,384,256]{2,1,0:T(8,128)} %mom_hbm.1), custom_call_target="tpu_custom_call" | custom-call | flops 196608 | bytes 1179648 | tf_op jit(solution)/shard_map/start/pallas_call | solution.py:589
  2.1 3.1 %collective-permute-start = (f32[10,4,128]{2,1,0:T(4,128)S(1)}, f32[10,4,128]{2,1,0:T(4,128)S(1)}, u32[]{:S(2)}, u32[]{:S(2)}) collective-permute-start(f32[10,4,128]{2,1,0:T(4,128)S(1)} %get-tuple-element.41), channel_id=1, source_target_pairs={{0,8},{8,16},{16,24},{24,0},{1,9},{9,17},{17,25},{25,1},{2,10},{10... | collective-permute-start | bytes 61448 | tf_op jit(solution)/shard_map/ppermute | solution.py:568
  5.2 2.1 %collective-permute-start.1 = (f32[10,4,128]{2,1,0:T(4,128)S(1)}, f32[10,4,128]{2,1,0:T(4,128)S(1)}, u32[]{:S(2)}, u32[]{:S(2)}) collective-permute-start(f32[10,4,128]{2,1,0:T(4,128)S(1)} %get-tuple-element.42), channel_id=1, source_target_pairs={{8,0},{16,8},{24,16},{0,24},{9,1},{17,9},{25,17},{1,25},{10,2},{18... | collective-permute-start | bytes 61448 | tf_op jit(solution)/shard_map/ppermute | solution.py:568
  7.2 1.0 %pack.1 = (f32[32,2,128]{2,1,0:T(2,128)}, f32[5,4,512]{2,1,0:T(4,128)S(1)}, f32[5,4,512]{2,1,0:T(4,128)S(1)}) custom-call(f32[15,400,128]{2,1,0:T(8,128)S(1)} %get-tuple-element.37.work.work_in), custom_call_target="tpu_custom_call" | custom-call | flops 1966080 | bytes 1179648 | tf_op jit(solution)/shard_map/pack/pallas_call | solution.py:622
  8.3 4.2 %all-to-all-start = ((f32[32,2,128]{2,1,0:T(2,128)}), f32[32,2,128]{2,1,0:T(2,128)S(1)}, u32[]{:S(2)}, u32[]{:S(2)}) async-start(f32[32,2,128]{2,1,0:T(2,128)} %get-tuple-element.38), calls=%async_computation | async-start | bytes 65536 | tf_op jit(solution)/shard_map/all_to_all | solution.py:558
  12.7 2.5 %collective-permute-start.3 = (f32[5,4,512]{2,1,0:T(4,128)S(1)}, f32[5,4,512]{2,1,0:T(4,128)S(1)}, u32[]{:S(2)}, u32[]{:S(2)}) collective-permute-start(f32[5,4,512]{2,1,0:T(4,128)S(1)} %get-tuple-element.44.own_left), channel_id=1, source_target_pairs={{1,0},{2,1},{3,2},{4,3},{5,4},{6,5},{7,6},{0,7},{9,8},{10,9},{11,1... | collective-permute-start | bytes 122888 | tf_op jit(solution)/shard_map/ppermute | solution.py:568
  15.2 2.7 %main.1.refs_0_ = f32[15,400,128]{2,1,0:T(8,128)S(1)} custom-call(f32[15,400,128]{2,1,0:T(8,128)S(1)} %get-tuple-element.43.refs_0_), custom_call_target="tpu_custom_call", output_to_operand_aliasing={{}: (0, {})} | custom-call | flops 14745600 | bytes 4718592 | tf_op jit(solution)/shard_map/main/pallas_call | solution.py:661
  17.8 1.7 %collective-permute-done.2.from_left = f32[5,4,512]{2,1,0:T(4,128)S(1)} collective-permute-done((f32[5,4,512]{2,1,0:T(4,128)S(1)}, f32[5,4,512]{2,1,0:T(4,128)S(1)}, u32[]{:S(2)}, u32[]{:S(2)}) %collective-permute-start.2) | collective-permute-done | bytes 40992 | tf_op jit(solution)/shard_map/ppermute | solution.py:568
  20.4 1.0 %update.3 = (f32[15,400,128]{2,1,0:T(8,128)S(1)}, f32[2,8,8,512]{3,2,1,0:T(8,128)S(1)}, f32[32,1,128]{2,1,0:T(1,128)}) custom-call(f32[32,2,128]{2,1,0:T(2,128)S(1)} %all-to-all-done.peak_ref, f32[15,400,128]{2,1,0:T(8,128)S(1)} %get-tuple-element.46.work_in, ...), custom_call_target="tpu_custom_call", output_to_operand_aliasing={{0}: (1, {}), {1}: (2, {})} | custom-call | flops 1966080 | bytes 1179648 | tf_op jit(solution)/shard_map/update/pallas_call | solution.py:687
  21.3 4.1 %all-to-all-start.1 = ((f32[32,1,128]{2,1,0:T(1,128)}), f32[32,1,128]{2,1,0:T(1,128)S(1)}, u32[]{:S(2)}, u32[]{:S(2)}) async-start(f32[32,1,128]{2,1,0:T(1,128)} %get-tuple-element.48), calls=%async_computation.1 | async-start | bytes 32768 | tf_op jit(solution)/shard_map/all_to_all | solution.py:558
  25.5 3.0 %flux.3 = (f32[15,400,128]{2,1,0:T(8,128)S(1)}, f32[2,8,8,512]{3,2,1,0:T(8,128)S(1)}) custom-call(f32[15,400,128]{2,1,0:T(8,128)S(1)} %get-tuple-element.49.refs_0_, f32[2,8,8,512]{3,2,1,0:T(8,128)S(1)} %get-tuple-element.50.refs_1_), custom_call_target="tpu_custom_call", output_to_operand_aliasing={{0}: (0, {}), {1}: (1, {})} | custom-call | flops 14745600 | bytes 4718592 | tf_op jit(solution)/shard_map/flux/pallas_call | solution.py:661
  28.5 4.1 %all-to-all-done.1.peak_ref = f32[32,1,128]{2,1,0:T(1,128)S(1)} async-done(((f32[32,1,128]{2,1,0:T(1,128)}), f32[32,1,128]{2,1,0:T(1,128)S(1)}, u32[]{:S(2)}, u32[]{:S(2)}) %all-to-all-start.1) | async-done | bytes 16416 | tf_op jit(solution)/shard_map/all_to_all | solution.py:558
  32.5 1.0 %update.4 = (f32[15,400,128]{2,1,0:T(8,128)S(1)}, f32[2,8,8,512]{3,2,1,0:T(8,128)S(1)}, f32[32,1,128]{2,1,0:T(1,128)}) custom-call(f32[32,1,128]{2,1,0:T(1,128)S(1)} %all-to-all-done.1.peak_ref, f32[15,400,128]{2,1,0:T(8,128)S(1)} %get-tuple-element.51.work_in, ...), custom_call_target="tpu_custom_call", output_to_operand_aliasing={{0}: (1, {}), {1}: (2, {})} | custom-call | flops 1966080 | bytes 1179648 | tf_op jit(solution)/shard_map/update/pallas_call | solution.py:687
  33.5 2.6 %all-to-all-start.2 = ((f32[32,1,128]{2,1,0:T(1,128)}), f32[32,1,128]{2,1,0:T(1,128)S(1)}, u32[]{:S(2)}, u32[]{:S(2)}) async-start(f32[32,1,128]{2,1,0:T(1,128)} %get-tuple-element.53), calls=%async_computation.2 | async-start | bytes 32768 | tf_op jit(solution)/shard_map/all_to_all | solution.py:558
  36.1 3.0 %flux.4 = (f32[15,400,128]{2,1,0:T(8,128)S(1)}, f32[2,8,8,512]{3,2,1,0:T(8,128)S(1)}) custom-call(f32[15,400,128]{2,1,0:T(8,128)S(1)} %get-tuple-element.54.refs_0_, f32[2,8,8,512]{3,2,1,0:T(8,128)S(1)} %get-tuple-element.55.refs_1_), custom_call_target="tpu_custom_call", output_to_operand_aliasing={{0}: (0, {}), {1}: (1, {})} | custom-call | flops 14745600 | bytes 4718592 | tf_op jit(solution)/shard_map/flux/pallas_call | solution.py:661
  39.1 4.1 %all-to-all-done.2.peak_ref = f32[32,1,128]{2,1,0:T(1,128)S(1)} async-done(((f32[32,1,128]{2,1,0:T(1,128)}), f32[32,1,128]{2,1,0:T(1,128)S(1)}, u32[]{:S(2)}, u32[]{:S(2)}) %all-to-all-start.2) | async-done | bytes 16416 | tf_op jit(solution)/shard_map/all_to_all | solution.py:558
  43.2 1.0 %update.5 = (f32[15,400,128]{2,1,0:T(8,128)S(1)}, f32[2,8,8,512]{3,2,1,0:T(8,128)S(1)}, f32[32,1,128]{2,1,0:T(1,128)}) custom-call(f32[32,1,128]{2,1,0:T(1,128)S(1)} %all-to-all-done.2.peak_ref, f32[15,400,128]{2,1,0:T(8,128)S(1)} %get-tuple-element.56.work_in, ...), custom_call_target="tpu_custom_call", output_to_operand_aliasing={{0}: (1, {}), {1}: (2, {})} | custom-call | flops 1966080 | bytes 1179648 | tf_op jit(solution)/shard_map/update/pallas_call | solution.py:687
  44.1 2.6 %all-to-all-start.3 = ((f32[32,1,128]{2,1,0:T(1,128)}), f32[32,1,128]{2,1,0:T(1,128)S(1)}, u32[]{:S(2)}, u32[]{:S(2)}) async-start(f32[32,1,128]{2,1,0:T(1,128)} %get-tuple-element.58), calls=%async_computation.3 | async-start | bytes 32768 | tf_op jit(solution)/shard_map/all_to_all | solution.py:558
  46.7 3.0 %flux.5 = (f32[15,400,128]{2,1,0:T(8,128)S(1)}, f32[2,8,8,512]{3,2,1,0:T(8,128)S(1)}) custom-call(f32[15,400,128]{2,1,0:T(8,128)S(1)} %get-tuple-element.59.refs_0_, f32[2,8,8,512]{3,2,1,0:T(8,128)S(1)} %get-tuple-element.60.refs_1_), custom_call_target="tpu_custom_call", output_to_operand_aliasing={{0}: (0, {}), {1}: (1, {})} | custom-call | flops 14745600 | bytes 4718592 | tf_op jit(solution)/shard_map/flux/pallas_call | solution.py:661
  49.7 4.1 %all-to-all-done.3.peak_ref = f32[32,1,128]{2,1,0:T(1,128)S(1)} async-done(((f32[32,1,128]{2,1,0:T(1,128)}), f32[32,1,128]{2,1,0:T(1,128)S(1)}, u32[]{:S(2)}, u32[]{:S(2)}) %all-to-all-start.3) | async-done | bytes 16416 | tf_op jit(solution)/shard_map/all_to_all | solution.py:558
  54.2 1.1 %collective-permute-done.4.other_ref = f32[4,1,128]{2,1,0:T(1,128)S(1)} collective-permute-done((f32[4,1,128]{2,1,0:T(1,128)S(1)}, f32[4,1,128]{2,1,0:T(1,128)S(1)}, u32[]{:S(2)}, u32[]{:S(2)}) %collective-permute-start.4) | collective-permute-done | bytes 2080 | tf_op jit(solution)/shard_map/ppermute | solution.py:562
  56.6 2.3 %collective-permute-start.7 = (f32[1,128]{1,0:T(1,128)S(1)}, f32[1,128]{1,0:T(1,128)S(1)}, u32[]{:S(2)}, u32[]{:S(2)}) collective-permute-start(f32[1,128]{1,0:T(1,128)S(1)} %get-tuple-element.70), channel_id=1, source_target_pairs={{0,6},{1,7},{2,4},{3,5},{4,2},{5,3},{6,0},{7,1},{8,14},{9,15},{10,... | collective-permute-start | bytes 1544 | tf_op jit(solution)/shard_map/ppermute | solution.py:562
  58.9 1.2 %store.1 = (f32[15,400,128]{2,1,0:T(8,128)S(1)}, f32[384,256]{1,0:T(8,128)}, f32[2,384,256]{2,1,0:T(8,128)}) custom-call(f32[32,1,128]{2,1,0:T(1,128)S(1)} %all-to-all-done.3.peak_ref, f32[15,400,128]{2,1,0:T(8,128)S(1)} %get-tuple-element.61.work_in.work), custom_call_target="tpu_custom_call", output_to_operand_aliasing={{0}: (1, {})} | custom-call | flops 983040 | bytes 2359296 | tf_op jit(solution)/shard_map/store/pallas_call | solution.py:729
  60.1 0.9 %collective-permute-done.7.refs_3_ = f32[1,128]{1,0:T(1,128)S(1)} collective-permute-done((f32[1,128]{1,0:T(1,128)S(1)}, f32[1,128]{1,0:T(1,128)S(1)}, u32[]{:S(2)}, u32[]{:S(2)}) %collective-permute-start.7) | collective-permute-done | bytes 544 | tf_op jit(solution)/shard_map/ppermute | solution.py:562
  (16 shorter events, 3.2 us)
Async XLA Ops:
  2.1 10.4 %collective-permute-start = (f32[10,4,128]{2,1,0:T(4,128)S(1)}, f32[10,4,128]{2,1,0:T(4,128)S(1)}, u32[]{:S(2)}, u32[]{:S(2)}) collective-permute-start(f32[10,4,128]{2,1,0:T(4,128)S(1)} %get-tuple-element.41), channel_id=1, source_target_pairs={{0,8},{8,16},{16,24},{24,0},{1,9},{9,17},{17,25},{25,1},{2,10},{10... | collective-permute-start | bytes 61448 | tf_op jit(solution)/shard_map/ppermute | solution.py:568
  5.2 7.4 %collective-permute-start.1 = (f32[10,4,128]{2,1,0:T(4,128)S(1)}, f32[10,4,128]{2,1,0:T(4,128)S(1)}, u32[]{:S(2)}, u32[]{:S(2)}) collective-permute-start(f32[10,4,128]{2,1,0:T(4,128)S(1)} %get-tuple-element.42), channel_id=1, source_target_pairs={{8,0},{16,8},{24,16},{0,24},{9,1},{17,9},{25,17},{1,25},{10,2},{18... | collective-permute-start | bytes 61448 | tf_op jit(solution)/shard_map/ppermute | solution.py:568
  8.3 12.1 %all-to-all-start = ((f32[32,2,128]{2,1,0:T(2,128)}), f32[32,2,128]{2,1,0:T(2,128)S(1)}, u32[]{:S(2)}, u32[]{:S(2)}) async-start(f32[32,2,128]{2,1,0:T(2,128)} %get-tuple-element.38), calls=%async_computation | async-start | bytes 65536 | tf_op jit(solution)/shard_map/all_to_all | solution.py:558
  12.7 5.1 %collective-permute-start.3 = (f32[5,4,512]{2,1,0:T(4,128)S(1)}, f32[5,4,512]{2,1,0:T(4,128)S(1)}, u32[]{:S(2)}, u32[]{:S(2)}) collective-permute-start(f32[5,4,512]{2,1,0:T(4,128)S(1)} %get-tuple-element.44.own_left), channel_id=1, source_target_pairs={{1,0},{2,1},{3,2},{4,3},{5,4},{6,5},{7,6},{0,7},{9,8},{10,9},{11,1... | collective-permute-start | bytes 122888 | tf_op jit(solution)/shard_map/ppermute | solution.py:568
  15.2 4.4 %collective-permute-start.2 = (f32[5,4,512]{2,1,0:T(4,128)S(1)}, f32[5,4,512]{2,1,0:T(4,128)S(1)}, u32[]{:S(2)}, u32[]{:S(2)}) collective-permute-start(f32[5,4,512]{2,1,0:T(4,128)S(1)} %get-tuple-element.45.own_right), channel_id=1, source_target_pairs={{0,1},{1,2},{2,3},{3,4},{4,5},{5,6},{6,7},{7,0},{8,9},{9,10},{10,1... | collective-permute-start | bytes 122888 | tf_op jit(solution)/shard_map/ppermute | solution.py:568
  21.3 11.2 %all-to-all-start.1 = ((f32[32,1,128]{2,1,0:T(1,128)}), f32[32,1,128]{2,1,0:T(1,128)S(1)}, u32[]{:S(2)}, u32[]{:S(2)}) async-start(f32[32,1,128]{2,1,0:T(1,128)} %get-tuple-element.48), calls=%async_computation.1 | async-start | bytes 32768 | tf_op jit(solution)/shard_map/all_to_all | solution.py:558
  33.5 9.6 %all-to-all-start.2 = ((f32[32,1,128]{2,1,0:T(1,128)}), f32[32,1,128]{2,1,0:T(1,128)S(1)}, u32[]{:S(2)}, u32[]{:S(2)}) async-start(f32[32,1,128]{2,1,0:T(1,128)} %get-tuple-element.53), calls=%async_computation.2 | async-start | bytes 32768 | tf_op jit(solution)/shard_map/all_to_all | solution.py:558
  44.1 9.6 %all-to-all-start.3 = ((f32[32,1,128]{2,1,0:T(1,128)}), f32[32,1,128]{2,1,0:T(1,128)S(1)}, u32[]{:S(2)}, u32[]{:S(2)}) async-start(f32[32,1,128]{2,1,0:T(1,128)} %get-tuple-element.58), calls=%async_computation.3 | async-start | bytes 32768 | tf_op jit(solution)/shard_map/all_to_all | solution.py:558
  54.2 1.2 %collective-permute-start.4 = (f32[4,1,128]{2,1,0:T(1,128)S(1)}, f32[4,1,128]{2,1,0:T(1,128)S(1)}, u32[]{:S(2)}, u32[]{:S(2)}) collective-permute-start(f32[4,1,128]{2,1,0:T(1,128)S(1)} %get-tuple-element.66), channel_id=1, source_target_pairs={{0,1},{1,0},{2,3},{3,2},{4,5},{5,4},{6,7},{7,6},{8,9},{9,8},{10,11... | collective-permute-start | bytes 6152 | tf_op jit(solution)/shard_map/ppermute | solution.py:562
  55.4 4.7 %collective-permute-start.5 = (f32[1,128]{1,0:T(1,128)S(1)}, f32[1,128]{1,0:T(1,128)S(1)}, u32[]{:S(2)}, u32[]{:S(2)}) collective-permute-start(f32[1,128]{1,0:T(1,128)S(1)} %get-tuple-element.68), channel_id=1, source_target_pairs={{0,2},{1,3},{2,0},{3,1},{4,6},{5,7},{6,4},{7,5},{8,10},{9,11},{10,... | collective-permute-start | bytes 1544 | tf_op jit(solution)/shard_map/ppermute | solution.py:562
  55.9 4.2 %collective-permute-start.6 = (f32[1,128]{1,0:T(1,128)S(1)}, f32[1,128]{1,0:T(1,128)S(1)}, u32[]{:S(2)}, u32[]{:S(2)}) collective-permute-start(f32[1,128]{1,0:T(1,128)S(1)} %get-tuple-element.69), channel_id=1, source_target_pairs={{0,4},{1,5},{2,6},{3,7},{4,0},{5,1},{6,2},{7,3},{8,12},{9,13},{10,... | collective-permute-start | bytes 1544 | tf_op jit(solution)/shard_map/ppermute | solution.py:562
  56.6 4.4 %collective-permute-start.7 = (f32[1,128]{1,0:T(1,128)S(1)}, f32[1,128]{1,0:T(1,128)S(1)}, u32[]{:S(2)}, u32[]{:S(2)}) collective-permute-start(f32[1,128]{1,0:T(1,128)S(1)} %get-tuple-element.70), channel_id=1, source_target_pairs={{0,6},{1,7},{2,4},{3,5},{4,2},{5,3},{6,0},{7,1},{8,14},{9,15},{10,... | collective-permute-start | bytes 1544 | tf_op jit(solution)/shard_map/ppermute | solution.py:562

commit v9 on v8

--- a/solution.py
+++ b/solution.py
@@ -194,7 +194,7 @@
         return acc
 
     zero = jnp.zeros((8, LANES), jnp.float32)
-    spread_peak(lax.fori_loop(0, rows // 8, find, zero, unroll=16), spread)
+    spread_peak(lax.fori_loop(0, rows // 8, find, zero, unroll=48), spread)
     copy = pltpu.make_async_copy(spread, peak_hbm, sem)
     copy.start()
 
@@ -468,7 +468,7 @@
         return acc
 
     zero = jnp.zeros((8, LANES), jnp.float32)
-    spread_peak(lax.fori_loop(0, row_tiles - 2, find, zero, unroll=16), spread)
+    spread_peak(lax.fori_loop(0, row_tiles - 2, find, zero, unroll=48), spread)
     copy = pltpu.make_async_copy(spread, next_hbm, sem)
     copy.start()
     for q in range(strips.shape[3] // LANES):
@@ -725,7 +725,7 @@
         cost_estimate=cost(tile_count, 4 * LANES * tile_count),
         name="chip",
     )(mine, other)
-    known = [known[0]] + [swap(known[x], "tile", 2 * x) for x in range(1, chips)]
+    known = [swap(known[x], "tile", 2 * x) for x in range(chips - 1, 0, -1)] + [known[0]]
     work, new_depth, new_momentum = pl.pallas_call(
         store_kernel,
         out_shape=(

time: 61.8 us -> 61.6 us (level)
  no operation moved by 1% of the time
where the time goes in v9:
time: 61.6 us; the launch traced here: 61.4 us
  starting transfers between devices  24.6 us (40%)
  Pallas kernels  20.1 us (33%)
  waiting for transfers between devices  15.9 us (26%)
  between operations  0.79 us (1%)
    all_to_all x4, starting transfers between devices, exchange(): return lax.all_to_all(x, axes, 0, 0)  13.5 us
    pallas_call x5, Pallas kernels, flux(): pl.pallas_call(functools.partial(flux_kernel, part), out_shape=outs, in_s...  12.4 us
    all_to_all x4, waiting for transfers between devices, exchange(): return lax.all_to_all(x, axes, 0, 0)  12.2 us
    ppermute x4, starting transfers between devices, send(): return lax.ppermute(x, axis, pairs)  7.64 us
    ppermute x4, starting transfers between devices, swap(): lax.ppermute(x, axis, [(i, i ^ apart) for i in range(lax.axis_size(axis))])  3.52 us
    pallas_call x3, Pallas kernels, on_device(): pl.pallas_call(update_kernel, out_shape=(work_out, strips_out, peak_out),...  2.82 us
    ppermute x4, waiting for transfers between devices, swap(): lax.ppermute(x, axis, [(i, i ^ apart) for i in range(lax.axis_size(axis))])  1.96 us
    ppermute x4, waiting for transfers between devices, send(): return lax.ppermute(x, axis, pairs)  1.71 us
  transfers between devices with their start and end apart: 12, of which 6 were waited for; matrix products, arithmetic and copies ran while one was open for 0% of the time, Pallas kernels for 24%

profile of v9, /device:TPU:0, one launch (start us, length us, event | category | flops | bytes accessed | tf_op | source)
XLA Modules:
  0.0 61.4 jit_solution(10527807973090442730)
XLA Ops:
  0.6 1.4 %start.1 = (f32[15,400,128]{2,1,0:T(8,128)S(1)}, s32[24,1,128]{2,1,0:T(1,128)S(1)}, f32[10,4,128]{2,1,0:T(4,128)S(1)}, f32[10,4,128]{2,1,0:T(4,128)S(1)}) custom-call(s32[24]{0:T(128)} %bitcast.4, s32[24]{0:T(128)} %bitcast.5, s32[64]{0:T(128)} %bitcast.6, f32[64]{0:T(128)} %bitcast.7, f32[384,256]{1,0:T(8,128)} %depth_hbm.1, f32[2,384,256]{2,1,0:T(8,128)} %mom_hbm.1), custom_call_target="tpu_custom_call" | custom-call | flops 196608 | bytes 1179648 | tf_op jit(solution)/shard_map/start/pallas_call | solution.py:589
  2.1 3.1 %collective-permute-start = (f32[10,4,128]{2,1,0:T(4,128)S(1)}, f32[10,4,128]{2,1,0:T(4,128)S(1)}, u32[]{:S(2)}, u32[]{:S(2)}) collective-permute-start(f32[10,4,128]{2,1,0:T(4,128)S(1)} %get-tuple-element.41), channel_id=1, source_target_pairs={{0,8},{8,16},{16,24},{24,0},{1,9},{9,17},{17,25},{25,1},{2,10},{10... | collective-permute-start | bytes 61448 | tf_op jit(solution)/shard_map/ppermute | solution.py:568
  5.2 2.1 %collective-permute-start.1 = (f32[10,4,128]{2,1,0:T(4,128)S(1)}, f32[10,4,128]{2,1,0:T(4,128)S(1)}, u32[]{:S(2)}, u32[]{:S(2)}) collective-permute-start(f32[10,4,128]{2,1,0:T(4,128)S(1)} %get-tuple-element.42), channel_id=1, source_target_pairs={{8,0},{16,8},{24,16},{0,24},{9,1},{17,9},{25,17},{1,25},{10,2},{18... | collective-permute-start | bytes 61448 | tf_op jit(solution)/shard_map/ppermute | solution.py:568
  7.2 1.0 %pack.1 = (f32[32,2,128]{2,1,0:T(2,128)}, f32[5,4,512]{2,1,0:T(4,128)S(1)}, f32[5,4,512]{2,1,0:T(4,128)S(1)}) custom-call(f32[15,400,128]{2,1,0:T(8,128)S(1)} %get-tuple-element.37.work.work_in), custom_call_target="tpu_custom_call" | custom-call | flops 1966080 | bytes 1179648 | tf_op jit(solution)/shard_map/pack/pallas_call | solution.py:622
  8.3 4.2 %all-to-all-start = ((f32[32,2,128]{2,1,0:T(2,128)}), f32[32,2,128]{2,1,0:T(2,128)S(1)}, u32[]{:S(2)}, u32[]{:S(2)}) async-start(f32[32,2,128]{2,1,0:T(2,128)} %get-tuple-element.38), calls=%async_computation | async-start | bytes 65536 | tf_op jit(solution)/shard_map/all_to_all | solution.py:558
  12.7 2.5 %collective-permute-start.3 = (f32[5,4,512]{2,1,0:T(4,128)S(1)}, f32[5,4,512]{2,1,0:T(4,128)S(1)}, u32[]{:S(2)}, u32[]{:S(2)}) collective-permute-start(f32[5,4,512]{2,1,0:T(4,128)S(1)} %get-tuple-element.44.own_left), channel_id=1, source_target_pairs={{1,0},{2,1},{3,2},{4,3},{5,4},{6,5},{7,6},{0,7},{9,8},{10,9},{11,1... | collective-permute-start | bytes 122888 | tf_op jit(solution)/shard_map/ppermute | solution.py:568
  15.2 2.7 %main.1.refs_0_ = f32[15,400,128]{2,1,0:T(8,128)S(1)} custom-call(f32[15,400,128]{2,1,0:T(8,128)S(1)} %get-tuple-element.43.refs_0_), custom_call_target="tpu_custom_call", output_to_operand_aliasing={{}: (0, {})} | custom-call | flops 14745600 | bytes 4718592 | tf_op jit(solution)/shard_map/main/pallas_call | solution.py:661
  17.8 1.7 %collective-permute-done.2.from_left = f32[5,4,512]{2,1,0:T(4,128)S(1)} collective-permute-done((f32[5,4,512]{2,1,0:T(4,128)S(1)}, f32[5,4,512]{2,1,0:T(4,128)S(1)}, u32[]{:S(2)}, u32[]{:S(2)}) %collective-permute-start.2) | collective-permute-done | bytes 40992 | tf_op jit(solution)/shard_map/ppermute | solution.py:568
  20.4 0.9 %update.3 = (f32[15,400,128]{2,1,0:T(8,128)S(1)}, f32[2,8,8,512]{3,2,1,0:T(8,128)S(1)}, f32[32,1,128]{2,1,0:T(1,128)}) custom-call(f32[32,2,128]{2,1,0:T(2,128)S(1)} %all-to-all-done.peak_ref, f32[15,400,128]{2,1,0:T(8,128)S(1)} %get-tuple-element.46.work_in, ...), custom_call_target="tpu_custom_call", output_to_operand_aliasing={{0}: (1, {}), {1}: (2, {})} | custom-call | flops 1966080 | bytes 1179648 | tf_op jit(solution)/shard_map/update/pallas_call | solution.py:687
  21.3 4.1 %all-to-all-start.1 = ((f32[32,1,128]{2,1,0:T(1,128)}), f32[32,1,128]{2,1,0:T(1,128)S(1)}, u32[]{:S(2)}, u32[]{:S(2)}) async-start(f32[32,1,128]{2,1,0:T(1,128)} %get-tuple-element.48), calls=%async_computation.1 | async-start | bytes 32768 | tf_op jit(solution)/shard_map/all_to_all | solution.py:558
  25.4 3.0 %flux.3 = (f32[15,400,128]{2,1,0:T(8,128)S(1)}, f32[2,8,8,512]{3,2,1,0:T(8,128)S(1)}) custom-call(f32[15,400,128]{2,1,0:T(8,128)S(1)} %get-tuple-element.49.refs_0_, f32[2,8,8,512]{3,2,1,0:T(8,128)S(1)} %get-tuple-element.50.refs_1_), custom_call_target="tpu_custom_call", output_to_operand_aliasing={{0}: (0, {}), {1}: (1, {})} | custom-call | flops 14745600 | bytes 4718592 | tf_op jit(solution)/shard_map/flux/pallas_call | solution.py:661
  28.4 4.1 %all-to-all-done.1.peak_ref = f32[32,1,128]{2,1,0:T(1,128)S(1)} async-done(((f32[32,1,128]{2,1,0:T(1,128)}), f32[32,1,128]{2,1,0:T(1,128)S(1)}, u32[]{:S(2)}, u32[]{:S(2)}) %all-to-all-start.1) | async-done | bytes 16416 | tf_op jit(solution)/shard_map/all_to_all | solution.py:558
  32.5 0.9 %update.4 = (f32[15,400,128]{2,1,0:T(8,128)S(1)}, f32[2,8,8,512]{3,2,1,0:T(8,128)S(1)}, f32[32,1,128]{2,1,0:T(1,128)}) custom-call(f32[32,1,128]{2,1,0:T(1,128)S(1)} %all-to-all-done.1.peak_ref, f32[15,400,128]{2,1,0:T(8,128)S(1)} %get-tuple-element.51.work_in, ...), custom_call_target="tpu_custom_call", output_to_operand_aliasing={{0}: (1, {}), {1}: (2, {})} | custom-call | flops 1966080 | bytes 1179648 | tf_op jit(solution)/shard_map/update/pallas_call | solution.py:687
  33.5 2.6 %all-to-all-start.2 = ((f32[32,1,128]{2,1,0:T(1,128)}), f32[32,1,128]{2,1,0:T(1,128)S(1)}, u32[]{:S(2)}, u32[]{:S(2)}) async-start(f32[32,1,128]{2,1,0:T(1,128)} %get-tuple-element.53), calls=%async_computation.2 | async-start | bytes 32768 | tf_op jit(solution)/shard_map/all_to_all | solution.py:558
  36.0 3.0 %flux.4 = (f32[15,400,128]{2,1,0:T(8,128)S(1)}, f32[2,8,8,512]{3,2,1,0:T(8,128)S(1)}) custom-call(f32[15,400,128]{2,1,0:T(8,128)S(1)} %get-tuple-element.54.refs_0_, f32[2,8,8,512]{3,2,1,0:T(8,128)S(1)} %get-tuple-element.55.refs_1_), custom_call_target="tpu_custom_call", output_to_operand_aliasing={{0}: (0, {}), {1}: (1, {})} | custom-call | flops 14745600 | bytes 4718592 | tf_op jit(solution)/shard_map/flux/pallas_call | solution.py:661
  39.0 4.1 %all-to-all-done.2.peak_ref = f32[32,1,128]{2,1,0:T(1,128)S(1)} async-done(((f32[32,1,128]{2,1,0:T(1,128)}), f32[32,1,128]{2,1,0:T(1,128)S(1)}, u32[]{:S(2)}, u32[]{:S(2)}) %all-to-all-start.2) | async-done | bytes 16416 | tf_op jit(solution)/shard_map/all_to_all | solution.py:558
  43.1 0.9 %update.5 = (f32[15,400,128]{2,1,0:T(8,128)S(1)}, f32[2,8,8,512]{3,2,1,0:T(8,128)S(1)}, f32[32,1,128]{2,1,0:T(1,128)}) custom-call(f32[32,1,128]{2,1,0:T(1,128)S(1)} %all-to-all-done.2.peak_ref, f32[15,400,128]{2,1,0:T(8,128)S(1)} %get-tuple-element.56.work_in, ...), custom_call_target="tpu_custom_call", output_to_operand_aliasing={{0}: (1, {}), {1}: (2, {})} | custom-call | flops 1966080 | bytes 1179648 | tf_op jit(solution)/shard_map/update/pallas_call | solution.py:687
  44.0 2.6 %all-to-all-start.3 = ((f32[32,1,128]{2,1,0:T(1,128)}), f32[32,1,128]{2,1,0:T(1,128)S(1)}, u32[]{:S(2)}, u32[]{:S(2)}) async-start(f32[32,1,128]{2,1,0:T(1,128)} %get-tuple-element.58), calls=%async_computation.3 | async-start | bytes 32768 | tf_op jit(solution)/shard_map/all_to_all | solution.py:558
  46.6 3.0 %flux.5 = (f32[15,400,128]{2,1,0:T(8,128)S(1)}, f32[2,8,8,512]{3,2,1,0:T(8,128)S(1)}) custom-call(f32[15,400,128]{2,1,0:T(8,128)S(1)} %get-tuple-element.59.refs_0_, f32[2,8,8,512]{3,2,1,0:T(8,128)S(1)} %get-tuple-element.60.refs_1_), custom_call_target="tpu_custom_call", output_to_operand_aliasing={{0}: (0, {}), {1}: (1, {})} | custom-call | flops 14745600 | bytes 4718592 | tf_op jit(solution)/shard_map/flux/pallas_call | solution.py:661
  49.6 4.1 %all-to-all-done.3.peak_ref = f32[32,1,128]{2,1,0:T(1,128)S(1)} async-done(((f32[32,1,128]{2,1,0:T(1,128)}), f32[32,1,128]{2,1,0:T(1,128)S(1)}, u32[]{:S(2)}, u32[]{:S(2)}) %all-to-all-start.3) | async-done | bytes 16416 | tf_op jit(solution)/shard_map/all_to_all | solution.py:558
  54.2 1.1 %collective-permute-done.4.other_ref = f32[4,1,128]{2,1,0:T(1,128)S(1)} collective-permute-done((f32[4,1,128]{2,1,0:T(1,128)S(1)}, f32[4,1,128]{2,1,0:T(1,128)S(1)}, u32[]{:S(2)}, u32[]{:S(2)}) %collective-permute-start.4) | collective-permute-done | bytes 2080 | tf_op jit(solution)/shard_map/ppermute | solution.py:562
  55.9 1.4 %collective-permute-start.6 = (f32[1,128]{1,0:T(1,128)S(1)}, f32[1,128]{1,0:T(1,128)S(1)}, u32[]{:S(2)}, u32[]{:S(2)}) collective-permute-start(f32[1,128]{1,0:T(1,128)S(1)} %get-tuple-element.68), channel_id=1, source_target_pairs={{0,4},{1,5},{2,6},{3,7},{4,0},{5,1},{6,2},{7,3},{8,12},{9,13},{10,... | collective-permute-start | bytes 1544 | tf_op jit(solution)/shard_map/ppermute | solution.py:562
  57.3 1.5 %collective-permute-start.7 = (f32[1,128]{1,0:T(1,128)S(1)}, f32[1,128]{1,0:T(1,128)S(1)}, u32[]{:S(2)}, u32[]{:S(2)}) collective-permute-start(f32[1,128]{1,0:T(1,128)S(1)} %get-tuple-element.69), channel_id=1, source_target_pairs={{0,2},{1,3},{2,0},{3,1},{4,6},{5,7},{6,4},{7,5},{8,10},{9,11},{10,... | collective-permute-start | bytes 1544 | tf_op jit(solution)/shard_map/ppermute | solution.py:562
  58.8 1.2 %store.1 = (f32[15,400,128]{2,1,0:T(8,128)S(1)}, f32[384,256]{1,0:T(8,128)}, f32[2,384,256]{2,1,0:T(8,128)}) custom-call(f32[32,1,128]{2,1,0:T(1,128)S(1)} %all-to-all-done.3.peak_ref, f32[15,400,128]{2,1,0:T(8,128)S(1)} %get-tuple-element.61.work_in.work), custom_call_target="tpu_custom_call", output_to_operand_aliasing={{0}: (1, {})} | custom-call | flops 983040 | bytes 2359296 | tf_op jit(solution)/shard_map/store/pallas_call | solution.py:729
  (16 shorter events, 3.4 us)
Async XLA Ops:
  2.1 10.4 %collective-permute-start = (f32[10,4,128]{2,1,0:T(4,128)S(1)}, f32[10,4,128]{2,1,0:T(4,128)S(1)}, u32[]{:S(2)}, u32[]{:S(2)}) collective-permute-start(f32[10,4,128]{2,1,0:T(4,128)S(1)} %get-tuple-element.41), channel_id=1, source_target_pairs={{0,8},{8,16},{16,24},{24,0},{1,9},{9,17},{17,25},{25,1},{2,10},{10... | collective-permute-start | bytes 61448 | tf_op jit(solution)/shard_map/ppermute | solution.py:568
  5.2 7.4 %collective-permute-start.1 = (f32[10,4,128]{2,1,0:T(4,128)S(1)}, f32[10,4,128]{2,1,0:T(4,128)S(1)}, u32[]{:S(2)}, u32[]{:S(2)}) collective-permute-start(f32[10,4,128]{2,1,0:T(4,128)S(1)} %get-tuple-element.42), channel_id=1, source_target_pairs={{8,0},{16,8},{24,16},{0,24},{9,1},{17,9},{25,17},{1,25},{10,2},{18... | collective-permute-start | bytes 61448 | tf_op jit(solution)/shard_map/ppermute | solution.py:568
  8.3 12.1 %all-to-all-start = ((f32[32,2,128]{2,1,0:T(2,128)}), f32[32,2,128]{2,1,0:T(2,128)S(1)}, u32[]{:S(2)}, u32[]{:S(2)}) async-start(f32[32,2,128]{2,1,0:T(2,128)} %get-tuple-element.38), calls=%async_computation | async-start | bytes 65536 | tf_op jit(solution)/shard_map/all_to_all | solution.py:558
  12.7 5.1 %collective-permute-start.3 = (f32[5,4,512]{2,1,0:T(4,128)S(1)}, f32[5,4,512]{2,1,0:T(4,128)S(1)}, u32[]{:S(2)}, u32[]{:S(2)}) collective-permute-start(f32[5,4,512]{2,1,0:T(4,128)S(1)} %get-tuple-element.44.own_left), channel_id=1, source_target_pairs={{1,0},{2,1},{3,2},{4,3},{5,4},{6,5},{7,6},{0,7},{9,8},{10,9},{11,1... | collective-permute-start | bytes 122888 | tf_op jit(solution)/shard_map/ppermute | solution.py:568
  15.2 4.4 %collective-permute-start.2 = (f32[5,4,512]{2,1,0:T(4,128)S(1)}, f32[5,4,512]{2,1,0:T(4,128)S(1)}, u32[]{:S(2)}, u32[]{:S(2)}) collective-permute-start(f32[5,4,512]{2,1,0:T(4,128)S(1)} %get-tuple-element.45.own_right), channel_id=1, source_target_pairs={{0,1},{1,2},{2,3},{3,4},{4,5},{5,6},{6,7},{7,0},{8,9},{9,10},{10,1... | collective-permute-start | bytes 122888 | tf_op jit(solution)/shard_map/ppermute | solution.py:568
  21.3 11.2 %all-to-all-start.1 = ((f32[32,1,128]{2,1,0:T(1,128)}), f32[32,1,128]{2,1,0:T(1,128)S(1)}, u32[]{:S(2)}, u32[]{:S(2)}) async-start(f32[32,1,128]{2,1,0:T(1,128)} %get-tuple-element.48), calls=%async_computation.1 | async-start | bytes 32768 | tf_op jit(solution)/shard_map/all_to_all | solution.py:558
  33.5 9.6 %all-to-all-start.2 = ((f32[32,1,128]{2,1,0:T(1,128)}), f32[32,1,128]{2,1,0:T(1,128)S(1)}, u32[]{:S(2)}, u32[]{:S(2)}) async-start(f32[32,1,128]{2,1,0:T(1,128)} %get-tuple-element.53), calls=%async_computation.2 | async-start | bytes 32768 | tf_op jit(solution)/shard_map/all_to_all | solution.py:558
  44.0 9.6 %all-to-all-start.3 = ((f32[32,1,128]{2,1,0:T(1,128)}), f32[32,1,128]{2,1,0:T(1,128)S(1)}, u32[]{:S(2)}, u32[]{:S(2)}) async-start(f32[32,1,128]{2,1,0:T(1,128)} %get-tuple-element.58), calls=%async_computation.3 | async-start | bytes 32768 | tf_op jit(solution)/shard_map/all_to_all | solution.py:558
  54.1 1.2 %collective-permute-start.4 = (f32[4,1,128]{2,1,0:T(1,128)S(1)}, f32[4,1,128]{2,1,0:T(1,128)S(1)}, u32[]{:S(2)}, u32[]{:S(2)}) collective-permute-start(f32[4,1,128]{2,1,0:T(1,128)S(1)} %get-tuple-element.66), channel_id=1, source_target_pairs={{0,1},{1,0},{2,3},{3,2},{4,5},{5,4},{6,7},{7,6},{8,9},{9,8},{10,11... | collective-permute-start | bytes 6152 | tf_op jit(solution)/shard_map/ppermute | solution.py:562
  55.3 4.7 %collective-permute-start.5 = (f32[1,128]{1,0:T(1,128)S(1)}, f32[1,128]{1,0:T(1,128)S(1)}, u32[]{:S(2)}, u32[]{:S(2)}) collective-permute-start(f32[1,128]{1,0:T(1,128)S(1)} %get-tuple-element.67), channel_id=1, source_target_pairs={{0,6},{1,7},{2,4},{3,5},{4,2},{5,3},{6,0},{7,1},{8,14},{9,15},{10,... | collective-permute-start | bytes 1544 | tf_op jit(solution)/shard_map/ppermute | solution.py:562
  55.9 4.1 %collective-permute-start.6 = (f32[1,128]{1,0:T(1,128)S(1)}, f32[1,128]{1,0:T(1,128)S(1)}, u32[]{:S(2)}, u32[]{:S(2)}) collective-permute-start(f32[1,128]{1,0:T(1,128)S(1)} %get-tuple-element.68), channel_id=1, source_target_pairs={{0,4},{1,5},{2,6},{3,7},{4,0},{5,1},{6,2},{7,3},{8,12},{9,13},{10,... | collective-permute-start | bytes 1544 | tf_op jit(solution)/shard_map/ppermute | solution.py:562
  57.3 3.5 %collective-permute-start.7 = (f32[1,128]{1,0:T(1,128)S(1)}, f32[1,128]{1,0:T(1,128)S(1)}, u32[]{:S(2)}, u32[]{:S(2)}) collective-permute-start(f32[1,128]{1,0:T(1,128)S(1)} %get-tuple-element.69), channel_id=1, source_target_pairs={{0,2},{1,3},{2,0},{3,1},{4,6},{5,7},{6,4},{7,5},{8,10},{9,11},{10,... | collective-permute-start | bytes 1544 | tf_op jit(solution)/shard_map/ppermute | solution.py:562

commit v10 on v9

--- a/solution.py
+++ b/solution.py
@@ -202,7 +202,7 @@
         pack[aligned(r * 8, 8), :] = packed(work, aligned(r * 8 + TOP, 8), lane)
         return carry
 
-    lax.fori_loop(0, rows // 8, one, 0, unroll=8)
+    lax.fori_loop(0, rows // 8, one, 0, unroll=24)
     for q in range(rows // LANES):
         at = slice(q * LANES, (q + 1) * LANES)
         split_packed(pack[at, :].T, left_ref, right_ref, at)
@@ -372,7 +372,7 @@
                 work[right, at, :] += jnp.where(active & last, edges[f], 0.0)
             return carry
 
-        lax.fori_loop(0, row_tiles, fix, 0, unroll=10)
+        lax.fori_loop(0, row_tiles, fix, 0, unroll=25)
         return
 
     def derive(r, carry):
@@ -384,7 +384,7 @@
                     derived[k * tiles + c, at, :] = roots[3 + k]
         return carry
 
-    lax.fori_loop(0, row_tiles // 5, derive, 0, unroll=2)
+    lax.fori_loop(0, row_tiles // 5, derive, 0, unroll=5)
     for p in range(3 * tiles):
         faces[p, 0:8, :] = jnp.zeros((8, LANES), jnp.float32)
 

time: 61.6 us -> 61.2 us (level)
  no operation moved by 1% of the time
where the time goes in v10:
time: 61.2 us; the launch traced here: 61 us
  starting transfers between devices  24.6 us (40%)
  Pallas kernels  19.6 us (32%)
  waiting for transfers between devices  16 us (26%)
  between operations  0.79 us (1%)
    all_to_all x4, starting transfers between devices, exchange(): return lax.all_to_all(x, axes, 0, 0)  13.4 us
    all_to_all x4, waiting for transfers between devices, exchange(): return lax.all_to_all(x, axes, 0, 0)  12.3 us
    pallas_call x5, Pallas kernels, flux(): pl.pallas_call(functools.partial(flux_kernel, part), out_shape=outs, in_s...  12.1 us
    ppermute x4, starting transfers between devices, send(): return lax.ppermute(x, axis, pairs)  7.64 us
    ppermute x4, starting transfers between devices, swap(): lax.ppermute(x, axis, [(i, i ^ apart) for i in range(lax.axis_size(axis))])  3.52 us
    pallas_call x3, Pallas kernels, on_device(): pl.pallas_call(update_kernel, out_shape=(work_out, strips_out, peak_out),...  2.82 us
    ppermute x4, waiting for transfers between devices, swap(): lax.ppermute(x, axis, [(i, i ^ apart) for i in range(lax.axis_size(axis))])  1.96 us
    ppermute x4, waiting for transfers between devices, send(): return lax.ppermute(x, axis, pairs)  1.74 us
  transfers between devices with their start and end apart: 12, of which 6 were waited for; matrix products, arithmetic and copies ran while one was open for 0% of the time, Pallas kernels for 24%

profile of v10, /device:TPU:0, one launch (start us, length us, event | category | flops | bytes accessed | tf_op | source)
XLA Modules:
  0.0 61.0 jit_solution(15045874272496630373)
XLA Ops:
  0.6 1.4 %start.1 = (f32[15,400,128]{2,1,0:T(8,128)S(1)}, s32[24,1,128]{2,1,0:T(1,128)S(1)}, f32[10,4,128]{2,1,0:T(4,128)S(1)}, f32[10,4,128]{2,1,0:T(4,128)S(1)}) custom-call(s32[24]{0:T(128)} %bitcast.4, s32[24]{0:T(128)} %bitcast.5, s32[64]{0:T(128)} %bitcast.6, f32[64]{0:T(128)} %bitcast.7, f32[384,256]{1,0:T(8,128)} %depth_hbm.1, f32[2,384,256]{2,1,0:T(8,128)} %mom_hbm.1), custom_call_target="tpu_custom_call" | custom-call | flops 196608 | bytes 1179648 | tf_op jit(solution)/shard_map/start/pallas_call | solution.py:589
  2.1 3.1 %collective-permute-start = (f32[10,4,128]{2,1,0:T(4,128)S(1)}, f32[10,4,128]{2,1,0:T(4,128)S(1)}, u32[]{:S(2)}, u32[]{:S(2)}) collective-permute-start(f32[10,4,128]{2,1,0:T(4,128)S(1)} %get-tuple-element.41), channel_id=1, source_target_pairs={{0,8},{8,16},{16,24},{24,0},{1,9},{9,17},{17,25},{25,1},{2,10},{10... | collective-permute-start | bytes 61448 | tf_op jit(solution)/shard_map/ppermute | solution.py:568
  5.2 2.1 %collective-permute-start.1 = (f32[10,4,128]{2,1,0:T(4,128)S(1)}, f32[10,4,128]{2,1,0:T(4,128)S(1)}, u32[]{:S(2)}, u32[]{:S(2)}) collective-permute-start(f32[10,4,128]{2,1,0:T(4,128)S(1)} %get-tuple-element.42), channel_id=1, source_target_pairs={{8,0},{16,8},{24,16},{0,24},{9,1},{17,9},{25,17},{1,25},{10,2},{18... | collective-permute-start | bytes 61448 | tf_op jit(solution)/shard_map/ppermute | solution.py:568
  7.2 0.9 %pack.1 = (f32[32,2,128]{2,1,0:T(2,128)}, f32[5,4,512]{2,1,0:T(4,128)S(1)}, f32[5,4,512]{2,1,0:T(4,128)S(1)}) custom-call(f32[15,400,128]{2,1,0:T(8,128)S(1)} %get-tuple-element.37.work.work_in), custom_call_target="tpu_custom_call" | custom-call | flops 1966080 | bytes 1179648 | tf_op jit(solution)/shard_map/pack/pallas_call | solution.py:622
  8.1 4.2 %all-to-all-start = ((f32[32,2,128]{2,1,0:T(2,128)}), f32[32,2,128]{2,1,0:T(2,128)S(1)}, u32[]{:S(2)}, u32[]{:S(2)}) async-start(f32[32,2,128]{2,1,0:T(2,128)} %get-tuple-element.38), calls=%async_computation | async-start | bytes 65536 | tf_op jit(solution)/shard_map/all_to_all | solution.py:558
  12.5 2.5 %collective-permute-start.3 = (f32[5,4,512]{2,1,0:T(4,128)S(1)}, f32[5,4,512]{2,1,0:T(4,128)S(1)}, u32[]{:S(2)}, u32[]{:S(2)}) collective-permute-start(f32[5,4,512]{2,1,0:T(4,128)S(1)} %get-tuple-element.44.own_left), channel_id=1, source_target_pairs={{1,0},{2,1},{3,2},{4,3},{5,4},{6,5},{7,6},{0,7},{9,8},{10,9},{11,1... | collective-permute-start | bytes 122888 | tf_op jit(solution)/shard_map/ppermute | solution.py:568
  15.0 2.6 %main.1.refs_0_ = f32[15,400,128]{2,1,0:T(8,128)S(1)} custom-call(f32[15,400,128]{2,1,0:T(8,128)S(1)} %get-tuple-element.43.refs_0_), custom_call_target="tpu_custom_call", output_to_operand_aliasing={{}: (0, {})} | custom-call | flops 14745600 | bytes 4718592 | tf_op jit(solution)/shard_map/main/pallas_call | solution.py:661
  17.6 1.7 %collective-permute-done.2.from_left = f32[5,4,512]{2,1,0:T(4,128)S(1)} collective-permute-done((f32[5,4,512]{2,1,0:T(4,128)S(1)}, f32[5,4,512]{2,1,0:T(4,128)S(1)}, u32[]{:S(2)}, u32[]{:S(2)}) %collective-permute-start.2) | collective-permute-done | bytes 40992 | tf_op jit(solution)/shard_map/ppermute | solution.py:568
  20.0 0.9 %update.3 = (f32[15,400,128]{2,1,0:T(8,128)S(1)}, f32[2,8,8,512]{3,2,1,0:T(8,128)S(1)}, f32[32,1,128]{2,1,0:T(1,128)}) custom-call(f32[32,2,128]{2,1,0:T(2,128)S(1)} %all-to-all-done.peak_ref, f32[15,400,128]{2,1,0:T(8,128)S(1)} %get-tuple-element.46.work_in, ...), custom_call_target="tpu_custom_call", output_to_operand_aliasing={{0}: (1, {}), {1}: (2, {})} | custom-call | flops 1966080 | bytes 1179648 | tf_op jit(solution)/shard_map/update/pallas_call | solution.py:687
  20.9 4.1 %all-to-all-start.1 = ((f32[32,1,128]{2,1,0:T(1,128)}), f32[32,1,128]{2,1,0:T(1,128)S(1)}, u32[]{:S(2)}, u32[]{:S(2)}) async-start(f32[32,1,128]{2,1,0:T(1,128)} %get-tuple-element.48), calls=%async_computation.1 | async-start | bytes 32768 | tf_op jit(solution)/shard_map/all_to_all | solution.py:558
  25.0 3.0 %flux.3 = (f32[15,400,128]{2,1,0:T(8,128)S(1)}, f32[2,8,8,512]{3,2,1,0:T(8,128)S(1)}) custom-call(f32[15,400,128]{2,1,0:T(8,128)S(1)} %get-tuple-element.49.refs_0_, f32[2,8,8,512]{3,2,1,0:T(8,128)S(1)} %get-tuple-element.50.refs_1_), custom_call_target="tpu_custom_call", output_to_operand_aliasing={{0}: (0, {}), {1}: (1, {})} | custom-call | flops 14745600 | bytes 4718592 | tf_op jit(solution)/shard_map/flux/pallas_call | solution.py:661
  28.0 4.1 %all-to-all-done.1.peak_ref = f32[32,1,128]{2,1,0:T(1,128)S(1)} async-done(((f32[32,1,128]{2,1,0:T(1,128)}), f32[32,1,128]{2,1,0:T(1,128)S(1)}, u32[]{:S(2)}, u32[]{:S(2)}) %all-to-all-start.1) | async-done | bytes 16416 | tf_op jit(solution)/shard_map/all_to_all | solution.py:558
  32.1 0.9 %update.4 = (f32[15,400,128]{2,1,0:T(8,128)S(1)}, f32[2,8,8,512]{3,2,1,0:T(8,128)S(1)}, f32[32,1,128]{2,1,0:T(1,128)}) custom-call(f32[32,1,128]{2,1,0:T(1,128)S(1)} %all-to-all-done.1.peak_ref, f32[15,400,128]{2,1,0:T(8,128)S(1)} %get-tuple-element.51.work_in, ...), custom_call_target="tpu_custom_call", output_to_operand_aliasing={{0}: (1, {}), {1}: (2, {})} | custom-call | flops 1966080 | bytes 1179648 | tf_op jit(solution)/shard_map/update/pallas_call | solution.py:687
  33.0 2.6 %all-to-all-start.2 = ((f32[32,1,128]{2,1,0:T(1,128)}), f32[32,1,128]{2,1,0:T(1,128)S(1)}, u32[]{:S(2)}, u32[]{:S(2)}) async-start(f32[32,1,128]{2,1,0:T(1,128)} %get-tuple-element.53), calls=%async_computation.2 | async-start | bytes 32768 | tf_op jit(solution)/shard_map/all_to_all | solution.py:558
  35.6 3.0 %flux.4 = (f32[15,400,128]{2,1,0:T(8,128)S(1)}, f32[2,8,8,512]{3,2,1,0:T(8,128)S(1)}) custom-call(f32[15,400,128]{2,1,0:T(8,128)S(1)} %get-tuple-element.54.refs_0_, f32[2,8,8,512]{3,2,1,0:T(8,128)S(1)} %get-tuple-element.55.refs_1_), custom_call_target="tpu_custom_call", output_to_operand_aliasing={{0}: (0, {}), {1}: (1, {})} | custom-call | flops 14745600 | bytes 4718592 | tf_op jit(solution)/shard_map/flux/pallas_call | solution.py:661
  38.6 4.1 %all-to-all-done.2.peak_ref = f32[32,1,128]{2,1,0:T(1,128)S(1)} async-done(((f32[32,1,128]{2,1,0:T(1,128)}), f32[32,1,128]{2,1,0:T(1,128)S(1)}, u32[]{:S(2)}, u32[]{:S(2)}) %all-to-all-start.2) | async-done | bytes 16416 | tf_op jit(solution)/shard_map/all_to_all | solution.py:558
  42.7 0.9 %update.5 = (f32[15,400,128]{2,1,0:T(8,128)S(1)}, f32[2,8,8,512]{3,2,1,0:T(8,128)S(1)}, f32[32,1,128]{2,1,0:T(1,128)}) custom-call(f32[32,1,128]{2,1,0:T(1,128)S(1)} %all-to-all-done.2.peak_ref, f32[15,400,128]{2,1,0:T(8,128)S(1)} %get-tuple-element.56.work_in, ...), custom_call_target="tpu_custom_call", output_to_operand_aliasing={{0}: (1, {}), {1}: (2, {})} | custom-call | flops 1966080 | bytes 1179648 | tf_op jit(solution)/shard_map/update/pallas_call | solution.py:687
  43.6 2.6 %all-to-all-start.3 = ((f32[32,1,128]{2,1,0:T(1,128)}), f32[32,1,128]{2,1,0:T(1,128)S(1)}, u32[]{:S(2)}, u32[]{:S(2)}) async-start(f32[32,1,128]{2,1,0:T(1,128)} %get-tuple-element.58), calls=%async_computation.3 | async-start | bytes 32768 | tf_op jit(solution)/shard_map/all_to_all | solution.py:558
  46.2 3.0 %flux.5 = (f32[15,400,128]{2,1,0:T(8,128)S(1)}, f32[2,8,8,512]{3,2,1,0:T(8,128)S(1)}) custom-call(f32[15,400,128]{2,1,0:T(8,128)S(1)} %get-tuple-element.59.refs_0_, f32[2,8,8,512]{3,2,1,0:T(8,128)S(1)} %get-tuple-element.60.refs_1_), custom_call_target="tpu_custom_call", output_to_operand_aliasing={{0}: (0, {}), {1}: (1, {})} | custom-call | flops 14745600 | bytes 4718592 | tf_op jit(solution)/shard_map/flux/pallas_call | solution.py:661
  49.2 4.1 %all-to-all-done.3.peak_ref = f32[32,1,128]{2,1,0:T(1,128)S(1)} async-done(((f32[32,1,128]{2,1,0:T(1,128)}), f32[32,1,128]{2,1,0:T(1,128)S(1)}, u32[]{:S(2)}, u32[]{:S(2)}) %all-to-all-start.3) | async-done | bytes 16416 | tf_op jit(solution)/shard_map/all_to_all | solution.py:558
  53.8 1.1 %collective-permute-done.4.other_ref = f32[4,1,128]{2,1,0:T(1,128)S(1)} collective-permute-done((f32[4,1,128]{2,1,0:T(1,128)S(1)}, f32[4,1,128]{2,1,0:T(1,128)S(1)}, u32[]{:S(2)}, u32[]{:S(2)}) %collective-permute-start.4) | collective-permute-done | bytes 2080 | tf_op jit(solution)/shard_map/ppermute | solution.py:562
  55.5 1.4 %collective-permute-start.6 = (f32[1,128]{1,0:T(1,128)S(1)}, f32[1,128]{1,0:T(1,128)S(1)}, u32[]{:S(2)}, u32[]{:S(2)}) collective-permute-start(f32[1,128]{1,0:T(1,128)S(1)} %get-tuple-element.68), channel_id=1, source_target_pairs={{0,4},{1,5},{2,6},{3,7},{4,0},{5,1},{6,2},{7,3},{8,12},{9,13},{10,... | collective-permute-start | bytes 1544 | tf_op jit(solution)/shard_map/ppermute | solution.py:562
  56.9 1.5 %collective-permute-start.7 = (f32[1,128]{1,0:T(1,128)S(1)}, f32[1,128]{1,0:T(1,128)S(1)}, u32[]{:S(2)}, u32[]{:S(2)}) collective-permute-start(f32[1,128]{1,0:T(1,128)S(1)} %get-tuple-element.69), channel_id=1, source_target_pairs={{0,2},{1,3},{2,0},{3,1},{4,6},{5,7},{6,4},{7,5},{8,10},{9,11},{10,... | collective-permute-start | bytes 1544 | tf_op jit(solution)/shard_map/ppermute | solution.py:562
  58.4 1.2 %store.1 = (f32[15,400,128]{2,1,0:T(8,128)S(1)}, f32[384,256]{1,0:T(8,128)}, f32[2,384,256]{2,1,0:T(8,128)}) custom-call(f32[32,1,128]{2,1,0:T(1,128)S(1)} %all-to-all-done.3.peak_ref, f32[15,400,128]{2,1,0:T(8,128)S(1)} %get-tuple-element.61.work_in.work), custom_call_target="tpu_custom_call", output_to_operand_aliasing={{0}: (1, {})} | custom-call | flops 983040 | bytes 2359296 | tf_op jit(solution)/shard_map/store/pallas_call | solution.py:729
  (16 shorter events, 3.2 us)
Async XLA Ops:
  2.1 10.3 %collective-permute-start = (f32[10,4,128]{2,1,0:T(4,128)S(1)}, f32[10,4,128]{2,1,0:T(4,128)S(1)}, u32[]{:S(2)}, u32[]{:S(2)}) collective-permute-start(f32[10,4,128]{2,1,0:T(4,128)S(1)} %get-tuple-element.41), channel_id=1, source_target_pairs={{0,8},{8,16},{16,24},{24,0},{1,9},{9,17},{17,25},{25,1},{2,10},{10... | collective-permute-start | bytes 61448 | tf_op jit(solution)/shard_map/ppermute | solution.py:568
  5.2 7.2 %collective-permute-start.1 = (f32[10,4,128]{2,1,0:T(4,128)S(1)}, f32[10,4,128]{2,1,0:T(4,128)S(1)}, u32[]{:S(2)}, u32[]{:S(2)}) collective-permute-start(f32[10,4,128]{2,1,0:T(4,128)S(1)} %get-tuple-element.42), channel_id=1, source_target_pairs={{8,0},{16,8},{24,16},{0,24},{9,1},{17,9},{25,17},{1,25},{10,2},{18... | collective-permute-start | bytes 61448 | tf_op jit(solution)/shard_map/ppermute | solution.py:568
  8.1 11.9 %all-to-all-start = ((f32[32,2,128]{2,1,0:T(2,128)}), f32[32,2,128]{2,1,0:T(2,128)S(1)}, u32[]{:S(2)}, u32[]{:S(2)}) async-start(f32[32,2,128]{2,1,0:T(2,128)} %get-tuple-element.38), calls=%async_computation | async-start | bytes 65536 | tf_op jit(solution)/shard_map/all_to_all | solution.py:558
  12.5 5.1 %collective-permute-start.3 = (f32[5,4,512]{2,1,0:T(4,128)S(1)}, f32[5,4,512]{2,1,0:T(4,128)S(1)}, u32[]{:S(2)}, u32[]{:S(2)}) collective-permute-start(f32[5,4,512]{2,1,0:T(4,128)S(1)} %get-tuple-element.44.own_left), channel_id=1, source_target_pairs={{1,0},{2,1},{3,2},{4,3},{5,4},{6,5},{7,6},{0,7},{9,8},{10,9},{11,1... | collective-permute-start | bytes 122888 | tf_op jit(solution)/shard_map/ppermute | solution.py:568
  15.0 4.4 %collective-permute-start.2 = (f32[5,4,512]{2,1,0:T(4,128)S(1)}, f32[5,4,512]{2,1,0:T(4,128)S(1)}, u32[]{:S(2)}, u32[]{:S(2)}) collective-permute-start(f32[5,4,512]{2,1,0:T(4,128)S(1)} %get-tuple-element.45.own_right), channel_id=1, source_target_pairs={{0,1},{1,2},{2,3},{3,4},{4,5},{5,6},{6,7},{7,0},{8,9},{9,10},{10,1... | collective-permute-start | bytes 122888 | tf_op jit(solution)/shard_map/ppermute | solution.py:568
  20.9 11.2 %all-to-all-start.1 = ((f32[32,1,128]{2,1,0:T(1,128)}), f32[32,1,128]{2,1,0:T(1,128)S(1)}, u32[]{:S(2)}, u32[]{:S(2)}) async-start(f32[32,1,128]{2,1,0:T(1,128)} %get-tuple-element.48), calls=%async_computation.1 | async-start | bytes 32768 | tf_op jit(solution)/shard_map/all_to_all | solution.py:558
  33.0 9.6 %all-to-all-start.2 = ((f32[32,1,128]{2,1,0:T(1,128)}), f32[32,1,128]{2,1,0:T(1,128)S(1)}, u32[]{:S(2)}, u32[]{:S(2)}) async-start(f32[32,1,128]{2,1,0:T(1,128)} %get-tuple-element.53), calls=%async_computation.2 | async-start | bytes 32768 | tf_op jit(solution)/shard_map/all_to_all | solution.py:558
  43.6 9.6 %all-to-all-start.3 = ((f32[32,1,128]{2,1,0:T(1,128)}), f32[32,1,128]{2,1,0:T(1,128)S(1)}, u32[]{:S(2)}, u32[]{:S(2)}) async-start(f32[32,1,128]{2,1,0:T(1,128)} %get-tuple-element.58), calls=%async_computation.3 | async-start | bytes 32768 | tf_op jit(solution)/shard_map/all_to_all | solution.py:558
  53.7 1.2 %collective-permute-start.4 = (f32[4,1,128]{2,1,0:T(1,128)S(1)}, f32[4,1,128]{2,1,0:T(1,128)S(1)}, u32[]{:S(2)}, u32[]{:S(2)}) collective-permute-start(f32[4,1,128]{2,1,0:T(1,128)S(1)} %get-tuple-element.66), channel_id=1, source_target_pairs={{0,1},{1,0},{2,3},{3,2},{4,5},{5,4},{6,7},{7,6},{8,9},{9,8},{10,11... | collective-permute-start | bytes 6152 | tf_op jit(solution)/shard_map/ppermute | solution.py:562
  54.9 4.7 %collective-permute-start.5 = (f32[1,128]{1,0:T(1,128)S(1)}, f32[1,128]{1,0:T(1,128)S(1)}, u32[]{:S(2)}, u32[]{:S(2)}) collective-permute-start(f32[1,128]{1,0:T(1,128)S(1)} %get-tuple-element.67), channel_id=1, source_target_pairs={{0,6},{1,7},{2,4},{3,5},{4,2},{5,3},{6,0},{7,1},{8,14},{9,15},{10,... | collective-permute-start | bytes 1544 | tf_op jit(solution)/shard_map/ppermute | solution.py:562
  55.5 4.1 %collective-permute-start.6 = (f32[1,128]{1,0:T(1,128)S(1)}, f32[1,128]{1,0:T(1,128)S(1)}, u32[]{:S(2)}, u32[]{:S(2)}) collective-permute-start(f32[1,128]{1,0:T(1,128)S(1)} %get-tuple-element.68), channel_id=1, source_target_pairs={{0,4},{1,5},{2,6},{3,7},{4,0},{5,1},{6,2},{7,3},{8,12},{9,13},{10,... | collective-permute-start | bytes 1544 | tf_op jit(solution)/shard_map/ppermute | solution.py:562
  56.9 3.5 %collective-permute-start.7 = (f32[1,128]{1,0:T(1,128)S(1)}, f32[1,128]{1,0:T(1,128)S(1)}, u32[]{:S(2)}, u32[]{:S(2)}) collective-permute-start(f32[1,128]{1,0:T(1,128)S(1)} %get-tuple-element.69), channel_id=1, source_target_pairs={{0,2},{1,3},{2,0},{3,1},{4,6},{5,7},{6,4},{7,5},{8,10},{9,11},{10,... | collective-permute-start | bytes 1544 | tf_op jit(solution)/shard_map/ppermute | solution.py:562

commit v11 on v10

--- a/solution.py
+++ b/solution.py
@@ -481,7 +481,7 @@
         move_own(work, aligned(r * 8, 8), ratio)
         return carry
 
-    lax.fori_loop(0, row_tiles, move, 0, unroll=10)
+    lax.fori_loop(0, row_tiles, move, 0, unroll=25)
     copy.wait()
 
 
@@ -500,7 +500,7 @@
         best[b] = acc
         return carry
 
-    lax.fori_loop(0, blocks, one_block, 0, unroll=8)
+    lax.fori_loop(0, blocks, one_block, 0, unroll=24)
     is_odd = lax.rem(lax.axis_index("tile"), 2) == 1
     for j in range(mine_ref.shape[0]):
         pair = []

time: 61.2 us -> 61.2 us (level)
  no operation moved by 1% of the time
where the time goes in v11:
time: 61.2 us; the launch traced here: 60.9 us
  starting transfers between devices  24.6 us (40%)
  Pallas kernels  19.6 us (32%)
  waiting for transfers between devices  16 us (26%)
  between operations  0.79 us (1%)
    all_to_all x4, starting transfers between devices, exchange(): return lax.all_to_all(x, axes, 0, 0)  13.4 us
    all_to_all x4, waiting for transfers between devices, exchange(): return lax.all_to_all(x, axes, 0, 0)  12.3 us
    pallas_call x5, Pallas kernels, flux(): pl.pallas_call(functools.partial(flux_kernel, part), out_shape=outs, in_s...  12.1 us
    ppermute x4, starting transfers between devices, send(): return lax.ppermute(x, axis, pairs)  7.64 us
    ppermute x4, starting transfers between devices, swap(): lax.ppermute(x, axis, [(i, i ^ apart) for i in range(lax.axis_size(axis))])  3.52 us
    pallas_call x3, Pallas kernels, on_device(): pl.pallas_call(update_kernel, out_shape=(work_out, strips_out, peak_out),...  2.82 us
    ppermute x4, waiting for transfers between devices, swap(): lax.ppermute(x, axis, [(i, i ^ apart) for i in range(lax.axis_size(axis))])  1.96 us
    ppermute x4, waiting for transfers between devices, send(): return lax.ppermute(x, axis, pairs)  1.74 us
  transfers between devices with their start and end apart: 12, of which 6 were waited for; matrix products, arithmetic and copies ran while one was open for 0% of the time, Pallas kernels for 24%

profile of v11, /device:TPU:0, one launch (start us, length us, event | category | flops | bytes accessed | tf_op | source)
XLA Modules:
  0.0 60.9 jit_solution(10669422488661892506)
XLA Ops:
  0.6 1.4 %start.1 = (f32[15,400,128]{2,1,0:T(8,128)S(1)}, s32[24,1,128]{2,1,0:T(1,128)S(1)}, f32[10,4,128]{2,1,0:T(4,128)S(1)}, f32[10,4,128]{2,1,0:T(4,128)S(1)}) custom-call(s32[24]{0:T(128)} %bitcast.4, s32[24]{0:T(128)} %bitcast.5, s32[64]{0:T(128)} %bitcast.6, f32[64]{0:T(128)} %bitcast.7, f32[384,256]{1,0:T(8,128)} %depth_hbm.1, f32[2,384,256]{2,1,0:T(8,128)} %mom_hbm.1), custom_call_target="tpu_custom_call" | custom-call | flops 196608 | bytes 1179648 | tf_op jit(solution)/shard_map/start/pallas_call | solution.py:589
  2.1 3.1 %collective-permute-start = (f32[10,4,128]{2,1,0:T(4,128)S(1)}, f32[10,4,128]{2,1,0:T(4,128)S(1)}, u32[]{:S(2)}, u32[]{:S(2)}) collective-permute-start(f32[10,4,128]{2,1,0:T(4,128)S(1)} %get-tuple-element.41), channel_id=1, source_target_pairs={{0,8},{8,16},{16,24},{24,0},{1,9},{9,17},{17,25},{25,1},{2,10},{10... | collective-permute-start | bytes 61448 | tf_op jit(solution)/shard_map/ppermute | solution.py:568
  5.2 2.1 %collective-permute-start.1 = (f32[10,4,128]{2,1,0:T(4,128)S(1)}, f32[10,4,128]{2,1,0:T(4,128)S(1)}, u32[]{:S(2)}, u32[]{:S(2)}) collective-permute-start(f32[10,4,128]{2,1,0:T(4,128)S(1)} %get-tuple-element.42), channel_id=1, source_target_pairs={{8,0},{16,8},{24,16},{0,24},{9,1},{17,9},{25,17},{1,25},{10,2},{18... | collective-permute-start | bytes 61448 | tf_op jit(solution)/shard_map/ppermute | solution.py:568
  7.2 0.9 %pack.1 = (f32[32,2,128]{2,1,0:T(2,128)}, f32[5,4,512]{2,1,0:T(4,128)S(1)}, f32[5,4,512]{2,1,0:T(4,128)S(1)}) custom-call(f32[15,400,128]{2,1,0:T(8,128)S(1)} %get-tuple-element.37.work.work_in), custom_call_target="tpu_custom_call" | custom-call | flops 1966080 | bytes 1179648 | tf_op jit(solution)/shard_map/pack/pallas_call | solution.py:622
  8.1 4.2 %all-to-all-start = ((f32[32,2,128]{2,1,0:T(2,128)}), f32[32,2,128]{2,1,0:T(2,128)S(1)}, u32[]{:S(2)}, u32[]{:S(2)}) async-start(f32[32,2,128]{2,1,0:T(2,128)} %get-tuple-element.38), calls=%async_computation | async-start | bytes 65536 | tf_op jit(solution)/shard_map/all_to_all | solution.py:558
  12.5 2.5 %collective-permute-start.3 = (f32[5,4,512]{2,1,0:T(4,128)S(1)}, f32[5,4,512]{2,1,0:T(4,128)S(1)}, u32[]{:S(2)}, u32[]{:S(2)}) collective-permute-start(f32[5,4,512]{2,1,0:T(4,128)S(1)} %get-tuple-element.44.own_left), channel_id=1, source_target_pairs={{1,0},{2,1},{3,2},{4,3},{5,4},{6,5},{7,6},{0,7},{9,8},{10,9},{11,1... | collective-permute-start | bytes 122888 | tf_op jit(solution)/shard_map/ppermute | solution.py:568
  15.0 2.6 %main.1.refs_0_ = f32[15,400,128]{2,1,0:T(8,128)S(1)} custom-call(f32[15,400,128]{2,1,0:T(8,128)S(1)} %get-tuple-element.43.refs_0_), custom_call_target="tpu_custom_call", output_to_operand_aliasing={{}: (0, {})} | custom-call | flops 14745600 | bytes 4718592 | tf_op jit(solution)/shard_map/main/pallas_call | solution.py:661
  17.6 1.7 %collective-permute-done.2.from_left = f32[5,4,512]{2,1,0:T(4,128)S(1)} collective-permute-done((f32[5,4,512]{2,1,0:T(4,128)S(1)}, f32[5,4,512]{2,1,0:T(4,128)S(1)}, u32[]{:S(2)}, u32[]{:S(2)}) %collective-permute-start.2) | collective-permute-done | bytes 40992 | tf_op jit(solution)/shard_map/ppermute | solution.py:568
  20.0 0.9 %update.3 = (f32[15,400,128]{2,1,0:T(8,128)S(1)}, f32[2,8,8,512]{3,2,1,0:T(8,128)S(1)}, f32[32,1,128]{2,1,0:T(1,128)}) custom-call(f32[32,2,128]{2,1,0:T(2,128)S(1)} %all-to-all-done.peak_ref, f32[15,400,128]{2,1,0:T(8,128)S(1)} %get-tuple-element.46.work_in, ...), custom_call_target="tpu_custom_call", output_to_operand_aliasing={{0}: (1, {}), {1}: (2, {})} | custom-call | flops 1966080 | bytes 1179648 | tf_op jit(solution)/shard_map/update/pallas_call | solution.py:687
  20.9 4.1 %all-to-all-start.1 = ((f32[32,1,128]{2,1,0:T(1,128)}), f32[32,1,128]{2,1,0:T(1,128)S(1)}, u32[]{:S(2)}, u32[]{:S(2)}) async-start(f32[32,1,128]{2,1,0:T(1,128)} %get-tuple-element.48), calls=%async_computation.1 | async-start | bytes 32768 | tf_op jit(solution)/shard_map/all_to_all | solution.py:558
  25.0 3.0 %flux.3 = (f32[15,400,128]{2,1,0:T(8,128)S(1)}, f32[2,8,8,512]{3,2,1,0:T(8,128)S(1)}) custom-call(f32[15,400,128]{2,1,0:T(8,128)S(1)} %get-tuple-element.49.refs_0_, f32[2,8,8,512]{3,2,1,0:T(8,128)S(1)} %get-tuple-element.50.refs_1_), custom_call_target="tpu_custom_call", output_to_operand_aliasing={{0}: (0, {}), {1}: (1, {})} | custom-call | flops 14745600 | bytes 4718592 | tf_op jit(solution)/shard_map/flux/pallas_call | solution.py:661
  28.0 4.1 %all-to-all-done.1.peak_ref = f32[32,1,128]{2,1,0:T(1,128)S(1)} async-done(((f32[32,1,128]{2,1,0:T(1,128)}), f32[32,1,128]{2,1,0:T(1,128)S(1)}, u32[]{:S(2)}, u32[]{:S(2)}) %all-to-all-start.1) | async-done | bytes 16416 | tf_op jit(solution)/shard_map/all_to_all | solution.py:558
  32.1 0.9 %update.4 = (f32[15,400,128]{2,1,0:T(8,128)S(1)}, f32[2,8,8,512]{3,2,1,0:T(8,128)S(1)}, f32[32,1,128]{2,1,0:T(1,128)}) custom-call(f32[32,1,128]{2,1,0:T(1,128)S(1)} %all-to-all-done.1.peak_ref, f32[15,400,128]{2,1,0:T(8,128)S(1)} %get-tuple-element.51.work_in, ...), custom_call_target="tpu_custom_call", output_to_operand_aliasing={{0}: (1, {}), {1}: (2, {})} | custom-call | flops 1966080 | bytes 1179648 | tf_op jit(solution)/shard_map/update/pallas_call | solution.py:687
  33.0 2.6 %all-to-all-start.2 = ((f32[32,1,128]{2,1,0:T(1,128)}), f32[32,1,128]{2,1,0:T(1,128)S(1)}, u32[]{:S(2)}, u32[]{:S(2)}) async-start(f32[32,1,128]{2,1,0:T(1,128)} %get-tuple-element.53), calls=%async_computation.2 | async-start | bytes 32768 | tf_op jit(solution)/shard_map/all_to_all | solution.py:558
  35.6 3.0 %flux.4 = (f32[15,400,128]{2,1,0:T(8,128)S(1)}, f32[2,8,8,512]{3,2,1,0:T(8,128)S(1)}) custom-call(f32[15,400,128]{2,1,0:T(8,128)S(1)} %get-tuple-element.54.refs_0_, f32[2,8,8,512]{3,2,1,0:T(8,128)S(1)} %get-tuple-element.55.refs_1_), custom_call_target="tpu_custom_call", output_to_operand_aliasing={{0}: (0, {}), {1}: (1, {})} | custom-call | flops 14745600 | bytes 4718592 | tf_op jit(solution)/shard_map/flux/pallas_call | solution.py:661
  38.6 4.1 %all-to-all-done.2.peak_ref = f32[32,1,128]{2,1,0:T(1,128)S(1)} async-done(((f32[32,1,128]{2,1,0:T(1,128)}), f32[32,1,128]{2,1,0:T(1,128)S(1)}, u32[]{:S(2)}, u32[]{:S(2)}) %all-to-all-start.2) | async-done | bytes 16416 | tf_op jit(solution)/shard_map/all_to_all | solution.py:558
  42.7 0.9 %update.5 = (f32[15,400,128]{2,1,0:T(8,128)S(1)}, f32[2,8,8,512]{3,2,1,0:T(8,128)S(1)}, f32[32,1,128]{2,1,0:T(1,128)}) custom-call(f32[32,1,128]{2,1,0:T(1,128)S(1)} %all-to-all-done.2.peak_ref, f32[15,400,128]{2,1,0:T(8,128)S(1)} %get-tuple-element.56.work_in, ...), custom_call_target="tpu_custom_call", output_to_operand_aliasing={{0}: (1, {}), {1}: (2, {})} | custom-call | flops 1966080 | bytes 1179648 | tf_op jit(solution)/shard_map/update/pallas_call | solution.py:687
  43.6 2.6 %all-to-all-start.3 = ((f32[32,1,128]{2,1,0:T(1,128)}), f32[32,1,128]{2,1,0:T(1,128)S(1)}, u32[]{:S(2)}, u32[]{:S(2)}) async-start(f32[32,1,128]{2,1,0:T(1,128)} %get-tuple-element.58), calls=%async_computation.3 | async-start | bytes 32768 | tf_op jit(solution)/shard_map/all_to_all | solution.py:558
  46.2 3.0 %flux.5 = (f32[15,400,128]{2,1,0:T(8,128)S(1)}, f32[2,8,8,512]{3,2,1,0:T(8,128)S(1)}) custom-call(f32[15,400,128]{2,1,0:T(8,128)S(1)} %get-tuple-element.59.refs_0_, f32[2,8,8,512]{3,2,1,0:T(8,128)S(1)} %get-tuple-element.60.refs_1_), custom_call_target="tpu_custom_call", output_to_operand_aliasing={{0}: (0, {}), {1}: (1, {})} | custom-call | flops 14745600 | bytes 4718592 | tf_op jit(solution)/shard_map/flux/pallas_call | solution.py:661
  49.2 4.1 %all-to-all-done.3.peak_ref = f32[32,1,128]{2,1,0:T(1,128)S(1)} async-done(((f32[32,1,128]{2,1,0:T(1,128)}), f32[32,1,128]{2,1,0:T(1,128)S(1)}, u32[]{:S(2)}, u32[]{:S(2)}) %all-to-all-start.3) | async-done | bytes 16416 | tf_op jit(solution)/shard_map/all_to_all | solution.py:558
  53.7 1.1 %collective-permute-done.4.other_ref = f32[4,1,128]{2,1,0:T(1,128)S(1)} collective-permute-done((f32[4,1,128]{2,1,0:T(1,128)S(1)}, f32[4,1,128]{2,1,0:T(1,128)S(1)}, u32[]{:S(2)}, u32[]{:S(2)}) %collective-permute-start.4) | collective-permute-done | bytes 2080 | tf_op jit(solution)/shard_map/ppermute | solution.py:562
  55.5 1.4 %collective-permute-start.6 = (f32[1,128]{1,0:T(1,128)S(1)}, f32[1,128]{1,0:T(1,128)S(1)}, u32[]{:S(2)}, u32[]{:S(2)}) collective-permute-start(f32[1,128]{1,0:T(1,128)S(1)} %get-tuple-element.68), channel_id=1, source_target_pairs={{0,4},{1,5},{2,6},{3,7},{4,0},{5,1},{6,2},{7,3},{8,12},{9,13},{10,... | collective-permute-start | bytes 1544 | tf_op jit(solution)/shard_map/ppermute | solution.py:562
  56.9 1.5 %collective-permute-start.7 = (f32[1,128]{1,0:T(1,128)S(1)}, f32[1,128]{1,0:T(1,128)S(1)}, u32[]{:S(2)}, u32[]{:S(2)}) collective-permute-start(f32[1,128]{1,0:T(1,128)S(1)} %get-tuple-element.69), channel_id=1, source_target_pairs={{0,2},{1,3},{2,0},{3,1},{4,6},{5,7},{6,4},{7,5},{8,10},{9,11},{10,... | collective-permute-start | bytes 1544 | tf_op jit(solution)/shard_map/ppermute | solution.py:562
  58.4 1.2 %store.1 = (f32[15,400,128]{2,1,0:T(8,128)S(1)}, f32[384,256]{1,0:T(8,128)}, f32[2,384,256]{2,1,0:T(8,128)}) custom-call(f32[32,1,128]{2,1,0:T(1,128)S(1)} %all-to-all-done.3.peak_ref, f32[15,400,128]{2,1,0:T(8,128)S(1)} %get-tuple-element.61.work_in.work), custom_call_target="tpu_custom_call", output_to_operand_aliasing={{0}: (1, {})} | custom-call | flops 983040 | bytes 2359296 | tf_op jit(solution)/shard_map/store/pallas_call | solution.py:729
  (16 shorter events, 3.2 us)
Async XLA Ops:
  2.1 10.3 %collective-permute-start = (f32[10,4,128]{2,1,0:T(4,128)S(1)}, f32[10,4,128]{2,1,0:T(4,128)S(1)}, u32[]{:S(2)}, u32[]{:S(2)}) collective-permute-start(f32[10,4,128]{2,1,0:T(4,128)S(1)} %get-tuple-element.41), channel_id=1, source_target_pairs={{0,8},{8,16},{16,24},{24,0},{1,9},{9,17},{17,25},{25,1},{2,10},{10... | collective-permute-start | bytes 61448 | tf_op jit(solution)/shard_map/ppermute | solution.py:568
  5.2 7.2 %collective-permute-start.1 = (f32[10,4,128]{2,1,0:T(4,128)S(1)}, f32[10,4,128]{2,1,0:T(4,128)S(1)}, u32[]{:S(2)}, u32[]{:S(2)}) collective-permute-start(f32[10,4,128]{2,1,0:T(4,128)S(1)} %get-tuple-element.42), channel_id=1, source_target_pairs={{8,0},{16,8},{24,16},{0,24},{9,1},{17,9},{25,17},{1,25},{10,2},{18... | collective-permute-start | bytes 61448 | tf_op jit(solution)/shard_map/ppermute | solution.py:568
  8.1 11.9 %all-to-all-start = ((f32[32,2,128]{2,1,0:T(2,128)}), f32[32,2,128]{2,1,0:T(2,128)S(1)}, u32[]{:S(2)}, u32[]{:S(2)}) async-start(f32[32,2,128]{2,1,0:T(2,128)} %get-tuple-element.38), calls=%async_computation | async-start | bytes 65536 | tf_op jit(solution)/shard_map/all_to_all | solution.py:558
  12.5 5.1 %collective-permute-start.3 = (f32[5,4,512]{2,1,0:T(4,128)S(1)}, f32[5,4,512]{2,1,0:T(4,128)S(1)}, u32[]{:S(2)}, u32[]{:S(2)}) collective-permute-start(f32[5,4,512]{2,1,0:T(4,128)S(1)} %get-tuple-element.44.own_left), channel_id=1, source_target_pairs={{1,0},{2,1},{3,2},{4,3},{5,4},{6,5},{7,6},{0,7},{9,8},{10,9},{11,1... | collective-permute-start | bytes 122888 | tf_op jit(solution)/shard_map/ppermute | solution.py:568
  15.0 4.4 %collective-permute-start.2 = (f32[5,4,512]{2,1,0:T(4,128)S(1)}, f32[5,4,512]{2,1,0:T(4,128)S(1)}, u32[]{:S(2)}, u32[]{:S(2)}) collective-permute-start(f32[5,4,512]{2,1,0:T(4,128)S(1)} %get-tuple-element.45.own_right), channel_id=1, source_target_pairs={{0,1},{1,2},{2,3},{3,4},{4,5},{5,6},{6,7},{7,0},{8,9},{9,10},{10,1... | collective-permute-start | bytes 122888 | tf_op jit(solution)/shard_map/ppermute | solution.py:568
  20.9 11.2 %all-to-all-start.1 = ((f32[32,1,128]{2,1,0:T(1,128)}), f32[32,1,128]{2,1,0:T(1,128)S(1)}, u32[]{:S(2)}, u32[]{:S(2)}) async-start(f32[32,1,128]{2,1,0:T(1,128)} %get-tuple-element.48), calls=%async_computation.1 | async-start | bytes 32768 | tf_op jit(solution)/shard_map/all_to_all | solution.py:558
  33.0 9.6 %all-to-all-start.2 = ((f32[32,1,128]{2,1,0:T(1,128)}), f32[32,1,128]{2,1,0:T(1,128)S(1)}, u32[]{:S(2)}, u32[]{:S(2)}) async-start(f32[32,1,128]{2,1,0:T(1,128)} %get-tuple-element.53), calls=%async_computation.2 | async-start | bytes 32768 | tf_op jit(solution)/shard_map/all_to_all | solution.py:558
  43.6 9.6 %all-to-all-start.3 = ((f32[32,1,128]{2,1,0:T(1,128)}), f32[32,1,128]{2,1,0:T(1,128)S(1)}, u32[]{:S(2)}, u32[]{:S(2)}) async-start(f32[32,1,128]{2,1,0:T(1,128)} %get-tuple-element.58), calls=%async_computation.3 | async-start | bytes 32768 | tf_op jit(solution)/shard_map/all_to_all | solution.py:558
  53.7 1.2 %collective-permute-start.4 = (f32[4,1,128]{2,1,0:T(1,128)S(1)}, f32[4,1,128]{2,1,0:T(1,128)S(1)}, u32[]{:S(2)}, u32[]{:S(2)}) collective-permute-start(f32[4,1,128]{2,1,0:T(1,128)S(1)} %get-tuple-element.66), channel_id=1, source_target_pairs={{0,1},{1,0},{2,3},{3,2},{4,5},{5,4},{6,7},{7,6},{8,9},{9,8},{10,11... | collective-permute-start | bytes 6152 | tf_op jit(solution)/shard_map/ppermute | solution.py:562
  54.9 4.7 %collective-permute-start.5 = (f32[1,128]{1,0:T(1,128)S(1)}, f32[1,128]{1,0:T(1,128)S(1)}, u32[]{:S(2)}, u32[]{:S(2)}) collective-permute-start(f32[1,128]{1,0:T(1,128)S(1)} %get-tuple-element.67), channel_id=1, source_target_pairs={{0,6},{1,7},{2,4},{3,5},{4,2},{5,3},{6,0},{7,1},{8,14},{9,15},{10,... | collective-permute-start | bytes 1544 | tf_op jit(solution)/shard_map/ppermute | solution.py:562
  55.5 4.1 %collective-permute-start.6 = (f32[1,128]{1,0:T(1,128)S(1)}, f32[1,128]{1,0:T(1,128)S(1)}, u32[]{:S(2)}, u32[]{:S(2)}) collective-permute-start(f32[1,128]{1,0:T(1,128)S(1)} %get-tuple-element.68), channel_id=1, source_target_pairs={{0,4},{1,5},{2,6},{3,7},{4,0},{5,1},{6,2},{7,3},{8,12},{9,13},{10,... | collective-permute-start | bytes 1544 | tf_op jit(solution)/shard_map/ppermute | solution.py:562
  56.9 3.5 %collective-permute-start.7 = (f32[1,128]{1,0:T(1,128)S(1)}, f32[1,128]{1,0:T(1,128)S(1)}, u32[]{:S(2)}, u32[]{:S(2)}) collective-permute-start(f32[1,128]{1,0:T(1,128)S(1)} %get-tuple-element.69), channel_id=1, source_target_pairs={{0,2},{1,3},{2,0},{3,1},{4,6},{5,7},{6,4},{7,5},{8,10},{9,11},{10,... | collective-permute-start | bytes 1544 | tf_op jit(solution)/shard_map/ppermute | solution.py:562
